TPU v7x, 256 devices: a whole 4x4x8 slice. The times are simulated.
256 devices in a mesh: dp: 2 (over core), expert: 4 (over x), tensor: 32 (over z, y).
Axes of the slice: x: 4, y: 4, z: 8, core: 2. Of those that a mesh axis runs over, the one named last changes fastest.
Arguments:
- tokens: bfloat16 [1024, 3072], P(('dp', 'expert')), may hold values from -6 to 6
- cotangent: bfloat16 [1024, 3072], P(('dp', 'expert')), may hold values from -6 to 6
- gate_weights: bfloat16 [1024, 2], P(('dp', 'expert')), may hold values from 0.099609375 to 0.8984375
- expert_ids: int32 [1024, 2], P(('dp', 'expert')), may hold values from 0 to 3, all different within a row; in each aligned block of 128 rows (0 to 127, 128 to 255, ...) at most 96 rows name the same one
- w_gate: bfloat16 [4, 3072, 8192], P('expert', 'dp', 'tensor'), may hold values from -0.109375 to 0.109375
- w_up: bfloat16 [4, 3072, 8192], P('expert', 'dp', 'tensor'), may hold values from -0.109375 to 0.109375
- w_down: bfloat16 [4, 3072, 8192], P('expert', 'dp', 'tensor'), may hold values from -0.0625 to 0.0625
Outputs:
- input_grad: bfloat16 [1024, 3072], P(('dp', 'expert'))
- gate_grad: bfloat16 [1024, 2], P(('dp', 'expert'))
- grad_gate: bfloat16 [4, 3072, 8192], P('expert', 'dp', 'tensor')
- grad_up: bfloat16 [4, 3072, 8192], P('expert', 'dp', 'tensor')
- grad_down: bfloat16 [4, 3072, 8192], P('expert', 'dp', 'tensor')
Inputs may be any that keep to these rules, and one draw needn't show every extreme that they name: `expert_ids`: each token names 2 different experts. Among the 128 tokens of one block, no expert is named more than 96 times, and in some blocks one expert is named exactly 96 times.
All inputs are finite; a program needn't handle non-finite values.
Results may differ from a plain program's by a relative error of at most 0.025.
Values may be sent and summed in bfloat16 or wider, within the bound.
No kernel may reach another device: no remote copies, remote signals or barrier semaphores. Data moves between devices by JAX's collectives and lax.ppermute only.
A program may use at most 64 MiB of HBM per device.

v0:
```python
import functools

import jax
import jax.numpy as jnp
from jax import lax
from jax.experimental import pallas as pl
from jax.experimental.pallas import tpu as pltpu
from jax.sharding import Mesh, PartitionSpec as P


BF = jnp.bfloat16
F32 = jnp.float32
NT = (((1,), (1,)), ((), ()))
TN = (((0,), (0,)), ((), ()))
LANES = 128


MIB = 1 << 20


def array(*shape):
    return pltpu.VMEM(shape, BF)


def plain(*shape):
    return pltpu.HBM(shape, BF)


def call(kernel, outs, operands, limit=8, scratch=(), free=(), unblocked=()):
    spec = pl.BlockSpec(memory_space=pltpu.VMEM)
    specs = [pl.BlockSpec(memory_space=pltpu.SMEM)]
    kept = [operands[0]]
    for k, value in enumerate(operands[1:]):
        if k in unblocked:
            specs.append(pl.BlockSpec(memory_space=pl.ANY))
        else:
            specs.append(spec)
            space = pltpu.HBM if k in free else pltpu.VMEM
            value = pltpu.with_memory_space_constraint(value, space)
        kept.append(value)
    return pl.pallas_call(
        kernel,
        out_shape=outs,
        in_specs=specs,
        out_specs=[spec] * len(outs),
        scratch_shapes=list(scratch),
        compiler_params=pltpu.CompilerParams(vmem_limit_bytes=limit * MIB),
    )(*kept)


def routing(pos, ids_ref, gw_ref, offsets):
    tokens = ids_ref.shape[1]
    ids = ids_ref[...]
    gates = gw_ref[...].astype(F32)
    before = (
        lax.broadcasted_iota(jnp.int32, (tokens, tokens), 0)
        < lax.broadcasted_iota(jnp.int32, (tokens, tokens), 1)
    ).astype(BF)
    rows = []
    weights = []
    for offset in offsets:
        hit = ids == lax.rem(pos[1] + offset + 4, 4)
        rows.append(jnp.max(hit.astype(F32), axis=0, keepdims=True))
        weights.append(jnp.sum(jnp.where(hit, gates, 0.0), axis=0, keepdims=True))
    member = jnp.concatenate(rows + [jnp.zeros((8 - len(rows), tokens), F32)], axis=0)
    rank = jnp.dot(member.astype(BF), before, preferred_element_type=F32)
    return member, rank, weights


def picks(rank, member, j, slots, first):
    slot = lax.broadcasted_iota(jnp.int32, (slots, rank.shape[1]), 0)
    slot = (slot + first).astype(F32)
    hit = (slot == rank[j : j + 1]) & (member[j : j + 1] > 0.5)
    return jnp.where(hit, 1.0, 0.0).astype(BF)


def facts_of(pick, weight):
    tokens = pick.shape[1]
    token = lax.broadcasted_iota(jnp.int32, (8, tokens), 1).astype(F32) + 1.0
    line = lax.broadcasted_iota(jnp.int32, (8, tokens), 0)
    facts = jnp.where(line == 0, weight, jnp.where(line == 1, token, 0.0))
    facts = jnp.concatenate([facts, jnp.zeros((LANES - 8, tokens), F32)], axis=0).astype(BF)
    return lax.dot_general(pick, facts, NT, preferred_element_type=F32).astype(BF)


def far_kernel(pos, ids_ref, gw_ref, tok_ref, cot_ref, out, held, sem):
    first = pos[3] < 2

    @pl.when(first)
    def _():
        pltpu.make_async_copy(tok_ref, held, sem).start()

    @pl.when(jnp.logical_not(first))
    def _():
        pltpu.make_async_copy(cot_ref, held, sem).start()

    member, rank, weights = routing(pos, ids_ref, gw_ref, (2,))
    width = tok_ref.shape[1]
    slots = out.shape[0]
    pick = picks(rank, member, 0, slots, lax.rem(pos[3], 2) * slots)
    out[:, width:] = facts_of(pick, weights[0])
    pltpu.make_async_copy(tok_ref, held, sem).wait()
    out[:, :width] = jnp.dot(pick, held[...], preferred_element_type=F32).astype(BF)


def near_kernel(offsets, pos, ids_ref, gw_ref, tok_ref, cot_ref, *outs):
    member, rank, weights = routing(pos, ids_ref, gw_ref, offsets)
    width = tok_ref.shape[1]
    for j, out in enumerate(outs):
        pick = picks(rank, member, j, out.shape[0], 0)
        out[:, :width] = jnp.dot(pick, tok_ref[...], preferred_element_type=F32).astype(BF)
        out[:, width : 2 * width] = jnp.dot(
            pick, cot_ref[...], preferred_element_type=F32
        ).astype(BF)
        out[:, 2 * width :] = facts_of(pick, weights[j])


def expert_kernel(kind, pos, *refs):
    count = {"here": 1, "far": 4, "sides": 2}[kind]
    pieces, refs = refs[:count], refs[count:]
    wg_own, wg_sib, wu_own, wu_sib, wd_own, wd_sib = (ref.at[0] for ref in refs[:6])
    sends, aux_ref, whole = refs[6:10], refs[10], refs[-1]
    half, units = wg_own.shape
    width = 2 * half
    block = half // 2
    if kind == "far":
        msgs = [refs[11]]
        rows = pieces[0].shape[0]
        for piece, shift in zip(pieces, (0, 1, -1, 2)):
            source = lax.rem(pos[3] - shift + 4, 4)
            at = pl.multiple_of(lax.rem(source, 2) * rows, 16)
            column = pl.multiple_of(lax.div(source, 2) * width, LANES)
            msgs[0][pl.ds(at, rows), pl.ds(column, width)] = piece[:, :width]
            msgs[0][pl.ds(at, rows), 2 * width :] = piece[:, width:]
    else:
        msgs = pieces
    own = pl.multiple_of(pos[0] * half, LANES)
    sib = pl.multiple_of((1 - pos[0]) * half, LANES)

    def columns(at, size):
        parts = [msg[:, pl.ds(at, size)] for msg in msgs]
        return parts[0] if len(parts) == 1 else jnp.concatenate(parts, axis=0)

    facts = columns(2 * width, LANES)
    g = facts[:, :1].astype(F32)

    def product(left_own, left_sib, w_own, w_sib):
        left = jnp.dot(left_own, w_own[...], preferred_element_type=F32)
        return left + jnp.dot(left_sib, w_sib[...], preferred_element_type=F32)

    x_own, x_sib = columns(own, half), columns(sib, half)
    gate = product(x_own, x_sib, wg_own, wg_sib)
    up = product(x_own, x_sib, wu_own, wu_sib)
    back = product(columns(width + own, half), columns(width + sib, half), wd_own, wd_sib)
    sig = jax.nn.sigmoid(gate)
    act = gate * sig
    hid = act * up
    slot_gate = jnp.sum(hid.astype(BF).astype(F32) * back, axis=1, keepdims=True)
    hg = g * back
    dpg = (hg * up * sig * (1.0 + gate * (1.0 - sig))).astype(BF)
    dpu = (hg * act).astype(BF)
    aux_ref[:, :units] = dpg
    aux_ref[:, units : 2 * units] = dpu
    aux_ref[:, 2 * units : 3 * units] = (g * hid).astype(BF)
    aux_ref[:, 3 * units :] = facts
    lane = lax.broadcasted_iota(jnp.int32, facts.shape, 1)
    extra = jnp.where(lane == pos[1], slot_gate, 0.0).astype(BF)
    for j in range(4):
        wg, wu = (wg_own, wu_own) if j < 2 else (wg_sib, wu_sib)
        at = (j % 2) * block
        part = lax.dot_general(dpg, wg[at : at + block, :], NT, preferred_element_type=F32)
        part += lax.dot_general(dpu, wu[at : at + block, :], NT, preferred_element_type=F32)
        whole[j] = part.astype(BF)
    for j, send in enumerate(sends):
        send[:, :block] = whole[lax.rem(pos[3] + j, 4)]
        send[:, block:] = extra


def expand_kernel(pos, a_ref, b_ref, c_ref, d_ref, aux_ref, *outs):
    tokens = outs[0].shape[0]
    slots = a_ref.shape[0] // len(outs)
    token = lax.broadcasted_iota(jnp.int32, (slots, tokens), 1).astype(F32) + 1.0
    for i, out in enumerate(outs):
        at = slice(i * slots, (i + 1) * slots)
        total = a_ref[at, :].astype(F32)
        for ref in (b_ref, c_ref, d_ref):
            total += ref[at, :].astype(F32)
        index = aux_ref[at, aux_ref.shape[1] - LANES :][:, 1:2].astype(F32)
        pick = jnp.where(index == token, 1.0, 0.0).astype(BF)
        out[...] = lax.dot_general(
            pick, total.astype(BF), TN, preferred_element_type=F32
        ).astype(BF)


def total_kernel(pos, *refs):
    out_ref = refs[-1]
    rows = out_ref.shape[1]
    for z in range(out_ref.shape[0]):
        at = slice(z * rows, (z + 1) * rows)
        total = refs[0][at, :].astype(F32)
        for ref in refs[1:-1]:
            total += ref[at, :].astype(F32)
        out_ref[z] = total.astype(BF)


def gather_kernel(pos, got_ref, out_ref):
    total = got_ref[0].astype(F32)
    for z in range(1, got_ref.shape[0]):
        total += got_ref[z].astype(F32)
    total = total.astype(BF)
    for z in range(out_ref.shape[0]):
        out_ref[z] = total


def rows_kernel(pos, ids_ref, got_ref, slab_ref, gate_ref):
    width = slab_ref.shape[1]
    slab_ref[...] = got_ref[:, :width]
    eye = lax.broadcasted_iota(jnp.int32, (8, LANES), 0) == lax.broadcasted_iota(
        jnp.int32, (8, LANES), 1
    )
    values = lax.dot_general(
        jnp.where(eye, 1.0, 0.0).astype(BF), got_ref[:, width:], NT, preferred_element_type=F32
    )
    ids = ids_ref[...]
    line = lax.broadcasted_iota(jnp.int32, values.shape, 0)
    for k in range(2):
        mine = jnp.where(line == ids[k : k + 1], values, 0.0)
        gate_ref[k : k + 1] = jnp.sum(mine, axis=0, keepdims=True).astype(BF)


def columns_kernel(pos, *refs):
    pieces, out_ref = refs[:4], refs[4]
    width = pieces[0].shape[1]
    for piece, shift in zip(pieces, (0, 1, -1, 2)):
        block = lax.rem(pos[3] - shift + 4 + 2 * pos[0], 4)
        out_ref[:, pl.ds(pl.multiple_of(block * width, LANES), width)] = piece[...]


def grad_kernel(other, pos, here_ref, far_ref, plus_ref, minus_ref, *refs):
    msgs = (here_ref, far_ref, plus_ref, minus_ref)
    auxs, added, outs = refs[:3], refs[3:-3], refs[-3:]
    half, units = outs[0].shape
    width = 2 * half
    base = ((1 - pos[0]) if other else pos[0]) * half
    step = 256
    right = jnp.concatenate([ref[:, : 2 * units] for ref in auxs], axis=0)
    hidden = jnp.concatenate([ref[:, 2 * units : 3 * units] for ref in auxs], axis=0)
    for i in range(half // step):
        rows = slice(i * step, (i + 1) * step)

        def left(start):
            at = pl.multiple_of(start + base + i * step, LANES)
            return jnp.concatenate([msg[:, pl.ds(at, step)] for msg in msgs], axis=0)

        both = lax.dot_general(left(0), right, TN, preferred_element_type=F32)
        down = lax.dot_general(left(width), hidden, TN, preferred_element_type=F32)
        for k, total in enumerate((both[:, :units], both[:, units:], down)):
            if added:
                total += added[k][rows].astype(F32)
            outs[k][rows] = total.astype(BF)


def shift(value, axis, offset):
    size = lax.axis_size(axis)
    return lax.ppermute(value, axis, [(i, (i + offset) % size) for i in range(size)])


def exchange(value, axis):
    return lax.all_to_all(value, axis, split_axis=0, concat_axis=0, tiled=True)


def after(value, *others):
    return lax.optimization_barrier((value, *others))[0]


def on_device(tokens, cotangent, gate_weights, expert_ids, w_gate, w_up, w_down):
    tok_count, width = tokens.shape
    slots = tok_count * 3 // 4
    units = w_gate.shape[2]
    block = width // 4
    zs = lax.axis_size("z")
    rows = tok_count // zs
    wide = block + LANES
    long = 2 * width + LANES
    pos = jnp.stack(
        [lax.axis_index(name) for name in ("dp", "expert", "z", "y")]
    ).astype(jnp.int32)
    given = (expert_ids.T, gate_weights.T, tokens, cotangent)

    (far,) = call(
        far_kernel,
        [array(slots // 2, width + LANES)],
        (pos, *given),
        free=(0, 1),
        unblocked=(2, 3),
        scratch=[pltpu.VMEM(tokens.shape, BF), pltpu.SemaphoreType.DMA],
    )
    plus, minus = call(
        functools.partial(near_kernel, (1, -1)),
        [array(slots, long)] * 2,
        (after(pos, far), *given),
        free=(0, 1),
    )
    then = after(pos, plus)
    (here,) = call(
        functools.partial(near_kernel, (0,)), [array(slots, long)], (then, *given),
        free=(0, 1),
    )
    weights = []
    for own in (w_gate, w_up, w_down):
        weights += [own, shift(after(own, plus), "dp", 1)]
    plus, minus = shift(plus, "expert", 1), shift(minus, "expert", -1)
    far = shift(far, "expert", 2)
    far = [far] + [shift(far, "y", offset) for offset in (1, -1, 2)]

    def expert(pos, msgs, kind):
        n = slots * (2 if kind == "sides" else 1)
        return call(
            functools.partial(expert_kernel, kind),
            [array(n, wide)] * 4
            + [plain(n, 3 * units + LANES)]
            + [array(slots, long)] * (kind == "far"),
            (pos, *msgs, *weights),
            scratch=[pltpu.VMEM((4, n, block), BF)],
        )

    def scatter(sends):
        return [sends[0]] + [shift(sends[j], "y", j) for j in (1, 3, 2)]

    def expand(pos, got, aux):
        count = aux.shape[0] // slots
        return call(expand_kernel, [array(tok_count, wide)] * count, (pos, *got, aux))

    local = expert(pos, [here], "here")
    remote = expert(after(pos, local[0]), far, "far")
    then = after(pos, remote[0])
    sides = expert(then, [plus, minus], "sides")
    (mine,) = expand(then, scatter(local[:4]), local[4])
    then = after(pos, sides[0])
    (from_far,) = expand(then, scatter(remote[:4]), remote[4])
    from_plus, from_minus = expand(then, scatter(sides[:4]), sides[4])
    early = after(pos, from_far)
    parts = [
        mine,
        shift(from_far, "expert", 2),
        shift(from_plus, "expert", -1),
        shift(from_minus, "expert", 1),
    ]
    (mine,) = call(total_kernel, [plain(zs, rows, wide)], (pos, *parts))
    late = after(pos, mine)
    (mine,) = call(gather_kernel, [plain(zs, rows, wide)], (pos, exchange(mine, "z")))
    mine = exchange(mine, "z").reshape(tok_count, wide)
    slab, gate_grad = call(
        rows_kernel, [array(tok_count, block), plain(2, tok_count)], (pos, expert_ids.T, mine)
    )
    (input_grad,) = call(
        columns_kernel,
        [plain(tok_count, width)],
        (pos, slab, *[shift(slab, "y", offset) for offset in (1, -1, 2)]),
    )
    used = [here, remote[5], plus, minus, local[4], remote[4], sides[4]]
    half = width // 2
    away = call(
        functools.partial(grad_kernel, True), [array(half, units)] * 3, (early, *used),
        limit=12,
    )
    received = [shift(part, "dp", 1) for part in away]
    grads = call(
        functools.partial(grad_kernel, False), [plain(half, units)] * 3, (late, *used, *received),
        limit=12,
    )
    return (input_grad, gate_grad.T, grads[0][None], grads[1][None], grads[2][None])


def solution(mesh):
    dp, experts, tensor = (mesh.shape[name] for name in ("dp", "expert", "tensor"))
    view = Mesh(mesh.devices.reshape(dp, experts, tensor // 4, 4), ("dp", "expert", "z", "y"))
    row = P(("dp", "expert"), None)
    weight = P("expert", "dp", ("z", "y"))

    return jax.shard_map(
        on_device,
        mesh=view,
        in_specs=(row, row, row, row, weight, weight, weight),
        out_specs=(row, row, weight, weight, weight),
        check_vma=False,
    )
```

profile of v0, /device:TPU:8, one launch (start us, length us, event | category | flops | bytes accessed | tf_op | source)
XLA Modules:
  0.0 139.7 jit_solution(2375296446517443566)
XLA Ops:
  4.4 3.1 %collective-permute-start.3 = (bf16[48,3200]{1,0:T(8,128)(2,1)S(1)}, bf16[48,3200]{1,0:T(8,128)(2,1)S(1)}, u32[]{:S(2)}, u32[]{:S(2)}) collective-permute-start(bf16[48,3200]{1,0:T(8,128)(2,1)S(1)} %shard_map.110), channel_id=1, source_target_pairs={{0,64},{32,96},{64,0},{96,32},{1,65},{33,97},{65,1},{97,33},{2,66}... | collective-permute-start | bytes 921608 | tf_op jit(solution)/shard_map/ppermute | solution.py:265
  9.8 2.6 %collective-permute-start.11 = (bf16[96,6272]{1,0:T(8,128)(2,1)S(1)}, bf16[96,6272]{1,0:T(8,128)(2,1)S(1)}, u32[]{:S(2)}, u32[]{:S(2)}) collective-permute-start(bf16[96,6272]{1,0:T(8,128)(2,1)S(1)} %get-tuple-element.57), channel_id=1, source_target_pairs={{0,96},{32,0},{64,32},{96,64},{1,97},{33,1},{65,33},{97,65},{2,98}... | collective-permute-start | bytes 3612680 | tf_op jit(solution)/shard_map/ppermute | solution.py:265
  12.9 3.2 %collective-permute-done.3.refs_0_ = bf16[48,3200]{1,0:T(8,128)(2,1)S(1)} collective-permute-done((bf16[48,3200]{1,0:T(8,128)(2,1)S(1)}, bf16[48,3200]{1,0:T(8,128)(2,1)S(1)}, u32[]{:S(2)}, u32[]{:S(2)}) %collective-permute-start.3) | collective-permute-done | bytes 307232 | tf_op jit(solution)/shard_map/ppermute | solution.py:265
  18.4 2.3 %collective-permute-start.6 = (bf16[48,3200]{1,0:T(8,128)(2,1)S(1)}, bf16[48,3200]{1,0:T(8,128)(2,1)S(1)}, u32[]{:S(2)}, u32[]{:S(2)}) collective-permute-start(bf16[48,3200]{1,0:T(8,128)(2,1)S(1)} %collective-permute-done.3.refs_0_), channel_id=1, source_target_pairs={{0,2},{1,3},{2,0},{3,1},{4,6},{5,7},{6,4},{7,5},{8,10},{9,11},{10,... | collective-permute-start | bytes 921608 | tf_op jit(solution)/shard_map/ppermute | solution.py:265
  22.0 3.3 %shard_map.113 = (bf16[96,896]{1,0:T(8,128)(2,1)S(1)}, bf16[96,896]{1,0:T(8,128)(2,1)S(1)}, bf16[96,896]{1,0:T(8,128)(2,1)S(1)}, bf16[96,896]{1,0:T(8,128)(2,1)S(1)}, bf16[96,896]{1,0:T(8,128)(2,1)}) custom-call(s32[4]{0:T(128)S(1)} %pad_add_fusion.pos, bf16[96,6272]{1,0:T(8,128)(2,1)S(1)} %shard_map.112.refs_0_.here_ref, ...), custom_call_target="tpu_custom_call" | custom-call | tf_op jit(solution)/shard_map/pallas_call | solution.py:41
  27.2 7.2 %collective-permute-done.6.refs_3_ = bf16[48,3200]{1,0:T(8,128)(2,1)S(1)} collective-permute-done((bf16[48,3200]{1,0:T(8,128)(2,1)S(1)}, bf16[48,3200]{1,0:T(8,128)(2,1)S(1)}, u32[]{:S(2)}, u32[]{:S(2)}) %collective-permute-start.6) | collective-permute-done | bytes 307232 | tf_op jit(solution)/shard_map/ppermute | solution.py:265
  34.4 3.4 %shard_map.114 = (bf16[96,896]{1,0:T(8,128)(2,1)S(1)}, bf16[96,896]{1,0:T(8,128)(2,1)S(1)}, bf16[96,896]{1,0:T(8,128)(2,1)S(1)}, bf16[96,896]{1,0:T(8,128)(2,1)S...) custom-call(s32[4]{0:T(128)S(1)} %pad_add_fusion.pos, bf16[48,3200]{1,0:T(8,128)(2,1)S(1)} %collective-permute-done.3.refs_0_, ...), custom_call_target="tpu_custom_call" | custom-call | tf_op jit(solution)/shard_map/pallas_call | solution.py:41
  37.8 3.0 %collective-permute-done.10.refs_0_.plus_ref = bf16[96,6272]{1,0:T(8,128)(2,1)S(1)} collective-permute-done((bf16[96,6272]{1,0:T(8,128)(2,1)S(1)}, bf16[96,6272]{1,0:T(8,128)(2,1)S(1)}, u32[]{:S(2)}, u32[]{:S(2)}) %collective-permute-start.10) | collective-permute-done | bytes 1204256 | tf_op jit(solution)/shard_map/ppermute | solution.py:265
  40.9 3.7 %shard_map.116 = (bf16[192,896]{1,0:T(8,128)(2,1)S(1)}, bf16[192,896]{1,0:T(8,128)(2,1)S(1)}, bf16[192,896]{1,0:T(8,128)(2,1)S(1)}, bf16[192,896]{1,0:T(8,128)(2,1)S(1)}, bf16[192,896]{1,0:T(8,128)(2,1)}) custom-call(s32[4]{0:T(128)S(1)} %pad_add_fusion.pos, bf16[96,6272]{1,0:T(8,128)(2,1)S(1)} %collective-permute-done.10.refs_0_.plus_ref, ...), custom_call_target="tpu_custom_call" | custom-call | tf_op jit(solution)/shard_map/pallas_call | solution.py:41
  46.7 2.3 %collective-permute-start.18 = (bf16[192,896]{1,0:T(8,128)(2,1)S(1)}, bf16[192,896]{1,0:T(8,128)(2,1)S(1)}, u32[]{:S(2)}, u32[]{:S(2)}) collective-permute-start(bf16[192,896]{1,0:T(8,128)(2,1)S(1)} %get-tuple-element.66), channel_id=1, source_target_pairs={{0,2},{1,3},{2,0},{3,1},{4,6},{5,7},{6,4},{7,5},{8,10},{9,11},{10,... | collective-permute-start | bytes 1032200 | tf_op jit(solution)/shard_map/ppermute | solution.py:265
  51.3 16.2 %collective-permute-done.13.c_ref = bf16[96,896]{1,0:T(8,128)(2,1)S(1)} collective-permute-done((bf16[96,896]{1,0:T(8,128)(2,1)S(1)}, bf16[96,896]{1,0:T(8,128)(2,1)S(1)}, u32[]{:S(2)}, u32[]{:S(2)}) %collective-permute-start.13) | collective-permute-done | bytes 172064 | tf_op jit(solution)/shard_map/ppermute | solution.py:265
  67.5 2.1 %collective-permute-start.7 = (bf16[96,896]{1,0:T(8,128)(2,1)S(1)}, bf16[96,896]{1,0:T(8,128)(2,1)S(1)}, u32[]{:S(2)}, u32[]{:S(2)}) collective-permute-start(bf16[96,896]{1,0:T(8,128)(2,1)S(1)} %get-tuple-element.53), channel_id=1, source_target_pairs={{0,1},{1,2},{2,3},{3,0},{4,5},{5,6},{6,7},{7,4},{8,9},{9,10},{10,1... | collective-permute-start | bytes 516104 | tf_op jit(solution)/shard_map/ppermute | solution.py:265
  69.6 1.8 %collective-permute-done.14.d_ref = bf16[96,896]{1,0:T(8,128)(2,1)S(1)} collective-permute-done((bf16[96,896]{1,0:T(8,128)(2,1)S(1)}, bf16[96,896]{1,0:T(8,128)(2,1)S(1)}, u32[]{:S(2)}, u32[]{:S(2)}) %collective-permute-start.14) | collective-permute-done | bytes 172064 | tf_op jit(solution)/shard_map/ppermute | solution.py:265
  72.2 3.1 %collective-permute-start.15 = (bf16[128,896]{1,0:T(8,128)(2,1)S(1)}, bf16[128,896]{1,0:T(8,128)(2,1)S(1)}, u32[]{:S(2)}, u32[]{:S(2)}) collective-permute-start(bf16[128,896]{1,0:T(8,128)(2,1)S(1)} %shard_map.117), channel_id=1, source_target_pairs={{0,64},{32,96},{64,0},{96,32},{1,65},{33,97},{65,1},{97,33},{2,66}... | collective-permute-start | bytes 688136 | tf_op jit(solution)/shard_map/ppermute | solution.py:265
  78.4 3.6 %collective-permute-start.9 = (bf16[96,896]{1,0:T(8,128)(2,1)S(1)}, bf16[96,896]{1,0:T(8,128)(2,1)S(1)}, u32[]{:S(2)}, u32[]{:S(2)}) collective-permute-start(bf16[96,896]{1,0:T(8,128)(2,1)S(1)} %get-tuple-element.55), channel_id=1, source_target_pairs={{0,2},{1,3},{2,0},{3,1},{4,6},{5,7},{6,4},{7,5},{8,10},{9,11},{10,... | collective-permute-start | bytes 516104 | tf_op jit(solution)/shard_map/ppermute | solution.py:265
  82.0 2.6 %collective-permute-done.8.c_ref = bf16[96,896]{1,0:T(8,128)(2,1)S(1)} collective-permute-done((bf16[96,896]{1,0:T(8,128)(2,1)S(1)}, bf16[96,896]{1,0:T(8,128)(2,1)S(1)}, u32[]{:S(2)}, u32[]{:S(2)}) %collective-permute-start.8) | collective-permute-done | bytes 172064 | tf_op jit(solution)/shard_map/ppermute | solution.py:265
  84.6 2.6 %collective-permute-done.9.d_ref = bf16[96,896]{1,0:T(8,128)(2,1)S(1)} collective-permute-done((bf16[96,896]{1,0:T(8,128)(2,1)S(1)}, bf16[96,896]{1,0:T(8,128)(2,1)S(1)}, u32[]{:S(2)}, u32[]{:S(2)}) %collective-permute-start.9) | collective-permute-done | bytes 172064 | tf_op jit(solution)/shard_map/ppermute | solution.py:265
  89.4 8.5 %all-to-all-start = ((bf16[8,16,896]{2,1,0:T(8,128)(2,1)}), bf16[8,16,896]{2,1,0:T(8,128)(2,1)S(1)}, u32[]{:S(2)}, u32[]{:S(2)}) async-start(bf16[8,16,896]{2,1,0:T(8,128)(2,1)} %shard_map.119), calls=%async_computation | async-start | bytes 458752 | tf_op jit(solution)/shard_map/all_to_all | solution.py:269
  100.5 3.2 %shard_map.123 = (bf16[1536,256]{1,0:T(8,128)(2,1)}, bf16[1536,256]{1,0:T(8,128)(2,1)}, bf16[1536,256]{1,0:T(8,128)(2,1)}) custom-call(s32[4]{0:T(128)S(1)} %pad_add_fusion.pos, bf16[96,6272]{1,0:T(8,128)(2,1)S(1)} %shard_map.112.refs_0_.here_ref, bf16[96,6272]{1,0:T(8,128)(2,1)S(1)} %copy-done.9, ...), custom_call_target="tpu_custom_call" | custom-call | tf_op jit(solution)/shard_map/pallas_call | solution.py:41
  104.2 3.8 %all-to-all-done.got_ref = bf16[8,16,896]{2,1,0:T(8,128)(2,1)S(1)} async-done(((bf16[8,16,896]{2,1,0:T(8,128)(2,1)}), bf16[8,16,896]{2,1,0:T(8,128)(2,1)S(1)}, u32[]{:S(2)}, u32[]{:S(2)}) %all-to-all-start) | async-done | bytes 229408 | tf_op jit(solution)/shard_map/all_to_all | solution.py:269
  109.3 15.2 %all_to_all.10 = bf16[8,16,896]{2,1,0:T(8,128)(2,1)S(1)} all-to-all(bf16[8,16,896]{2,1,0:T(8,128)(2,1)} %shard_map.120), channel_id=1, replica_groups=mesh['dp'=2,'expert'=4,'z'=8,'y'=4] {'z'}, dimensions={0} | all-to-all | bytes 458752 | tf_op jit(solution)/shard_map/all_to_all | solution.py:269
  126.0 1.8 %collective-permute-start.22 = (bf16[128,768]{1,0:T(8,128)(2,1)S(1)}, bf16[128,768]{1,0:T(8,128)(2,1)S(1)}, u32[]{:S(2)}, u32[]{:S(2)}) collective-permute-start(bf16[128,768]{1,0:T(8,128)(2,1)S(1)} %get-tuple-element.70.refs_0_), channel_id=1, source_target_pairs={{0,3},{1,0},{2,1},{3,2},{4,7},{5,4},{6,5},{7,6},{8,11},{9,8},{10,9... | collective-permute-start | bytes 589832 | tf_op jit(solution)/shard_map/ppermute | solution.py:265
  132.0 4.4 %shard_map.124 = (bf16[1536,256]{1,0:T(8,128)(2,1)}, bf16[1536,256]{1,0:T(8,128)(2,1)}, bf16[1536,256]{1,0:T(8,128)(2,1)}) custom-call(s32[4]{0:T(128)S(1)} %pad_add_fusion.pos, bf16[96,6272]{1,0:T(8,128)(2,1)S(1)} %shard_map.112.refs_0_.here_ref, bf16[96,6272]{1,0:T(8,128)(2,1)S(1)} %copy-done.10, ...), custom_call_target="tpu_custom_call" | custom-call | tf_op jit(solution)/shard_map/pallas_call | solution.py:41
  136.4 1.8 %collective-permute-done.23.refs_3_ = bf16[128,768]{1,0:T(8,128)(2,1)S(1)} collective-permute-done((bf16[128,768]{1,0:T(8,128)(2,1)S(1)}, bf16[128,768]{1,0:T(8,128)(2,1)S(1)}, u32[]{:S(2)}, u32[]{:S(2)}) %collective-permute-start.23) | collective-permute-done | bytes 196640 | tf_op jit(solution)/shard_map/ppermute | solution.py:265
  (79 shorter events, 34.1 us)
Async XLA Ops:
  4.4 11.7 %collective-permute-start.3 = (bf16[48,3200]{1,0:T(8,128)(2,1)S(1)}, bf16[48,3200]{1,0:T(8,128)(2,1)S(1)}, u32[]{:S(2)}, u32[]{:S(2)}) collective-permute-start(bf16[48,3200]{1,0:T(8,128)(2,1)S(1)} %shard_map.110), channel_id=1, source_target_pairs={{0,64},{32,96},{64,0},{96,32},{1,65},{33,97},{65,1},{97,33},{2,66}... | collective-permute-start | bytes 921608 | tf_op jit(solution)/shard_map/ppermute | solution.py:265
  9.1 31.7 %collective-permute-start.10 = (bf16[96,6272]{1,0:T(8,128)(2,1)S(1)}, bf16[96,6272]{1,0:T(8,128)(2,1)S(1)}, u32[]{:S(2)}, u32[]{:S(2)}) collective-permute-start(bf16[96,6272]{1,0:T(8,128)(2,1)S(1)} %get-tuple-element.44), channel_id=1, source_target_pairs={{0,32},{32,64},{64,96},{96,0},{1,33},{33,65},{65,97},{97,1},{2,34}... | collective-permute-start | bytes 3612680 | tf_op jit(solution)/shard_map/ppermute | solution.py:265
  9.8 31.1 %collective-permute-start.11 = (bf16[96,6272]{1,0:T(8,128)(2,1)S(1)}, bf16[96,6272]{1,0:T(8,128)(2,1)S(1)}, u32[]{:S(2)}, u32[]{:S(2)}) collective-permute-start(bf16[96,6272]{1,0:T(8,128)(2,1)S(1)} %get-tuple-element.57), channel_id=1, source_target_pairs={{0,96},{32,0},{64,32},{96,64},{1,97},{33,1},{65,33},{97,65},{2,98}... | collective-permute-start | bytes 3612680 | tf_op jit(solution)/shard_map/ppermute | solution.py:265
  16.1 10.2 %collective-permute-start.4 = (bf16[48,3200]{1,0:T(8,128)(2,1)S(1)}, bf16[48,3200]{1,0:T(8,128)(2,1)S(1)}, u32[]{:S(2)}, u32[]{:S(2)}) collective-permute-start(bf16[48,3200]{1,0:T(8,128)(2,1)S(1)} %collective-permute-done.3.refs_0_), channel_id=1, source_target_pairs={{0,1},{1,2},{2,3},{3,0},{4,5},{5,6},{6,7},{7,4},{8,9},{9,10},{10,1... | collective-permute-start | bytes 921608 | tf_op jit(solution)/shard_map/ppermute | solution.py:265
  17.8 9.4 %collective-permute-start.5 = (bf16[48,3200]{1,0:T(8,128)(2,1)S(1)}, bf16[48,3200]{1,0:T(8,128)(2,1)S(1)}, u32[]{:S(2)}, u32[]{:S(2)}) collective-permute-start(bf16[48,3200]{1,0:T(8,128)(2,1)S(1)} %collective-permute-done.3.refs_0_), channel_id=1, source_target_pairs={{0,3},{1,0},{2,1},{3,2},{4,7},{5,4},{6,5},{7,6},{8,11},{9,8},{10,9... | collective-permute-start | bytes 921608 | tf_op jit(solution)/shard_map/ppermute | solution.py:265
  18.4 16.0 %collective-permute-start.6 = (bf16[48,3200]{1,0:T(8,128)(2,1)S(1)}, bf16[48,3200]{1,0:T(8,128)(2,1)S(1)}, u32[]{:S(2)}, u32[]{:S(2)}) collective-permute-start(bf16[48,3200]{1,0:T(8,128)(2,1)S(1)} %collective-permute-done.3.refs_0_), channel_id=1, source_target_pairs={{0,2},{1,3},{2,0},{3,1},{4,6},{5,7},{6,4},{7,5},{8,10},{9,11},{10,... | collective-permute-start | bytes 921608 | tf_op jit(solution)/shard_map/ppermute | solution.py:265
  37.8 12.5 %collective-permute-start.12 = (bf16[96,896]{1,0:T(8,128)(2,1)S(1)}, bf16[96,896]{1,0:T(8,128)(2,1)S(1)}, u32[]{:S(2)}, u32[]{:S(2)}) collective-permute-start(bf16[96,896]{1,0:T(8,128)(2,1)S(1)} %get-tuple-element.60), channel_id=1, source_target_pairs={{0,1},{1,2},{2,3},{3,0},{4,5},{5,6},{6,7},{7,4},{8,9},{9,10},{10,1... | collective-permute-start | bytes 516104 | tf_op jit(solution)/shard_map/ppermute | solution.py:265
  44.6 30.8 %collective-permute-start.16 = (bf16[192,896]{1,0:T(8,128)(2,1)S(1)}, bf16[192,896]{1,0:T(8,128)(2,1)S(1)}, u32[]{:S(2)}, u32[]{:S(2)}) collective-permute-start(bf16[192,896]{1,0:T(8,128)(2,1)S(1)} %get-tuple-element.64), channel_id=1, source_target_pairs={{0,1},{1,2},{2,3},{3,0},{4,5},{5,6},{6,7},{7,4},{8,9},{9,10},{10,1... | collective-permute-start | bytes 1032200 | tf_op jit(solution)/shard_map/ppermute | solution.py:265
  46.2 29.1 %collective-permute-start.17 = (bf16[192,896]{1,0:T(8,128)(2,1)S(1)}, bf16[192,896]{1,0:T(8,128)(2,1)S(1)}, u32[]{:S(2)}, u32[]{:S(2)}) collective-permute-start(bf16[192,896]{1,0:T(8,128)(2,1)S(1)} %get-tuple-element.65), channel_id=1, source_target_pairs={{0,3},{1,0},{2,1},{3,2},{4,7},{5,4},{6,5},{7,6},{8,11},{9,8},{10,9... | collective-permute-start | bytes 1032200 | tf_op jit(solution)/shard_map/ppermute | solution.py:265
  46.7 28.7 %collective-permute-start.18 = (bf16[192,896]{1,0:T(8,128)(2,1)S(1)}, bf16[192,896]{1,0:T(8,128)(2,1)S(1)}, u32[]{:S(2)}, u32[]{:S(2)}) collective-permute-start(bf16[192,896]{1,0:T(8,128)(2,1)S(1)} %get-tuple-element.66), channel_id=1, source_target_pairs={{0,2},{1,3},{2,0},{3,1},{4,6},{5,7},{6,4},{7,5},{8,10},{9,11},{10,... | collective-permute-start | bytes 1032200 | tf_op jit(solution)/shard_map/ppermute | solution.py:265
  49.0 18.5 %collective-permute-start.13 = (bf16[96,896]{1,0:T(8,128)(2,1)S(1)}, bf16[96,896]{1,0:T(8,128)(2,1)S(1)}, u32[]{:S(2)}, u32[]{:S(2)}) collective-permute-start(bf16[96,896]{1,0:T(8,128)(2,1)S(1)} %get-tuple-element.61), channel_id=1, source_target_pairs={{0,3},{1,0},{2,1},{3,2},{4,7},{5,4},{6,5},{7,6},{8,11},{9,8},{10,9... | collective-permute-start | bytes 516104 | tf_op jit(solution)/shard_map/ppermute | solution.py:265
  50.3 21.0 %collective-permute-start.14 = (bf16[96,896]{1,0:T(8,128)(2,1)S(1)}, bf16[96,896]{1,0:T(8,128)(2,1)S(1)}, u32[]{:S(2)}, u32[]{:S(2)}) collective-permute-start(bf16[96,896]{1,0:T(8,128)(2,1)S(1)} %get-tuple-element.62), channel_id=1, source_target_pairs={{0,2},{1,3},{2,0},{3,1},{4,6},{5,7},{6,4},{7,5},{8,10},{9,11},{10,... | collective-permute-start | bytes 516104 | tf_op jit(solution)/shard_map/ppermute | solution.py:265
  67.5 10.9 %collective-permute-start.7 = (bf16[96,896]{1,0:T(8,128)(2,1)S(1)}, bf16[96,896]{1,0:T(8,128)(2,1)S(1)}, u32[]{:S(2)}, u32[]{:S(2)}) collective-permute-start(bf16[96,896]{1,0:T(8,128)(2,1)S(1)} %get-tuple-element.53), channel_id=1, source_target_pairs={{0,1},{1,2},{2,3},{3,0},{4,5},{5,6},{6,7},{7,4},{8,9},{9,10},{10,1... | collective-permute-start | bytes 516104 | tf_op jit(solution)/shard_map/ppermute | solution.py:265
  72.2 15.8 %collective-permute-start.15 = (bf16[128,896]{1,0:T(8,128)(2,1)S(1)}, bf16[128,896]{1,0:T(8,128)(2,1)S(1)}, u32[]{:S(2)}, u32[]{:S(2)}) collective-permute-start(bf16[128,896]{1,0:T(8,128)(2,1)S(1)} %shard_map.117), channel_id=1, source_target_pairs={{0,64},{32,96},{64,0},{96,32},{1,65},{33,97},{65,1},{97,33},{2,66}... | collective-permute-start | bytes 688136 | tf_op jit(solution)/shard_map/ppermute | solution.py:265
  76.3 11.8 %collective-permute-start.19 = (bf16[128,896]{1,0:T(8,128)(2,1)S(1)}, bf16[128,896]{1,0:T(8,128)(2,1)S(1)}, u32[]{:S(2)}, u32[]{:S(2)}) collective-permute-start(bf16[128,896]{1,0:T(8,128)(2,1)S(1)} %get-tuple-element.68), channel_id=1, source_target_pairs={{0,96},{32,0},{64,32},{96,64},{1,97},{33,1},{65,33},{97,65},{2,98}... | collective-permute-start | bytes 688136 | tf_op jit(solution)/shard_map/ppermute | solution.py:265
  77.5 10.6 %collective-permute-start.20 = (bf16[128,896]{1,0:T(8,128)(2,1)S(1)}, bf16[128,896]{1,0:T(8,128)(2,1)S(1)}, u32[]{:S(2)}, u32[]{:S(2)}) collective-permute-start(bf16[128,896]{1,0:T(8,128)(2,1)S(1)} %get-tuple-element.69), channel_id=1, source_target_pairs={{0,32},{32,64},{64,96},{96,0},{1,33},{33,65},{65,97},{97,1},{2,34}... | collective-permute-start | bytes 688136 | tf_op jit(solution)/shard_map/ppermute | solution.py:265
  78.4 8.8 %collective-permute-start.9 = (bf16[96,896]{1,0:T(8,128)(2,1)S(1)}, bf16[96,896]{1,0:T(8,128)(2,1)S(1)}, u32[]{:S(2)}, u32[]{:S(2)}) collective-permute-start(bf16[96,896]{1,0:T(8,128)(2,1)S(1)} %get-tuple-element.55), channel_id=1, source_target_pairs={{0,2},{1,3},{2,0},{3,1},{4,6},{5,7},{6,4},{7,5},{8,10},{9,11},{10,... | collective-permute-start | bytes 516104 | tf_op jit(solution)/shard_map/ppermute | solution.py:265
  89.4 18.6 %all-to-all-start = ((bf16[8,16,896]{2,1,0:T(8,128)(2,1)}), bf16[8,16,896]{2,1,0:T(8,128)(2,1)S(1)}, u32[]{:S(2)}, u32[]{:S(2)}) async-start(bf16[8,16,896]{2,1,0:T(8,128)(2,1)} %shard_map.119), calls=%async_computation | async-start | bytes 458752 | tf_op jit(solution)/shard_map/all_to_all | solution.py:269
  103.7 24.1 %collective-permute-start.24 = (bf16[1536,256]{1,0:T(8,128)(2,1)}, bf16[1536,256]{1,0:T(8,128)(2,1)}, u32[]{:S(2)}, u32[]{:S(2)}) collective-permute-start(bf16[1536,256]{1,0:T(8,128)(2,1)} %get-tuple-element.75), channel_id=1, source_target_pairs={{0,128},{128,0},{1,129},{129,1},{2,130},{130,2},{3,131},{131,3},{4... | collective-permute-start | bytes 2359304 | tf_op jit(solution)/shard_map/ppermute | solution.py:265
  103.7 25.8 %collective-permute-start.25 = (bf16[1536,256]{1,0:T(8,128)(2,1)}, bf16[1536,256]{1,0:T(8,128)(2,1)}, u32[]{:S(2)}, u32[]{:S(2)}) collective-permute-start(bf16[1536,256]{1,0:T(8,128)(2,1)} %get-tuple-element.76), channel_id=1, source_target_pairs={{0,128},{128,0},{1,129},{129,1},{2,130},{130,2},{3,131},{131,3},{4... | collective-permute-start | bytes 2359304 | tf_op jit(solution)/shard_map/ppermute | solution.py:265
  104.2 25.3 %collective-permute-start.26 = (bf16[1536,256]{1,0:T(8,128)(2,1)}, bf16[1536,256]{1,0:T(8,128)(2,1)}, u32[]{:S(2)}, u32[]{:S(2)}) collective-permute-start(bf16[1536,256]{1,0:T(8,128)(2,1)} %get-tuple-element.77), channel_id=1, source_target_pairs={{0,128},{128,0},{1,129},{129,1},{2,130},{130,2},{3,131},{131,3},{4... | collective-permute-start | bytes 2359304 | tf_op jit(solution)/shard_map/ppermute | solution.py:265
  125.8 10.7 %collective-permute-start.21 = (bf16[128,768]{1,0:T(8,128)(2,1)S(1)}, bf16[128,768]{1,0:T(8,128)(2,1)S(1)}, u32[]{:S(2)}, u32[]{:S(2)}) collective-permute-start(bf16[128,768]{1,0:T(8,128)(2,1)S(1)} %get-tuple-element.70.refs_0_), channel_id=1, source_target_pairs={{0,1},{1,2},{2,3},{3,0},{4,5},{5,6},{6,7},{7,4},{8,9},{9,10},{10,1... | collective-permute-start | bytes 589832 | tf_op jit(solution)/shard_map/ppermute | solution.py:265
  126.0 10.4 %collective-permute-start.22 = (bf16[128,768]{1,0:T(8,128)(2,1)S(1)}, bf16[128,768]{1,0:T(8,128)(2,1)S(1)}, u32[]{:S(2)}, u32[]{:S(2)}) collective-permute-start(bf16[128,768]{1,0:T(8,128)(2,1)S(1)} %get-tuple-element.70.refs_0_), channel_id=1, source_target_pairs={{0,3},{1,0},{2,1},{3,2},{4,7},{5,4},{6,5},{7,6},{8,11},{9,8},{10,9... | collective-permute-start | bytes 589832 | tf_op jit(solution)/shard_map/ppermute | solution.py:265
  127.8 10.4 %collective-permute-start.23 = (bf16[128,768]{1,0:T(8,128)(2,1)S(1)}, bf16[128,768]{1,0:T(8,128)(2,1)S(1)}, u32[]{:S(2)}, u32[]{:S(2)}) collective-permute-start(bf16[128,768]{1,0:T(8,128)(2,1)S(1)} %get-tuple-element.70.refs_0_), channel_id=1, source_target_pairs={{0,2},{1,3},{2,0},{3,1},{4,6},{5,7},{6,4},{7,5},{8,10},{9,11},{10,... | collective-permute-start | bytes 589832 | tf_op jit(solution)/shard_map/ppermute | solution.py:265
  (19 other events, 168.8 us)
where the time goes:
time: 141 us; the launch traced here: 140 us
  waiting for transfers between devices  44.3 us (31%)
  starting transfers between devices  41.6 us (30%)
  Pallas kernels  30.2 us (21%)
  blocking collectives  15.2 us (11%)
  local copies, waits for them, and re-layouts  7.42 us (5%)
    ppermute x27, waiting for transfers between devices, shift(): lax.ppermute(value, axis, [(i, (i + offset) % size) for i in range(size)])  40.4 us
    ppermute x27, starting transfers between devices, shift(): lax.ppermute(value, axis, [(i, (i + offset) % size) for i in range(size)])  33.2 us
    pallas_call x15, Pallas kernels, call(): pl.pallas_call(kernel, out_shape=outs, in_specs=specs, out_specs=[spec] *...  30.2 us
    all_to_all x1, blocking collectives, exchange(): return lax.all_to_all(value, axis, split_axis=0, concat_axis=0, tiled=True)  15.2 us
    all_to_all x1, starting transfers between devices, exchange(): return lax.all_to_all(value, axis, split_axis=0, concat_axis=0, tiled=True)  8.47 us
    unnamed x30, local copies, waits for them, and re-layouts  7.42 us
    all_to_all x1, waiting for transfers between devices, exchange(): return lax.all_to_all(value, axis, split_axis=0, concat_axis=0, tiled=True)  3.82 us
  transfers between devices with their start and end apart: 28, of which 13 were waited for; matrix products, arithmetic and copies ran while one was open for 0% of the time, Pallas kernels for 19%

commit v1 on v0

v1 whole, which is shorter than its diff:
```python
import functools

import jax
import jax.numpy as jnp
from jax import lax
from jax.experimental import pallas as pl
from jax.experimental.pallas import tpu as pltpu
from jax.sharding import Mesh, PartitionSpec as P


BF = jnp.bfloat16
F32 = jnp.float32
NT = (((1,), (1,)), ((), ()))
TN = (((0,), (0,)), ((), ()))
LANES = 128
OFFSETS = (0, 1, -1, 2)


MIB = 1 << 20


def array(*shape):
    return pltpu.VMEM(shape, BF)


def plain(*shape):
    return pltpu.HBM(shape, BF)


def call(kernel, outs, operands, limit=8, scratch=(), free=(), unblocked=()):
    spec = pl.BlockSpec(memory_space=pltpu.VMEM)
    specs = [pl.BlockSpec(memory_space=pltpu.SMEM)]
    kept = [operands[0]]
    for k, value in enumerate(operands[1:]):
        specs.append(pl.BlockSpec(memory_space=pl.ANY) if k in unblocked else spec)
        space = pltpu.HBM if k in free else pltpu.VMEM
        kept.append(pltpu.with_memory_space_constraint(value, space))
    return pl.pallas_call(
        kernel,
        out_shape=outs,
        in_specs=specs,
        out_specs=[spec] * len(outs),
        scratch_shapes=list(scratch),
        compiler_params=pltpu.CompilerParams(vmem_limit_bytes=limit * MIB),
    )(*kept)


def routing(pos, ids_ref, offsets):
    tokens = ids_ref.shape[1]
    ids = ids_ref[...]
    before = (
        lax.broadcasted_iota(jnp.int32, (tokens, tokens), 0)
        < lax.broadcasted_iota(jnp.int32, (tokens, tokens), 1)
    ).astype(BF)
    hits = [ids == lax.rem(pos[1] + offset + 4, 4) for offset in offsets]
    rows = [jnp.max(hit.astype(F32), axis=0, keepdims=True) for hit in hits]
    member = jnp.concatenate(rows + [jnp.zeros((8 - len(rows), tokens), F32)], axis=0)
    rank = jnp.dot(member.astype(BF), before, preferred_element_type=F32)
    return member, rank, hits


def picks(rank, member, j, slots, first):
    slot = lax.broadcasted_iota(jnp.int32, (slots, rank.shape[1]), 0)
    slot = (slot + first).astype(F32)
    hit = (slot == rank[j : j + 1]) & (member[j : j + 1] > 0.5)
    return jnp.where(hit, 1.0, 0.0).astype(BF)


def facts_of(pick, hit, gw_ref):
    tokens = pick.shape[1]
    weight = jnp.sum(jnp.where(hit, gw_ref[...].astype(F32), 0.0), axis=0, keepdims=True)
    facts = jnp.where(lax.broadcasted_iota(jnp.int32, (LANES, tokens), 0) == 0, weight, 0.0)
    return lax.dot_general(pick, facts.astype(BF), NT, preferred_element_type=F32).astype(BF)


def far_kernel(pos, ids_ref, gw_ref, tok_ref, cot_ref, out, tok_out, cot_out, sems):
    copies = [
        pltpu.make_async_copy(tok_ref, tok_out, sems.at[0]),
        pltpu.make_async_copy(cot_ref, cot_out, sems.at[1]),
    ]
    for copy in copies:
        copy.start()
    member, rank, hits = routing(pos, ids_ref, (2,))
    width = tok_ref.shape[1]
    slots = out.shape[0]
    pick = picks(rank, member, 0, slots, lax.rem(pos[3], 2) * slots)
    out[:, width:] = facts_of(pick, hits[0], gw_ref)
    for copy in copies:
        copy.wait()

    @pl.when(pos[3] < 2)
    def _():
        out[:, :width] = jnp.dot(pick, tok_out[...], preferred_element_type=F32).astype(BF)

    @pl.when(pos[3] >= 2)
    def _():
        out[:, :width] = jnp.dot(pick, cot_out[...], preferred_element_type=F32).astype(BF)


def near_kernel(offsets, pos, ids_ref, gw_ref, tok_ref, cot_ref, *outs):
    member, rank, hits = routing(pos, ids_ref, offsets)
    width = tok_ref.shape[1]
    for j, out in enumerate(outs):
        pick = picks(rank, member, j, out.shape[0], 0)
        out[:, :width] = jnp.dot(pick, tok_ref[...], preferred_element_type=F32).astype(BF)
        out[:, width : 2 * width] = jnp.dot(
            pick, cot_ref[...], preferred_element_type=F32
        ).astype(BF)
        out[:, 2 * width :] = facts_of(pick, hits[j], gw_ref)


def expert_kernel(kind, pos, *refs):
    count = {"here": 1, "far": 4, "sides": 2}[kind]
    pieces, refs = refs[:count], refs[count:]
    wg_own, wg_sib, wu_own, wu_sib, wd_own, wd_sib = (ref.at[0] for ref in refs[:6])
    ends = 14 if kind == "sides" else 10
    sends, aux_ref, whole = refs[6:ends], refs[ends], refs[-1]
    half, units = wg_own.shape
    width = 2 * half
    block = half // 2
    if kind == "far":
        msgs = [refs[ends + 1]]
        rows = pieces[0].shape[0]
        for piece, shift in zip(pieces, (0, 1, -1, 2)):
            source = lax.rem(pos[3] - shift + 4, 4)
            at = pl.multiple_of(lax.rem(source, 2) * rows, 16)
            column = pl.multiple_of(lax.div(source, 2) * width, LANES)
            msgs[0][pl.ds(at, rows), pl.ds(column, width)] = piece[:, :width]
            msgs[0][pl.ds(at, rows), 2 * width :] = piece[:, width:]
    else:
        msgs = pieces
    own = pl.multiple_of(pos[0] * half, LANES)
    sib = pl.multiple_of((1 - pos[0]) * half, LANES)

    def columns(at, size):
        parts = [msg[:, pl.ds(at, size)] for msg in msgs]
        return parts[0] if len(parts) == 1 else jnp.concatenate(parts, axis=0)

    facts = columns(2 * width, LANES)
    g = facts[:, :1].astype(F32)

    def product(left_own, left_sib, w_own, w_sib):
        left = jnp.dot(left_own, w_own[...], preferred_element_type=F32)
        return left + jnp.dot(left_sib, w_sib[...], preferred_element_type=F32)

    x_own, x_sib = columns(own, half), columns(sib, half)
    gate = product(x_own, x_sib, wg_own, wg_sib)
    up = product(x_own, x_sib, wu_own, wu_sib)
    back = product(columns(width + own, half), columns(width + sib, half), wd_own, wd_sib)
    sig = jax.nn.sigmoid(gate)
    act = gate * sig
    hid = act * up
    share = hid.astype(BF).astype(F32) * back
    hg = g * back
    dpg = (hg * up * sig * (1.0 + gate * (1.0 - sig))).astype(BF)
    dpu = (hg * act).astype(BF)
    aux_ref[:, :units] = dpg
    aux_ref[:, units : 2 * units] = dpu
    aux_ref[:, 2 * units : 3 * units] = (g * hid).astype(BF)
    for j in range(4):
        wg, wu = (wg_own, wu_own) if j < 2 else (wg_sib, wu_sib)
        at = (j % 2) * block
        part = lax.dot_general(dpg, wg[at : at + block, :], NT, preferred_element_type=F32)
        part += lax.dot_general(dpu, wu[at : at + block, :], NT, preferred_element_type=F32)
        whole[j] = part.astype(BF)
    slots = sends[0].shape[0] - 8
    for c in range(len(sends) // 4):
        at = slice(c * slots, (c + 1) * slots)
        padded = jnp.concatenate([share[at], jnp.zeros((LANES - slots, units), F32)], axis=0)
        line = lax.dot_general(
            jnp.ones((8, units), F32), padded, NT,
            precision=lax.Precision.HIGHEST, preferred_element_type=F32,
        ).astype(BF)
        for j in range(4):
            send = sends[4 * c + j]
            send[:slots] = whole[lax.rem(pos[3] + j, 4), at, :]
            send[slots:, :LANES] = line
            send[slots:, LANES:] = jnp.zeros((8, block - LANES), BF)


def combine_kernel(pos, ids_ref, *refs):
    out_ref = refs[-1]
    zs, rows, wide = out_ref.shape
    tokens = zs * rows
    width = wide - LANES
    slots = refs[0].shape[0] - 8
    member, rank, _ = routing(pos, ids_ref, OFFSETS)
    result = jnp.zeros((tokens, width), F32)
    gates = []
    for k in range(4):
        group = refs[4 * k : 4 * k + 4]
        total = group[0][...].astype(F32)
        for ref in group[1:]:
            total += ref[...].astype(F32)
        total = total.astype(BF)
        pick = picks(rank, member, k, slots, 0)
        result += lax.dot_general(pick, total[:slots], TN, preferred_element_type=F32)
        pick = picks(rank, member, k, LANES, 0)
        line = jnp.dot(total[slots:, :LANES], pick, preferred_element_type=F32)
        gates.append(line[:1])
    gates = jnp.concatenate(gates + [jnp.zeros((rows - 4, tokens), F32)], axis=0).astype(BF)
    result = result.astype(BF)
    for z in range(zs):
        out_ref[z, :, :width] = result[z * rows : (z + 1) * rows]
        out_ref[z, :, width:] = gates


def gather_kernel(pos, ids_ref, got_ref, out_ref, gate_ref):
    width = out_ref.shape[2]
    total = got_ref[0].astype(F32)
    for z in range(1, got_ref.shape[0]):
        total += got_ref[z].astype(F32)
    slab = total[:, :width].astype(BF)
    for z in range(out_ref.shape[0]):
        out_ref[z] = slab
    ids = ids_ref[...]
    gates = jnp.zeros(ids.shape, F32)
    for k, offset in enumerate(OFFSETS):
        hit = ids == lax.rem(pos[1] + offset + 4, 4)
        gates += jnp.where(hit, total[k : k + 1, width:], 0.0)
    gate_ref[...] = gates.astype(BF)


def columns_kernel(pos, *refs):
    pieces, out_ref = refs[:4], refs[4]
    width = pieces[0].shape[1]
    for piece, shift in zip(pieces, (0, 1, -1, 2)):
        block = lax.rem(pos[3] - shift + 4 + 2 * pos[0], 4)
        out_ref[:, pl.ds(pl.multiple_of(block * width, LANES), width)] = piece[...]


def grad_kernel(other, pos, here_ref, far_ref, plus_ref, minus_ref, *refs):
    msgs = (here_ref, far_ref, plus_ref, minus_ref)
    auxs, added, outs = refs[:3], refs[3:-3], refs[-3:]
    half, units = outs[0].shape
    width = 2 * half
    base = ((1 - pos[0]) if other else pos[0]) * half
    step = 256
    right = jnp.concatenate([ref[:, : 2 * units] for ref in auxs], axis=0)
    hidden = jnp.concatenate([ref[:, 2 * units : 3 * units] for ref in auxs], axis=0)
    for i in range(half // step):
        rows = slice(i * step, (i + 1) * step)

        def left(start):
            at = pl.multiple_of(start + base + i * step, LANES)
            return jnp.concatenate([msg[:, pl.ds(at, step)] for msg in msgs], axis=0)

        both = lax.dot_general(left(0), right, TN, preferred_element_type=F32)
        down = lax.dot_general(left(width), hidden, TN, preferred_element_type=F32)
        for k, total in enumerate((both[:, :units], both[:, units:], down)):
            if added:
                total += added[k][rows].astype(F32)
            outs[k][rows] = total.astype(BF)


def shift(value, axis, offset):
    size = lax.axis_size(axis)
    return lax.ppermute(value, axis, [(i, (i + offset) % size) for i in range(size)])


def shift_two(value, offset, column):
    pairs = [
        (4 * i + j, 4 * ((i + offset) % 4) + (j + column) % 4) for i in range(4) for j in range(4)
    ]
    return lax.ppermute(value, ("expert", "y"), pairs)


def exchange(value, axis):
    return lax.all_to_all(value, axis, split_axis=0, concat_axis=0, tiled=True)


def after(value, *others):
    return lax.optimization_barrier((value, *others))[0]


def on_device(tokens, cotangent, gate_weights, expert_ids, w_gate, w_up, w_down):
    tok_count, width = tokens.shape
    slots = tok_count * 3 // 4
    units = w_gate.shape[2]
    block = width // 4
    zs = lax.axis_size("z")
    rows = tok_count // zs
    long = 2 * width + LANES
    pos = jnp.stack(
        [lax.axis_index(name) for name in ("dp", "expert", "z", "y")]
    ).astype(jnp.int32)
    given = (expert_ids.T, gate_weights.T)

    far, tokens, cotangent = call(
        far_kernel,
        [array(slots // 2, width + LANES), array(*tokens.shape), array(*tokens.shape)],
        (pos, *given, tokens, cotangent),
        free=(0, 1, 2, 3),
        unblocked=(2, 3),
        scratch=[pltpu.SemaphoreType.DMA((2,))],
    )
    given = (*given, tokens, cotangent)
    plus, minus = call(
        functools.partial(near_kernel, (1, -1)),
        [array(slots, long)] * 2,
        (pos, *given),
        free=(0, 1),
    )
    then = after(pos, plus)
    (here,) = call(
        functools.partial(near_kernel, (0,)), [array(slots, long)], (then, *given),
        free=(0, 1),
    )
    weights = []
    for own in (w_gate, w_up, w_down):
        weights += [own, shift(after(own, plus), "dp", 1)]
    plus, minus = shift(plus, "expert", 1), shift(minus, "expert", -1)
    far = shift(far, "expert", 2)
    far = [far] + [shift(far, "y", offset) for offset in (1, -1, 2)]

    def expert(pos, msgs, kind):
        count = 2 if kind == "sides" else 1
        return call(
            functools.partial(expert_kernel, kind),
            [array(slots + 8, block)] * (4 * count)
            + [plain(count * slots, 3 * units)]
            + [array(slots, long)] * (kind == "far"),
            (pos, *msgs, *weights),
            scratch=[pltpu.VMEM((4, count * slots, block), BF)],
        )

    def back(sends, offset):
        kept = [sends[0]] if offset == 0 else [shift_two(sends[0], -offset, 0)]
        return kept + [shift_two(sends[j], -offset, j) for j in (1, 3, 2)]

    local = expert(pos, [here], "here")
    remote = expert(after(pos, local[0]), far, "far")
    sides = expert(after(pos, remote[0]), [plus, minus], "sides")
    groups = [*back(local[:4], 0), *back(sides[:4], 1), *back(sides[4:8], -1), *back(remote[:4], 2)]
    (mine,) = call(combine_kernel, [plain(zs, rows, block + LANES)], (pos, expert_ids.T, *groups))
    mine, gate_grad = call(
        gather_kernel,
        [plain(zs, rows, block), plain(2, tok_count)],
        (pos, expert_ids.T, exchange(mine, "z")),
    )
    slab = exchange(mine, "z").reshape(tok_count, block)
    (input_grad,) = call(
        columns_kernel,
        [plain(tok_count, width)],
        (pos, slab, *[shift(slab, "y", offset) for offset in (1, -1, 2)]),
    )
    used = [here, remote[5], plus, minus, local[4], remote[4], sides[8]]
    half = width // 2
    away = call(
        functools.partial(grad_kernel, True), [array(half, units)] * 3, (pos, *used),
        limit=12,
    )
    received = [shift(part, "dp", 1) for part in away]
    grads = call(
        functools.partial(grad_kernel, False), [plain(half, units)] * 3, (pos, *used, *received),
        limit=12,
    )
    return (input_grad, gate_grad.T, grads[0][None], grads[1][None], grads[2][None])


def solution(mesh):
    dp, experts, tensor = (mesh.shape[name] for name in ("dp", "expert", "tensor"))
    view = Mesh(mesh.devices.reshape(dp, experts, tensor // 4, 4), ("dp", "expert", "z", "y"))
    row = P(("dp", "expert"), None)
    weight = P("expert", "dp", ("z", "y"))

    return jax.shard_map(
        on_device,
        mesh=view,
        in_specs=(row, row, row, row, weight, weight, weight),
        out_specs=(row, row, weight, weight, weight),
        check_vma=False,
    )
```

time: 141 us -> 129 us (0.915)
  the two profiles are of different devices: /device:TPU:8 before, /device:TPU:2 now
where the time goes in v1:
time: 129 us
  starting transfers between devices  53.6 us (42%)
  Pallas kernels  27.7 us (21%)
  waiting for transfers between devices  27.2 us (21%)
  blocking collectives  14.2 us (11%)
  local copies, waits for them, and re-layouts  5.3 us (4%)
    ppermute x15, starting transfers between devices, shift_two(): return lax.ppermute(value, ('expert', 'y'), pairs)  32 us
    pallas_call x11, Pallas kernels, call(): pl.pallas_call(kernel, out_shape=outs, in_specs=specs, out_specs=[spec] *...  27.7 us
    all_to_all x1, blocking collectives, exchange(): return lax.all_to_all(value, axis, split_axis=0, concat_axis=0, tiled=True)  14.2 us
    ppermute x15, starting transfers between devices, shift(): lax.ppermute(value, axis, [(i, (i + offset) % size) for i in range(size)])  13.1 us
    ppermute x15, waiting for transfers between devices, shift(): lax.ppermute(value, axis, [(i, (i + offset) % size) for i in range(size)])  12.6 us
    all_to_all x1, waiting for transfers between devices, exchange(): return lax.all_to_all(value, axis, split_axis=0, concat_axis=0, tiled=True)  11.3 us
    all_to_all x1, starting transfers between devices, exchange(): return lax.all_to_all(value, axis, split_axis=0, concat_axis=0, tiled=True)  8.59 us
    unnamed x28, local copies, waits for them, and re-layouts  5.3 us
  transfers between devices with their start and end apart: 31, of which 9 were waited for; matrix products, arithmetic and copies ran while one was open for 0% of the time, Pallas kernels for 18%

profile of v1, /device:TPU:2, one launch (start us, length us, event | category | flops | bytes accessed | tf_op | source)
XLA Modules:
  0.0 128.8 jit_solution(7466067731511695643)
XLA Ops:
  0.7 2.5 %shard_map.110 = (bf16[48,3200]{1,0:T(8,128)(2,1)S(1)}, bf16[128,3072]{1,0:T(8,128)(2,1)S(1)}, bf16[128,3072]{1,0:T(8,128)(2,1)S(1)}) custom-call(s32[4]{0:T(128)S(1)} %pad_add_fusion.pos, s32[2,128]{1,0:T(2,128)} %bitcast.15, bf16[2,128]{1,0:T(2,128)(2,1)} %bitcast.20, bf16[128,3072]{1,0:T(8,128)(2,1)} %tok_ref.1, bf16[128,3072]{1,0:T(8,128)(2,1)} %cot_ref.1), custom_call_target="tpu_custom_call" | custom-call | tf_op jit(solution)/shard_map/pallas_call | solution.py:38
  3.2 2.2 %collective-permute-start.6 = (bf16[48,3200]{1,0:T(8,128)(2,1)S(1)}, bf16[48,3200]{1,0:T(8,128)(2,1)S(1)}, u32[]{:S(2)}, u32[]{:S(2)}) collective-permute-start(bf16[48,3200]{1,0:T(8,128)(2,1)S(1)} %get-tuple-element.56), channel_id=1, source_target_pairs={{0,64},{32,96},{64,0},{96,32},{1,65},{33,97},{65,1},{97,33},{2,66}... | collective-permute-start | bytes 921608 | tf_op jit(solution)/shard_map/ppermute | solution.py:258
  9.2 5.8 %collective-permute-done.6.refs_0_ = bf16[48,3200]{1,0:T(8,128)(2,1)S(1)} collective-permute-done((bf16[48,3200]{1,0:T(8,128)(2,1)S(1)}, bf16[48,3200]{1,0:T(8,128)(2,1)S(1)}, u32[]{:S(2)}, u32[]{:S(2)}) %collective-permute-start.6) | collective-permute-done | bytes 307232 | tf_op jit(solution)/shard_map/ppermute | solution.py:258
  15.3 3.2 %collective-permute-start.9 = (bf16[48,3200]{1,0:T(8,128)(2,1)S(1)}, bf16[48,3200]{1,0:T(8,128)(2,1)S(1)}, u32[]{:S(2)}, u32[]{:S(2)}) collective-permute-start(bf16[48,3200]{1,0:T(8,128)(2,1)S(1)} %collective-permute-done.6.refs_0_), channel_id=1, source_target_pairs={{0,2},{1,3},{2,0},{3,1},{4,6},{5,7},{6,4},{7,5},{8,10},{9,11},{10,... | collective-permute-start | bytes 921608 | tf_op jit(solution)/shard_map/ppermute | solution.py:258
  21.8 3.4 %shard_map.113 = (bf16[104,768]{1,0:T(8,128)(2,1)S(1)}, bf16[104,768]{1,0:T(8,128)(2,1)S(1)}, bf16[104,768]{1,0:T(8,128)(2,1)S(1)}, bf16[104,768]{1,0:T(8,128)(2,1)S(1)}, bf16[96,768]{1,0:T(8,128)(2,1)}) custom-call(s32[4]{0:T(128)S(1)} %pad_add_fusion.pos, bf16[96,6272]{1,0:T(8,128)(2,1)S(1)} %shard_map.112.refs_0_.here_ref, ...), custom_call_target="tpu_custom_call" | custom-call | tf_op jit(solution)/shard_map/pallas_call | solution.py:38
  28.5 3.1 %collective-permute-done.8.refs_2_ = bf16[48,3200]{1,0:T(8,128)(2,1)S(1)} collective-permute-done((bf16[48,3200]{1,0:T(8,128)(2,1)S(1)}, bf16[48,3200]{1,0:T(8,128)(2,1)S(1)}, u32[]{:S(2)}, u32[]{:S(2)}) %collective-permute-start.8) | collective-permute-done | bytes 307232 | tf_op jit(solution)/shard_map/ppermute | solution.py:258
  31.7 2.6 %collective-permute-start.4 = (bf16[104,768]{1,0:T(8,128)(2,1)S(1)}, bf16[104,768]{1,0:T(8,128)(2,1)S(1)}, u32[]{:S(2)}, u32[]{:S(2)}) collective-permute-start(bf16[104,768]{1,0:T(8,128)(2,1)S(1)} %get-tuple-element.53), channel_id=1, source_target_pairs={{0,3},{1,0},{2,1},{3,2},{32,35},{33,32},{34,33},{35,34},{64,67},{6... | collective-permute-start | bytes 479240 | tf_op jit(solution)/shard_map/ppermute | solution.py:265
  34.9 3.5 %shard_map.114 = (bf16[104,768]{1,0:T(8,128)(2,1)S(1)}, bf16[104,768]{1,0:T(8,128)(2,1)S(1)}, bf16[104,768]{1,0:T(8,128)(2,1)S(1)}, bf16[104,768]{1,0:T(8,128)(2...) custom-call(s32[4]{0:T(128)S(1)} %pad_add_fusion.pos, ...), custom_call_target="tpu_custom_call" | custom-call | tf_op jit(solution)/shard_map/pallas_call | solution.py:38
  39.6 4.6 %collective-permute-start.22 = (bf16[104,768]{1,0:T(8,128)(2,1)S(1)}, bf16[104,768]{1,0:T(8,128)(2,1)S(1)}, u32[]{:S(2)}, u32[]{:S(2)}) collective-permute-start(bf16[104,768]{1,0:T(8,128)(2,1)S(1)} %get-tuple-element.69), channel_id=1, source_target_pairs={{0,67},{1,64},{2,65},{3,66},{32,99},{33,96},{34,97},{35,98},{64,3}... | collective-permute-start | bytes 479240 | tf_op jit(solution)/shard_map/ppermute | solution.py:265
  44.2 4.0 %collective-permute-start.23 = (bf16[104,768]{1,0:T(8,128)(2,1)S(1)}, bf16[104,768]{1,0:T(8,128)(2,1)S(1)}, u32[]{:S(2)}, u32[]{:S(2)}) collective-permute-start(bf16[104,768]{1,0:T(8,128)(2,1)S(1)} %get-tuple-element.70), channel_id=1, source_target_pairs={{0,66},{1,67},{2,64},{3,65},{32,98},{33,99},{34,96},{35,97},{64,2}... | collective-permute-start | bytes 479240 | tf_op jit(solution)/shard_map/ppermute | solution.py:265
  48.2 3.7 %shard_map.115 = (bf16[104,768]{1,0:T(8,128)(2,1)S(1)}, bf16[104,768]{1,0:T(8,128)(2,1)S(1)}, bf16[104,768]{1,0:T(8,128)(2,1)S(1)}, bf16[104,768]{1,0:T(8,128)(2...) custom-call(s32[4]{0:T(128)S(1)} %pad_add_fusion.pos, ...), custom_call_target="tpu_custom_call" | custom-call | tf_op jit(solution)/shard_map/pallas_call | solution.py:38
  52.4 2.0 %collective-permute-start.12 = (bf16[104,768]{1,0:T(8,128)(2,1)S(1)}, bf16[104,768]{1,0:T(8,128)(2,1)S(1)}, u32[]{:S(2)}, u32[]{:S(2)}) collective-permute-start(bf16[104,768]{1,0:T(8,128)(2,1)S(1)} %get-tuple-element.60), channel_id=1, source_target_pairs={{0,96},{1,97},{2,98},{3,99},{32,0},{33,1},{34,2},{35,3},{64,32},{6... | collective-permute-start | bytes 479240 | tf_op jit(solution)/shard_map/ppermute | solution.py:265
  54.4 2.2 %collective-permute-start.13 = (bf16[104,768]{1,0:T(8,128)(2,1)S(1)}, bf16[104,768]{1,0:T(8,128)(2,1)S(1)}, u32[]{:S(2)}, u32[]{:S(2)}) collective-permute-start(bf16[104,768]{1,0:T(8,128)(2,1)S(1)} %get-tuple-element.61), channel_id=1, source_target_pairs={{0,97},{1,98},{2,99},{3,96},{32,1},{33,2},{34,3},{35,0},{64,33},{6... | collective-permute-start | bytes 479240 | tf_op jit(solution)/shard_map/ppermute | solution.py:265
  56.6 2.2 %collective-permute-start.14 = (bf16[104,768]{1,0:T(8,128)(2,1)S(1)}, bf16[104,768]{1,0:T(8,128)(2,1)S(1)}, u32[]{:S(2)}, u32[]{:S(2)}) collective-permute-start(bf16[104,768]{1,0:T(8,128)(2,1)S(1)} %get-tuple-element.62), channel_id=1, source_target_pairs={{0,99},{1,96},{2,97},{3,98},{32,3},{33,0},{34,1},{35,2},{64,35},{6... | collective-permute-start | bytes 479240 | tf_op jit(solution)/shard_map/ppermute | solution.py:265
  61.1 3.3 %collective-permute-start.17 = (bf16[104,768]{1,0:T(8,128)(2,1)S(1)}, bf16[104,768]{1,0:T(8,128)(2,1)S(1)}, u32[]{:S(2)}, u32[]{:S(2)}) collective-permute-start(bf16[104,768]{1,0:T(8,128)(2,1)S(1)} %get-tuple-element.65), channel_id=1, source_target_pairs={{0,33},{1,34},{2,35},{3,32},{32,65},{33,66},{34,67},{35,64},{64,97... | collective-permute-start | bytes 479240 | tf_op jit(solution)/shard_map/ppermute | solution.py:265
  64.4 2.0 %collective-permute-done.13.refs_5_ = bf16[104,768]{1,0:T(8,128)(2,1)S(1)} collective-permute-done((bf16[104,768]{1,0:T(8,128)(2,1)S(1)}, bf16[104,768]{1,0:T(8,128)(2,1)S(1)}, u32[]{:S(2)}, u32[]{:S(2)}) %collective-permute-start.13) | collective-permute-done | bytes 159776 | tf_op jit(solution)/shard_map/ppermute | solution.py:265
  68.0 4.9 %collective-permute-start.19 = (bf16[104,768]{1,0:T(8,128)(2,1)S(1)}, bf16[104,768]{1,0:T(8,128)(2,1)S(1)}, u32[]{:S(2)}, u32[]{:S(2)}) collective-permute-start(bf16[104,768]{1,0:T(8,128)(2,1)S(1)} %get-tuple-element.67), channel_id=1, source_target_pairs={{0,34},{1,35},{2,32},{3,33},{32,66},{33,67},{34,64},{35,65},{64,98... | collective-permute-start | bytes 479240 | tf_op jit(solution)/shard_map/ppermute | solution.py:265
  73.9 2.7 %shard_map.119 = (bf16[1536,256]{1,0:T(8,128)(2,1)}, bf16[1536,256]{1,0:T(8,128)(2,1)S(1)}, bf16[1536,256]{1,0:T(8,128)(2,1)S(1)}) custom-call(s32[4]{0:T(128)S(1)} %pad_add_fusion.pos, bf16[96,6272]{1,0:T(8,128)(2,1)S(1)} %shard_map.112.refs_0_.here_ref, bf16[96,6272]{1,0:T(8,128)(2,1)S(1)} %get-tuple-element.73.far_ref, ...), custom_call_target="tpu_custom_call" | custom-call | tf_op jit(solution)/shard_map/pallas_call | solution.py:38
  78.4 1.9 %shard_map.116 = bf16[8,16,896]{2,1,0:T(8,128)(2,1)} custom-call(s32[4]{0:T(128)S(1)} %pad_add_fusion.pos, s32[2,128]{1,0:T(2,128)S(1)} %bitcast.18, bf16[104,768]{1,0:T(8,128)(2,1)S(1)} %get-tuple-element.51.refs_0_, bf16[104,768]{1,0:T(8,128)(2,1)S(1)} %collective-permute-done.3.refs_1_, bf16[104,768]{1,0:T(8,128)(2,1)S(1)} %collective-permute-done.4.refs_2_, ...), custom_call_target="tpu_custom_call" | custom-call | tf_op jit(solution)/shard_map/pallas_call | solution.py:38
  80.3 8.6 %all-to-all-start = ((bf16[8,16,896]{2,1,0:T(8,128)(2,1)}), bf16[8,16,896]{2,1,0:T(8,128)(2,1)S(1)}, u32[]{:S(2)}, u32[]{:S(2)}) async-start(bf16[8,16,896]{2,1,0:T(8,128)(2,1)} %shard_map.116), calls=%async_computation | async-start | bytes 458752 | tf_op jit(solution)/shard_map/all_to_all | solution.py:269
  89.4 11.3 %all-to-all-done.got_ref = bf16[8,16,896]{2,1,0:T(8,128)(2,1)S(1)} async-done(((bf16[8,16,896]{2,1,0:T(8,128)(2,1)}), bf16[8,16,896]{2,1,0:T(8,128)(2,1)S(1)}, u32[]{:S(2)}, u32[]{:S(2)}) %all-to-all-start) | async-done | bytes 229408 | tf_op jit(solution)/shard_map/all_to_all | solution.py:269
  102.0 14.2 %all_to_all.10 = bf16[8,16,768]{2,1,0:T(8,128)(2,1)S(1)} all-to-all(bf16[8,16,768]{2,1,0:T(8,128)(2,1)} %get-tuple-element.71), channel_id=1, replica_groups=mesh['dp'=2,'expert'=4,'z'=8,'y'=4] {'z'}, dimensions={0} | all-to-all | bytes 393216 | tf_op jit(solution)/shard_map/all_to_all | solution.py:269
  116.2 2.7 %collective-permute-start.25 = (bf16[128,768]{1,0:T(8,128)(2,1)S(1)}, bf16[128,768]{1,0:T(8,128)(2,1)S(1)}, u32[]{:S(2)}, u32[]{:S(2)}) collective-permute-start(bf16[128,768]{1,0:T(8,128)(2,1)S(1)} %bitcast.12), channel_id=1, source_target_pairs={{0,3},{1,0},{2,1},{3,2},{4,7},{5,4},{6,5},{7,6},{8,11},{9,8},{10,9... | collective-permute-start | bytes 589832 | tf_op jit(solution)/shard_map/ppermute | solution.py:258
  121.4 4.4 %shard_map.120 = (bf16[1536,256]{1,0:T(8,128)(2,1)}, bf16[1536,256]{1,0:T(8,128)(2,1)}, bf16[1536,256]{1,0:T(8,128)(2,1)}) custom-call(s32[4]{0:T(128)S(1)} %pad_add_fusion.pos, bf16[96,6272]{1,0:T(8,128)(2,1)S(1)} %shard_map.112.refs_0_.here_ref, bf16[96,6272]{1,0:T(8,128)(2,1)S(1)} %copy-done.6, bf16[96,6272]{1,0:T(8,128)(2,1)S(1)} %copy-done.1, ...), custom_call_target="tpu_custom_call" | custom-call | tf_op jit(solution)/shard_map/pallas_call | solution.py:38
  (79 shorter events, 27.2 us)
Async XLA Ops:
  3.2 11.8 %collective-permute-start.6 = (bf16[48,3200]{1,0:T(8,128)(2,1)S(1)}, bf16[48,3200]{1,0:T(8,128)(2,1)S(1)}, u32[]{:S(2)}, u32[]{:S(2)}) collective-permute-start(bf16[48,3200]{1,0:T(8,128)(2,1)S(1)} %get-tuple-element.56), channel_id=1, source_target_pairs={{0,64},{32,96},{64,0},{96,32},{1,65},{33,97},{65,1},{97,33},{2,66}... | collective-permute-start | bytes 921608 | tf_op jit(solution)/shard_map/ppermute | solution.py:258
  7.1 32.5 %collective-permute-start.11 = (bf16[96,6272]{1,0:T(8,128)(2,1)S(1)}, bf16[96,6272]{1,0:T(8,128)(2,1)S(1)}, u32[]{:S(2)}, u32[]{:S(2)}) collective-permute-start(bf16[96,6272]{1,0:T(8,128)(2,1)S(1)} %get-tuple-element.59), channel_id=1, source_target_pairs={{0,96},{32,0},{64,32},{96,64},{1,97},{33,1},{65,33},{97,65},{2,98}... | collective-permute-start | bytes 3612680 | tf_op jit(solution)/shard_map/ppermute | solution.py:258
  8.8 10.8 %collective-permute-start.2 = (bf16[1,1536,256]{2,1,0:T(8,128)(2,1)S(1)}, bf16[1,1536,256]{2,1,0:T(8,128)(2,1)S(1)}, u32[]{:S(2)}, u32[]{:S(2)}) collective-permute-start(bf16[1,1536,256]{2,1,0:T(8,128)(2,1)S(1)} %copy-done.4), channel_id=1, source_target_pairs={{0,128},{128,0},{1,129},{129,1},{2,130},{130,2},{3,131},{131,3},{4... | collective-permute-start | bytes 2359304 | tf_op jit(solution)/shard_map/ppermute | solution.py:258
  15.0 29.2 %collective-permute-start.10 = (bf16[96,6272]{1,0:T(8,128)(2,1)S(1)}, bf16[96,6272]{1,0:T(8,128)(2,1)S(1)}, u32[]{:S(2)}, u32[]{:S(2)}) collective-permute-start(bf16[96,6272]{1,0:T(8,128)(2,1)S(1)} %get-tuple-element.46), channel_id=1, source_target_pairs={{0,32},{32,64},{64,96},{96,0},{1,33},{33,65},{65,97},{97,1},{2,34}... | collective-permute-start | bytes 3612680 | tf_op jit(solution)/shard_map/ppermute | solution.py:258
  15.3 11.6 %collective-permute-start.9 = (bf16[48,3200]{1,0:T(8,128)(2,1)S(1)}, bf16[48,3200]{1,0:T(8,128)(2,1)S(1)}, u32[]{:S(2)}, u32[]{:S(2)}) collective-permute-start(bf16[48,3200]{1,0:T(8,128)(2,1)S(1)} %collective-permute-done.6.refs_0_), channel_id=1, source_target_pairs={{0,2},{1,3},{2,0},{3,1},{4,6},{5,7},{6,4},{7,5},{8,10},{9,11},{10,... | collective-permute-start | bytes 921608 | tf_op jit(solution)/shard_map/ppermute | solution.py:258
  18.5 13.2 %collective-permute-start.8 = (bf16[48,3200]{1,0:T(8,128)(2,1)S(1)}, bf16[48,3200]{1,0:T(8,128)(2,1)S(1)}, u32[]{:S(2)}, u32[]{:S(2)}) collective-permute-start(bf16[48,3200]{1,0:T(8,128)(2,1)S(1)} %collective-permute-done.6.refs_0_), channel_id=1, source_target_pairs={{0,3},{1,0},{2,1},{3,2},{4,7},{5,4},{6,5},{7,6},{8,11},{9,8},{10,9... | collective-permute-start | bytes 921608 | tf_op jit(solution)/shard_map/ppermute | solution.py:258
  19.6 14.7 %collective-permute-start.7 = (bf16[48,3200]{1,0:T(8,128)(2,1)S(1)}, bf16[48,3200]{1,0:T(8,128)(2,1)S(1)}, u32[]{:S(2)}, u32[]{:S(2)}) collective-permute-start(bf16[48,3200]{1,0:T(8,128)(2,1)S(1)} %collective-permute-done.6.refs_0_), channel_id=1, source_target_pairs={{0,1},{1,2},{2,3},{3,0},{4,5},{5,6},{6,7},{7,4},{8,9},{9,10},{10,1... | collective-permute-start | bytes 921608 | tf_op jit(solution)/shard_map/ppermute | solution.py:258
  27.0 11.5 %collective-permute-start.3 = (bf16[104,768]{1,0:T(8,128)(2,1)S(1)}, bf16[104,768]{1,0:T(8,128)(2,1)S(1)}, u32[]{:S(2)}, u32[]{:S(2)}) collective-permute-start(bf16[104,768]{1,0:T(8,128)(2,1)S(1)} %get-tuple-element.52), channel_id=1, source_target_pairs={{0,1},{1,2},{2,3},{3,0},{32,33},{33,34},{34,35},{35,32},{64,65},{6... | collective-permute-start | bytes 479240 | tf_op jit(solution)/shard_map/ppermute | solution.py:265
  31.7 20.3 %collective-permute-start.4 = (bf16[104,768]{1,0:T(8,128)(2,1)S(1)}, bf16[104,768]{1,0:T(8,128)(2,1)S(1)}, u32[]{:S(2)}, u32[]{:S(2)}) collective-permute-start(bf16[104,768]{1,0:T(8,128)(2,1)S(1)} %get-tuple-element.53), channel_id=1, source_target_pairs={{0,3},{1,0},{2,1},{3,2},{32,35},{33,32},{34,33},{35,34},{64,67},{6... | collective-permute-start | bytes 479240 | tf_op jit(solution)/shard_map/ppermute | solution.py:265
  34.3 18.2 %collective-permute-start.5 = (bf16[104,768]{1,0:T(8,128)(2,1)S(1)}, bf16[104,768]{1,0:T(8,128)(2,1)S(1)}, u32[]{:S(2)}, u32[]{:S(2)}) collective-permute-start(bf16[104,768]{1,0:T(8,128)(2,1)S(1)} %get-tuple-element.54), channel_id=1, source_target_pairs={{0,2},{1,3},{2,0},{3,1},{32,34},{33,35},{34,32},{35,33},{64,66},{6... | collective-permute-start | bytes 479240 | tf_op jit(solution)/shard_map/ppermute | solution.py:265
  38.4 16.0 %collective-permute-start.21 = (bf16[104,768]{1,0:T(8,128)(2,1)S(1)}, bf16[104,768]{1,0:T(8,128)(2,1)S(1)}, u32[]{:S(2)}, u32[]{:S(2)}) collective-permute-start(bf16[104,768]{1,0:T(8,128)(2,1)S(1)} %get-tuple-element.68), channel_id=1, source_target_pairs={{0,65},{1,66},{2,67},{3,64},{32,97},{33,98},{34,99},{35,96},{64,1}... | collective-permute-start | bytes 479240 | tf_op jit(solution)/shard_map/ppermute | solution.py:265
  39.6 17.0 %collective-permute-start.22 = (bf16[104,768]{1,0:T(8,128)(2,1)S(1)}, bf16[104,768]{1,0:T(8,128)(2,1)S(1)}, u32[]{:S(2)}, u32[]{:S(2)}) collective-permute-start(bf16[104,768]{1,0:T(8,128)(2,1)S(1)} %get-tuple-element.69), channel_id=1, source_target_pairs={{0,67},{1,64},{2,65},{3,66},{32,99},{33,96},{34,97},{35,98},{64,3}... | collective-permute-start | bytes 479240 | tf_op jit(solution)/shard_map/ppermute | solution.py:265
  44.2 14.6 %collective-permute-start.23 = (bf16[104,768]{1,0:T(8,128)(2,1)S(1)}, bf16[104,768]{1,0:T(8,128)(2,1)S(1)}, u32[]{:S(2)}, u32[]{:S(2)}) collective-permute-start(bf16[104,768]{1,0:T(8,128)(2,1)S(1)} %get-tuple-element.70), channel_id=1, source_target_pairs={{0,66},{1,67},{2,64},{3,65},{32,98},{33,99},{34,96},{35,97},{64,2}... | collective-permute-start | bytes 479240 | tf_op jit(solution)/shard_map/ppermute | solution.py:265
  54.4 11.9 %collective-permute-start.13 = (bf16[104,768]{1,0:T(8,128)(2,1)S(1)}, bf16[104,768]{1,0:T(8,128)(2,1)S(1)}, u32[]{:S(2)}, u32[]{:S(2)}) collective-permute-start(bf16[104,768]{1,0:T(8,128)(2,1)S(1)} %get-tuple-element.61), channel_id=1, source_target_pairs={{0,97},{1,98},{2,99},{3,96},{32,1},{33,2},{34,3},{35,0},{64,33},{6... | collective-permute-start | bytes 479240 | tf_op jit(solution)/shard_map/ppermute | solution.py:265
  56.6 11.4 %collective-permute-start.14 = (bf16[104,768]{1,0:T(8,128)(2,1)S(1)}, bf16[104,768]{1,0:T(8,128)(2,1)S(1)}, u32[]{:S(2)}, u32[]{:S(2)}) collective-permute-start(bf16[104,768]{1,0:T(8,128)(2,1)S(1)} %get-tuple-element.62), channel_id=1, source_target_pairs={{0,99},{1,96},{2,97},{3,98},{32,3},{33,0},{34,1},{35,2},{64,35},{6... | collective-permute-start | bytes 479240 | tf_op jit(solution)/shard_map/ppermute | solution.py:265
  58.8 19.6 %collective-permute-start.15 = (bf16[104,768]{1,0:T(8,128)(2,1)S(1)}, bf16[104,768]{1,0:T(8,128)(2,1)S(1)}, u32[]{:S(2)}, u32[]{:S(2)}) collective-permute-start(bf16[104,768]{1,0:T(8,128)(2,1)S(1)} %get-tuple-element.63), channel_id=1, source_target_pairs={{0,98},{1,99},{2,96},{3,97},{32,2},{33,3},{34,0},{35,1},{64,34},{6... | collective-permute-start | bytes 479240 | tf_op jit(solution)/shard_map/ppermute | solution.py:265
  60.4 18.0 %collective-permute-start.16 = (bf16[104,768]{1,0:T(8,128)(2,1)S(1)}, bf16[104,768]{1,0:T(8,128)(2,1)S(1)}, u32[]{:S(2)}, u32[]{:S(2)}) collective-permute-start(bf16[104,768]{1,0:T(8,128)(2,1)S(1)} %get-tuple-element.64), channel_id=1, source_target_pairs={{0,32},{1,33},{2,34},{3,35},{32,64},{33,65},{34,66},{35,67},{64,96... | collective-permute-start | bytes 479240 | tf_op jit(solution)/shard_map/ppermute | solution.py:265
  61.1 17.3 %collective-permute-start.17 = (bf16[104,768]{1,0:T(8,128)(2,1)S(1)}, bf16[104,768]{1,0:T(8,128)(2,1)S(1)}, u32[]{:S(2)}, u32[]{:S(2)}) collective-permute-start(bf16[104,768]{1,0:T(8,128)(2,1)S(1)} %get-tuple-element.65), channel_id=1, source_target_pairs={{0,33},{1,34},{2,35},{3,32},{32,65},{33,66},{34,67},{35,64},{64,97... | collective-permute-start | bytes 479240 | tf_op jit(solution)/shard_map/ppermute | solution.py:265
  66.4 12.0 %collective-permute-start.18 = (bf16[104,768]{1,0:T(8,128)(2,1)S(1)}, bf16[104,768]{1,0:T(8,128)(2,1)S(1)}, u32[]{:S(2)}, u32[]{:S(2)}) collective-permute-start(bf16[104,768]{1,0:T(8,128)(2,1)S(1)} %get-tuple-element.66), channel_id=1, source_target_pairs={{0,35},{1,32},{2,33},{3,34},{32,67},{33,64},{34,65},{35,66},{64,99... | collective-permute-start | bytes 479240 | tf_op jit(solution)/shard_map/ppermute | solution.py:265
  68.0 10.4 %collective-permute-start.19 = (bf16[104,768]{1,0:T(8,128)(2,1)S(1)}, bf16[104,768]{1,0:T(8,128)(2,1)S(1)}, u32[]{:S(2)}, u32[]{:S(2)}) collective-permute-start(bf16[104,768]{1,0:T(8,128)(2,1)S(1)} %get-tuple-element.67), channel_id=1, source_target_pairs={{0,34},{1,35},{2,32},{3,33},{32,66},{33,67},{34,64},{35,65},{64,98... | collective-permute-start | bytes 479240 | tf_op jit(solution)/shard_map/ppermute | solution.py:265
  78.4 40.5 %collective-permute-start.27 = (bf16[1536,256]{1,0:T(8,128)(2,1)}, bf16[1536,256]{1,0:T(8,128)(2,1)}, u32[]{:S(2)}, u32[]{:S(2)}) collective-permute-start(bf16[1536,256]{1,0:T(8,128)(2,1)} %get-tuple-element.77), channel_id=1, source_target_pairs={{0,128},{128,0},{1,129},{129,1},{2,130},{130,2},{3,131},{131,3},{4... | collective-permute-start | bytes 2359304 | tf_op jit(solution)/shard_map/ppermute | solution.py:258
  80.3 20.4 %all-to-all-start = ((bf16[8,16,896]{2,1,0:T(8,128)(2,1)}), bf16[8,16,896]{2,1,0:T(8,128)(2,1)S(1)}, u32[]{:S(2)}, u32[]{:S(2)}) async-start(bf16[8,16,896]{2,1,0:T(8,128)(2,1)} %shard_map.116), calls=%async_computation | async-start | bytes 458752 | tf_op jit(solution)/shard_map/all_to_all | solution.py:269
  88.9 30.0 %collective-permute-start.28 = (bf16[1536,256]{1,0:T(8,128)(2,1)}, bf16[1536,256]{1,0:T(8,128)(2,1)}, u32[]{:S(2)}, u32[]{:S(2)}) collective-permute-start(bf16[1536,256]{1,0:T(8,128)(2,1)} %copy-done.13), channel_id=1, source_target_pairs={{0,128},{128,0},{1,129},{129,1},{2,130},{130,2},{3,131},{131,3},{4... | collective-permute-start | bytes 2359304 | tf_op jit(solution)/shard_map/ppermute | solution.py:258
  89.1 29.8 %collective-permute-start.29 = (bf16[1536,256]{1,0:T(8,128)(2,1)}, bf16[1536,256]{1,0:T(8,128)(2,1)}, u32[]{:S(2)}, u32[]{:S(2)}) collective-permute-start(bf16[1536,256]{1,0:T(8,128)(2,1)} %copy-done.12), channel_id=1, source_target_pairs={{0,128},{128,0},{1,129},{129,1},{2,130},{130,2},{3,131},{131,3},{4... | collective-permute-start | bytes 2359304 | tf_op jit(solution)/shard_map/ppermute | solution.py:258
  (21 other events, 246.4 us)

commit v2 on v1

--- a/solution.py
+++ b/solution.py
@@ -113,13 +113,12 @@
     count = {"here": 1, "far": 4, "sides": 2}[kind]
     pieces, refs = refs[:count], refs[count:]
     wg_own, wg_sib, wu_own, wu_sib, wd_own, wd_sib = (ref.at[0] for ref in refs[:6])
-    ends = 14 if kind == "sides" else 10
-    sends, aux_ref, whole = refs[6:ends], refs[ends], refs[-1]
+    sends, aux_ref, whole = refs[6:10], refs[10], refs[-1]
     half, units = wg_own.shape
     width = 2 * half
     block = half // 2
     if kind == "far":
-        msgs = [refs[ends + 1]]
+        msgs = [refs[11]]
         rows = pieces[0].shape[0]
         for piece, shift in zip(pieces, (0, 1, -1, 2)):
             source = lax.rem(pos[3] - shift + 4, 4)
@@ -163,19 +162,29 @@
         part = lax.dot_general(dpg, wg[at : at + block, :], NT, preferred_element_type=F32)
         part += lax.dot_general(dpu, wu[at : at + block, :], NT, preferred_element_type=F32)
         whole[j] = part.astype(BF)
-    slots = sends[0].shape[0] - 8
-    for c in range(len(sends) // 4):
+    count = len(msgs)
+    long = sends[0].shape[0] // count
+    slots = long - 8
+    for c in range(count):
         at = slice(c * slots, (c + 1) * slots)
+        first = c * long
         padded = jnp.concatenate([share[at], jnp.zeros((LANES - slots, units), F32)], axis=0)
         line = lax.dot_general(
             jnp.ones((8, units), F32), padded, NT,
             precision=lax.Precision.HIGHEST, preferred_element_type=F32,
         ).astype(BF)
-        for j in range(4):
-            send = sends[4 * c + j]
-            send[:slots] = whole[lax.rem(pos[3] + j, 4), at, :]
-            send[slots:, :LANES] = line
-            send[slots:, LANES:] = jnp.zeros((8, block - LANES), BF)
+        for j, send in enumerate(sends):
+            send[first : first + slots] = whole[lax.rem(pos[3] + j, 4), at, :]
+            send[first + slots : first + long, :LANES] = line
+            send[first + slots : first + long, LANES:] = jnp.zeros((8, block - LANES), BF)
+
+
+def sum_kernel(pos, a_ref, b_ref, c_ref, d_ref, *outs):
+    long = outs[0].shape[0]
+    for i, out in enumerate(outs):
+        at = slice(i * long, (i + 1) * long)
+        total = a_ref[at].astype(F32) + b_ref[at].astype(F32)
+        out[...] = (total + (c_ref[at].astype(F32) + d_ref[at].astype(F32))).astype(BF)
 
 
 def combine_kernel(pos, ids_ref, *refs):
@@ -188,11 +197,7 @@
     result = jnp.zeros((tokens, width), F32)
     gates = []
     for k in range(4):
-        group = refs[4 * k : 4 * k + 4]
-        total = group[0][...].astype(F32)
-        for ref in group[1:]:
-            total += ref[...].astype(F32)
-        total = total.astype(BF)
+        total = refs[k][...]
         pick = picks(rank, member, k, slots, 0)
         result += lax.dot_general(pick, total[:slots], TN, preferred_element_type=F32)
         pick = picks(rank, member, k, LANES, 0)
@@ -258,13 +263,6 @@
     return lax.ppermute(value, axis, [(i, (i + offset) % size) for i in range(size)])
 
 
-def shift_two(value, offset, column):
-    pairs = [
-        (4 * i + j, 4 * ((i + offset) % 4) + (j + column) % 4) for i in range(4) for j in range(4)
-    ]
-    return lax.ppermute(value, ("expert", "y"), pairs)
-
-
 def exchange(value, axis):
     return lax.all_to_all(value, axis, split_axis=0, concat_axis=0, tiled=True)
 
@@ -317,21 +315,30 @@
         count = 2 if kind == "sides" else 1
         return call(
             functools.partial(expert_kernel, kind),
-            [array(slots + 8, block)] * (4 * count)
+            [array(count * (slots + 8), block)] * 4
             + [plain(count * slots, 3 * units)]
             + [array(slots, long)] * (kind == "far"),
             (pos, *msgs, *weights),
             scratch=[pltpu.VMEM((4, count * slots, block), BF)],
         )
 
-    def back(sends, offset):
-        kept = [sends[0]] if offset == 0 else [shift_two(sends[0], -offset, 0)]
-        return kept + [shift_two(sends[j], -offset, j) for j in (1, 3, 2)]
+    def scatter(sends, name):
+        got = [sends[0]] + [shift(sends[j], "y", j) for j in (1, 3, 2)]
+        count = 2 if name == "sides" else 1
+        return call(sum_kernel, [array(slots + 8, block)] * count, (pos, *got))
 
     local = expert(pos, [here], "here")
     remote = expert(after(pos, local[0]), far, "far")
     sides = expert(after(pos, remote[0]), [plus, minus], "sides")
-    groups = [*back(local[:4], 0), *back(sides[:4], 1), *back(sides[4:8], -1), *back(remote[:4], 2)]
+    (from_here,) = scatter(local[:4], "here")
+    (from_far,) = scatter(remote[:4], "far")
+    from_plus, from_minus = scatter(sides[:4], "sides")
+    groups = [
+        from_here,
+        shift(from_plus, "expert", -1),
+        shift(from_minus, "expert", 1),
+        shift(from_far, "expert", 2),
+    ]
     (mine,) = call(combine_kernel, [plain(zs, rows, block + LANES)], (pos, expert_ids.T, *groups))
     mine, gate_grad = call(
         gather_kernel,
@@ -344,7 +351,7 @@
         [plain(tok_count, width)],
         (pos, slab, *[shift(slab, "y", offset) for offset in (1, -1, 2)]),
     )
-    used = [here, remote[5], plus, minus, local[4], remote[4], sides[8]]
+    used = [here, remote[5], plus, minus, local[4], remote[4], sides[4]]
     half = width // 2
     away = call(
         functools.partial(grad_kernel, True), [array(half, units)] * 3, (pos, *used),

time: 129 us -> 133 us (1.031)
  the two profiles are of different devices: /device:TPU:2 before, /device:TPU:8 now
where the time goes in v2:
time: 133 us; the launch traced here: 130 us
  waiting for transfers between devices  42.5 us (32%)
  starting transfers between devices  41.5 us (31%)
  Pallas kernels  29.8 us (22%)
  blocking collectives  13.1 us (10%)
  local copies, waits for them, and re-layouts  2.59 us (2%)
    ppermute x27, starting transfers between devices, shift(): lax.ppermute(value, axis, [(i, (i + offset) % size) for i in range(size)])  33 us
    ppermute x27, waiting for transfers between devices, shift(): lax.ppermute(value, axis, [(i, (i + offset) % size) for i in range(size)])  32.9 us
    pallas_call x14, Pallas kernels, call(): pl.pallas_call(kernel, out_shape=outs, in_specs=specs, out_specs=[spec] *...  29.8 us
    all_to_all x1, blocking collectives, exchange(): return lax.all_to_all(value, axis, split_axis=0, concat_axis=0, tiled=True)  13.1 us
    all_to_all x1, waiting for transfers between devices, exchange(): return lax.all_to_all(value, axis, split_axis=0, concat_axis=0, tiled=True)  9.62 us
    all_to_all x1, starting transfers between devices, exchange(): return lax.all_to_all(value, axis, split_axis=0, concat_axis=0, tiled=True)  8.46 us
  transfers between devices with their start and end apart: 28, of which 9 were waited for; matrix products, arithmetic and copies ran while one was open for 0% of the time, Pallas kernels for 20%

profile of v2, /device:TPU:8, one launch (start us, length us, event | category | flops | bytes accessed | tf_op | source)
XLA Modules:
  0.0 130.3 jit_solution(17155320111565391994)
XLA Ops:
  0.7 2.5 %shard_map.110 = (bf16[48,3200]{1,0:T(8,128)(2,1)S(1)}, bf16[128,3072]{1,0:T(8,128)(2,1)S(1)}, bf16[128,3072]{1,0:T(8,128)(2,1)S(1)}) custom-call(s32[4]{0:T(128)S(1)} %pad_add_fusion.pos, s32[2,128]{1,0:T(2,128)} %bitcast.15, bf16[2,128]{1,0:T(2,128)(2,1)} %bitcast.20, bf16[128,3072]{1,0:T(8,128)(2,1)} %tok_ref.1, bf16[128,3072]{1,0:T(8,128)(2,1)} %cot_ref.1), custom_call_target="tpu_custom_call" | custom-call | tf_op jit(solution)/shard_map/pallas_call | solution.py:38
  3.2 3.1 %collective-permute-start.6 = (bf16[48,3200]{1,0:T(8,128)(2,1)S(1)}, bf16[48,3200]{1,0:T(8,128)(2,1)S(1)}, u32[]{:S(2)}, u32[]{:S(2)}) collective-permute-start(bf16[48,3200]{1,0:T(8,128)(2,1)S(1)} %get-tuple-element.54), channel_id=1, source_target_pairs={{0,64},{32,96},{64,0},{96,32},{1,65},{33,97},{65,1},{97,33},{2,66}... | collective-permute-start | bytes 921608 | tf_op jit(solution)/shard_map/ppermute | solution.py:263
  6.3 1.6 %shard_map.111 = (bf16[96,6272]{1,0:T(8,128)(2,1)S(1)}, bf16[96,6272]{1,0:T(8,128)(2,1)S(1)}) custom-call(s32[4]{0:T(128)S(1)} %pad_add_fusion.pos, s32[2,128]{1,0:T(2,128)} %bitcast.16, bf16[2,128]{1,0:T(2,128)(2,1)} %bitcast.21, bf16[128,3072]{1,0:T(8,128)(2,1)S(1)} %get-tuple-element.42.tok_ref, bf16[128,3072]{1,0:T(8,128)(2,1)S(1)} %get-tuple-element.43.cot_ref), custom_call_target="tpu_custom_call" | custom-call | tf_op jit(solution)/shard_map/pallas_call | solution.py:38
  10.5 4.4 %collective-permute-done.6.refs_0_ = bf16[48,3200]{1,0:T(8,128)(2,1)S(1)} collective-permute-done((bf16[48,3200]{1,0:T(8,128)(2,1)S(1)}, bf16[48,3200]{1,0:T(8,128)(2,1)S(1)}, u32[]{:S(2)}, u32[]{:S(2)}) %collective-permute-start.6) | collective-permute-done | bytes 307232 | tf_op jit(solution)/shard_map/ppermute | solution.py:263
  15.0 2.4 %collective-permute-start.9 = (bf16[48,3200]{1,0:T(8,128)(2,1)S(1)}, bf16[48,3200]{1,0:T(8,128)(2,1)S(1)}, u32[]{:S(2)}, u32[]{:S(2)}) collective-permute-start(bf16[48,3200]{1,0:T(8,128)(2,1)S(1)} %collective-permute-done.6.refs_0_), channel_id=1, source_target_pairs={{0,2},{1,3},{2,0},{3,1},{4,6},{5,7},{6,4},{7,5},{8,10},{9,11},{10,... | collective-permute-start | bytes 921608 | tf_op jit(solution)/shard_map/ppermute | solution.py:263
  20.7 3.5 %shard_map.113 = (bf16[104,768]{1,0:T(8,128)(2,1)S(1)}, bf16[104,768]{1,0:T(8,128)(2,1)S(1)}, bf16[104,768]{1,0:T(8,128)(2,1)S(1)}, bf16[104,768]{1,0:T(8,128)(2,1)S(1)}, bf16[96,768]{1,0:T(8,128)(2,1)}) custom-call(s32[4]{0:T(128)S(1)} %pad_add_fusion.pos, bf16[96,6272]{1,0:T(8,128)(2,1)S(1)} %shard_map.112.refs_0_.here_ref, ...), custom_call_target="tpu_custom_call" | custom-call | tf_op jit(solution)/shard_map/pallas_call | solution.py:38
  24.1 2.6 %collective-permute-done.9.refs_3_ = bf16[48,3200]{1,0:T(8,128)(2,1)S(1)} collective-permute-done((bf16[48,3200]{1,0:T(8,128)(2,1)S(1)}, bf16[48,3200]{1,0:T(8,128)(2,1)S(1)}, u32[]{:S(2)}, u32[]{:S(2)}) %collective-permute-start.9) | collective-permute-done | bytes 307232 | tf_op jit(solution)/shard_map/ppermute | solution.py:263
  26.7 6.0 %collective-permute-done.8.refs_2_ = bf16[48,3200]{1,0:T(8,128)(2,1)S(1)} collective-permute-done((bf16[48,3200]{1,0:T(8,128)(2,1)S(1)}, bf16[48,3200]{1,0:T(8,128)(2,1)S(1)}, u32[]{:S(2)}, u32[]{:S(2)}) %collective-permute-start.8) | collective-permute-done | bytes 307232 | tf_op jit(solution)/shard_map/ppermute | solution.py:263
  32.9 3.5 %shard_map.115 = (bf16[104,768]{1,0:T(8,128)(2,1)S(1)}, bf16[104,768]{1,0:T(8,128)(2,1)S(1)}, bf16[104,768]{1,0:T(8,128)(2,1)S(1)}, bf16[104,768]{1,0:T(8,128)(2...) custom-call(s32[4]{0:T(128)S(1)} %pad_add_fusion.pos, ...), custom_call_target="tpu_custom_call" | custom-call | tf_op jit(solution)/shard_map/pallas_call | solution.py:38
  37.8 1.9 %collective-permute-done.11.refs_1_.minus_ref = bf16[96,6272]{1,0:T(8,128)(2,1)S(1)} collective-permute-done((bf16[96,6272]{1,0:T(8,128)(2,1)S(1)}, bf16[96,6272]{1,0:T(8,128)(2,1)S(1)}, u32[]{:S(2)}, u32[]{:S(2)}) %collective-permute-start.11) | collective-permute-done | bytes 1204256 | tf_op jit(solution)/shard_map/ppermute | solution.py:263
  39.8 3.9 %shard_map.116 = (bf16[208,768]{1,0:T(8,128)(2,1)S(1)}, bf16[208,768]{1,0:T(8,128)(2,1)S(1)}, bf16[208,768]{1,0:T(8,128)(2,1)S(1)}, bf16[208,768]{1,0:T(8,128)(2,1)S(1)}, bf16[192,768]{1,0:T(8,128)(2,1)}) custom-call(s32[4]{0:T(128)S(1)} %pad_add_fusion.pos, bf16[96,6272]{1,0:T(8,128)(2,1)S(1)} %collective-permute-done.10.refs_0_.plus_ref, ...), custom_call_target="tpu_custom_call" | custom-call | tf_op jit(solution)/shard_map/pallas_call | solution.py:38
  45.7 2.3 %collective-permute-start.14 = (bf16[208,768]{1,0:T(8,128)(2,1)S(1)}, bf16[208,768]{1,0:T(8,128)(2,1)S(1)}, u32[]{:S(2)}, u32[]{:S(2)}) collective-permute-start(bf16[208,768]{1,0:T(8,128)(2,1)S(1)} %get-tuple-element.61), channel_id=1, source_target_pairs={{0,2},{1,3},{2,0},{3,1},{4,6},{5,7},{6,4},{7,5},{8,10},{9,11},{10,... | collective-permute-start | bytes 958472 | tf_op jit(solution)/shard_map/ppermute | solution.py:263
  50.6 14.5 %collective-permute-done.18.c_ref = bf16[104,768]{1,0:T(8,128)(2,1)S(1)} collective-permute-done((bf16[104,768]{1,0:T(8,128)(2,1)S(1)}, bf16[104,768]{1,0:T(8,128)(2,1)S(1)}, u32[]{:S(2)}, u32[]{:S(2)}) %collective-permute-start.18) | collective-permute-done | bytes 159776 | tf_op jit(solution)/shard_map/ppermute | solution.py:263
  65.1 1.9 %collective-permute-start.3 = (bf16[104,768]{1,0:T(8,128)(2,1)S(1)}, bf16[104,768]{1,0:T(8,128)(2,1)S(1)}, u32[]{:S(2)}, u32[]{:S(2)}) collective-permute-start(bf16[104,768]{1,0:T(8,128)(2,1)S(1)} %get-tuple-element.50), channel_id=1, source_target_pairs={{0,1},{1,2},{2,3},{3,0},{4,5},{5,6},{6,7},{7,4},{8,9},{9,10},{10,1... | collective-permute-start | bytes 479240 | tf_op jit(solution)/shard_map/ppermute | solution.py:263
  68.9 3.7 %collective-permute-start.5 = (bf16[104,768]{1,0:T(8,128)(2,1)S(1)}, bf16[104,768]{1,0:T(8,128)(2,1)S(1)}, u32[]{:S(2)}, u32[]{:S(2)}) collective-permute-start(bf16[104,768]{1,0:T(8,128)(2,1)S(1)} %get-tuple-element.52), channel_id=1, source_target_pairs={{0,2},{1,3},{2,0},{3,1},{4,6},{5,7},{6,4},{7,5},{8,10},{9,11},{10,... | collective-permute-start | bytes 479240 | tf_op jit(solution)/shard_map/ppermute | solution.py:263
  72.6 3.4 %collective-permute-start.20 = (bf16[104,768]{1,0:T(8,128)(2,1)S(1)}, bf16[104,768]{1,0:T(8,128)(2,1)S(1)}, u32[]{:S(2)}, u32[]{:S(2)}) collective-permute-start(bf16[104,768]{1,0:T(8,128)(2,1)S(1)} %shard_map.118), channel_id=1, source_target_pairs={{0,64},{32,96},{64,0},{96,32},{1,65},{33,97},{65,1},{97,33},{2,66}... | collective-permute-start | bytes 479240 | tf_op jit(solution)/shard_map/ppermute | solution.py:263
  78.9 2.7 %shard_map.122 = (bf16[1536,256]{1,0:T(8,128)(2,1)}, bf16[1536,256]{1,0:T(8,128)(2,1)S(1)}, bf16[1536,256]{1,0:T(8,128)(2,1)S(1)}) custom-call(s32[4]{0:T(128)S(1)} %pad_add_fusion.pos, bf16[96,6272]{1,0:T(8,128)(2,1)S(1)} %shard_map.112.refs_0_.here_ref, bf16[96,6272]{1,0:T(8,128)(2,1)S(1)} %get-tuple-element.69.far_ref, ...), custom_call_target="tpu_custom_call" | custom-call | tf_op jit(solution)/shard_map/pallas_call | solution.py:38
  82.4 2.1 %collective-permute-done.16.refs_2_ = bf16[104,768]{1,0:T(8,128)(2,1)S(1)} collective-permute-done((bf16[104,768]{1,0:T(8,128)(2,1)S(1)}, bf16[104,768]{1,0:T(8,128)(2,1)S(1)}, u32[]{:S(2)}, u32[]{:S(2)}) %collective-permute-start.16) | collective-permute-done | bytes 159776 | tf_op jit(solution)/shard_map/ppermute | solution.py:263
  84.5 1.8 %shard_map.119 = bf16[8,16,896]{2,1,0:T(8,128)(2,1)} custom-call(s32[4]{0:T(128)S(1)} %pad_add_fusion.pos, s32[2,128]{1,0:T(2,128)S(1)} %bitcast.18, bf16[104,768]{1,0:T(8,128)(2,1)S(1)} %shard_map.114.refs_0_, bf16[104,768]{1,0:T(8,128)(2,1)S(1)} %collective-permute-done.15.refs_1_, bf16[104,768]{1,0:T(8,128)(2,1)S(1)} %collective-permute-done.16.refs_2_, ...), custom_call_target="tpu_custom_call" | custom-call | tf_op jit(solution)/shard_map/pallas_call | solution.py:38
  86.3 8.5 %all-to-all-start = ((bf16[8,16,896]{2,1,0:T(8,128)(2,1)}), bf16[8,16,896]{2,1,0:T(8,128)(2,1)S(1)}, u32[]{:S(2)}, u32[]{:S(2)}) async-start(bf16[8,16,896]{2,1,0:T(8,128)(2,1)} %shard_map.119), calls=%async_computation | async-start | bytes 458752 | tf_op jit(solution)/shard_map/all_to_all | solution.py:267
  95.2 9.6 %all-to-all-done.got_ref = bf16[8,16,896]{2,1,0:T(8,128)(2,1)S(1)} async-done(((bf16[8,16,896]{2,1,0:T(8,128)(2,1)}), bf16[8,16,896]{2,1,0:T(8,128)(2,1)S(1)}, u32[]{:S(2)}, u32[]{:S(2)}) %all-to-all-start) | async-done | bytes 229408 | tf_op jit(solution)/shard_map/all_to_all | solution.py:267
  106.1 13.1 %all_to_all.10 = bf16[8,16,768]{2,1,0:T(8,128)(2,1)S(1)} all-to-all(bf16[8,16,768]{2,1,0:T(8,128)(2,1)} %get-tuple-element.67), channel_id=1, replica_groups=mesh['dp'=2,'expert'=4,'z'=8,'y'=4] {'z'}, dimensions={0} | all-to-all | bytes 393216 | tf_op jit(solution)/shard_map/all_to_all | solution.py:267
  119.3 2.6 %collective-permute-start.22 = (bf16[128,768]{1,0:T(8,128)(2,1)S(1)}, bf16[128,768]{1,0:T(8,128)(2,1)S(1)}, u32[]{:S(2)}, u32[]{:S(2)}) collective-permute-start(bf16[128,768]{1,0:T(8,128)(2,1)S(1)} %bitcast.12), channel_id=1, source_target_pairs={{0,3},{1,0},{2,1},{3,2},{4,7},{5,4},{6,5},{7,6},{8,11},{9,8},{10,9... | collective-permute-start | bytes 589832 | tf_op jit(solution)/shard_map/ppermute | solution.py:263
  124.5 4.3 %shard_map.123 = (bf16[1536,256]{1,0:T(8,128)(2,1)}, bf16[1536,256]{1,0:T(8,128)(2,1)}, bf16[1536,256]{1,0:T(8,128)(2,1)}) custom-call(s32[4]{0:T(128)S(1)} %pad_add_fusion.pos, bf16[96,6272]{1,0:T(8,128)(2,1)S(1)} %shard_map.112.refs_0_.here_ref, bf16[96,6272]{1,0:T(8,128)(2,1)S(1)} %copy-done.6, bf16[96,6272]{1,0:T(8,128)(2,1)S(1)} %copy-done.1, ...), custom_call_target="tpu_custom_call" | custom-call | tf_op jit(solution)/shard_map/pallas_call | solution.py:38
  (74 shorter events, 23.5 us)
Async XLA Ops:
  3.2 11.7 %collective-permute-start.6 = (bf16[48,3200]{1,0:T(8,128)(2,1)S(1)}, bf16[48,3200]{1,0:T(8,128)(2,1)S(1)}, u32[]{:S(2)}, u32[]{:S(2)}) collective-permute-start(bf16[48,3200]{1,0:T(8,128)(2,1)S(1)} %get-tuple-element.54), channel_id=1, source_target_pairs={{0,64},{32,96},{64,0},{96,32},{1,65},{33,97},{65,1},{97,33},{2,66}... | collective-permute-start | bytes 921608 | tf_op jit(solution)/shard_map/ppermute | solution.py:263
  7.9 31.8 %collective-permute-start.11 = (bf16[96,6272]{1,0:T(8,128)(2,1)S(1)}, bf16[96,6272]{1,0:T(8,128)(2,1)S(1)}, u32[]{:S(2)}, u32[]{:S(2)}) collective-permute-start(bf16[96,6272]{1,0:T(8,128)(2,1)S(1)} %get-tuple-element.57), channel_id=1, source_target_pairs={{0,96},{32,0},{64,32},{96,64},{1,97},{33,1},{65,33},{97,65},{2,98}... | collective-permute-start | bytes 3612680 | tf_op jit(solution)/shard_map/ppermute | solution.py:263
  9.1 30.6 %collective-permute-start.10 = (bf16[96,6272]{1,0:T(8,128)(2,1)S(1)}, bf16[96,6272]{1,0:T(8,128)(2,1)S(1)}, u32[]{:S(2)}, u32[]{:S(2)}) collective-permute-start(bf16[96,6272]{1,0:T(8,128)(2,1)S(1)} %get-tuple-element.44), channel_id=1, source_target_pairs={{0,32},{32,64},{64,96},{96,0},{1,33},{33,65},{65,97},{97,1},{2,34}... | collective-permute-start | bytes 3612680 | tf_op jit(solution)/shard_map/ppermute | solution.py:263
  10.0 7.3 %collective-permute-start.1 = (bf16[1,1536,256]{2,1,0:T(8,128)(2,1)S(1)}, bf16[1,1536,256]{2,1,0:T(8,128)(2,1)S(1)}, u32[]{:S(2)}, u32[]{:S(2)}) collective-permute-start(bf16[1,1536,256]{2,1,0:T(8,128)(2,1)S(1)} %copy-done.3), channel_id=1, source_target_pairs={{0,128},{128,0},{1,129},{129,1},{2,130},{130,2},{3,131},{131,3},{4... | collective-permute-start | bytes 2359304 | tf_op jit(solution)/shard_map/ppermute | solution.py:263
  15.0 11.8 %collective-permute-start.9 = (bf16[48,3200]{1,0:T(8,128)(2,1)S(1)}, bf16[48,3200]{1,0:T(8,128)(2,1)S(1)}, u32[]{:S(2)}, u32[]{:S(2)}) collective-permute-start(bf16[48,3200]{1,0:T(8,128)(2,1)S(1)} %collective-permute-done.6.refs_0_), channel_id=1, source_target_pairs={{0,2},{1,3},{2,0},{3,1},{4,6},{5,7},{6,4},{7,5},{8,10},{9,11},{10,... | collective-permute-start | bytes 921608 | tf_op jit(solution)/shard_map/ppermute | solution.py:263
  17.3 15.4 %collective-permute-start.8 = (bf16[48,3200]{1,0:T(8,128)(2,1)S(1)}, bf16[48,3200]{1,0:T(8,128)(2,1)S(1)}, u32[]{:S(2)}, u32[]{:S(2)}) collective-permute-start(bf16[48,3200]{1,0:T(8,128)(2,1)S(1)} %collective-permute-done.6.refs_0_), channel_id=1, source_target_pairs={{0,3},{1,0},{2,1},{3,2},{4,7},{5,4},{6,5},{7,6},{8,11},{9,8},{10,9... | collective-permute-start | bytes 921608 | tf_op jit(solution)/shard_map/ppermute | solution.py:263
  18.7 14.2 %collective-permute-start.7 = (bf16[48,3200]{1,0:T(8,128)(2,1)S(1)}, bf16[48,3200]{1,0:T(8,128)(2,1)S(1)}, u32[]{:S(2)}, u32[]{:S(2)}) collective-permute-start(bf16[48,3200]{1,0:T(8,128)(2,1)S(1)} %collective-permute-done.6.refs_0_), channel_id=1, source_target_pairs={{0,1},{1,2},{2,3},{3,0},{4,5},{5,6},{6,7},{7,4},{8,9},{9,10},{10,1... | collective-permute-start | bytes 921608 | tf_op jit(solution)/shard_map/ppermute | solution.py:263
  36.4 12.9 %collective-permute-start.17 = (bf16[104,768]{1,0:T(8,128)(2,1)S(1)}, bf16[104,768]{1,0:T(8,128)(2,1)S(1)}, u32[]{:S(2)}, u32[]{:S(2)}) collective-permute-start(bf16[104,768]{1,0:T(8,128)(2,1)S(1)} %get-tuple-element.64), channel_id=1, source_target_pairs={{0,1},{1,2},{2,3},{3,0},{4,5},{5,6},{6,7},{7,4},{8,9},{9,10},{10,1... | collective-permute-start | bytes 479240 | tf_op jit(solution)/shard_map/ppermute | solution.py:263
  43.7 25.2 %collective-permute-start.12 = (bf16[208,768]{1,0:T(8,128)(2,1)S(1)}, bf16[208,768]{1,0:T(8,128)(2,1)S(1)}, u32[]{:S(2)}, u32[]{:S(2)}) collective-permute-start(bf16[208,768]{1,0:T(8,128)(2,1)S(1)} %get-tuple-element.59), channel_id=1, source_target_pairs={{0,1},{1,2},{2,3},{3,0},{4,5},{5,6},{6,7},{7,4},{8,9},{9,10},{10,1... | collective-permute-start | bytes 958472 | tf_op jit(solution)/shard_map/ppermute | solution.py:263
  45.2 27.4 %collective-permute-start.13 = (bf16[208,768]{1,0:T(8,128)(2,1)S(1)}, bf16[208,768]{1,0:T(8,128)(2,1)S(1)}, u32[]{:S(2)}, u32[]{:S(2)}) collective-permute-start(bf16[208,768]{1,0:T(8,128)(2,1)S(1)} %get-tuple-element.60), channel_id=1, source_target_pairs={{0,3},{1,0},{2,1},{3,2},{4,7},{5,4},{6,5},{7,6},{8,11},{9,8},{10,9... | collective-permute-start | bytes 958472 | tf_op jit(solution)/shard_map/ppermute | solution.py:263
  45.7 30.4 %collective-permute-start.14 = (bf16[208,768]{1,0:T(8,128)(2,1)S(1)}, bf16[208,768]{1,0:T(8,128)(2,1)S(1)}, u32[]{:S(2)}, u32[]{:S(2)}) collective-permute-start(bf16[208,768]{1,0:T(8,128)(2,1)S(1)} %get-tuple-element.61), channel_id=1, source_target_pairs={{0,2},{1,3},{2,0},{3,1},{4,6},{5,7},{6,4},{7,5},{8,10},{9,11},{10,... | collective-permute-start | bytes 958472 | tf_op jit(solution)/shard_map/ppermute | solution.py:263
  48.0 17.2 %collective-permute-start.18 = (bf16[104,768]{1,0:T(8,128)(2,1)S(1)}, bf16[104,768]{1,0:T(8,128)(2,1)S(1)}, u32[]{:S(2)}, u32[]{:S(2)}) collective-permute-start(bf16[104,768]{1,0:T(8,128)(2,1)S(1)} %get-tuple-element.65), channel_id=1, source_target_pairs={{0,3},{1,0},{2,1},{3,2},{4,7},{5,4},{6,5},{7,6},{8,11},{9,8},{10,9... | collective-permute-start | bytes 479240 | tf_op jit(solution)/shard_map/ppermute | solution.py:263
  49.3 18.9 %collective-permute-start.19 = (bf16[104,768]{1,0:T(8,128)(2,1)S(1)}, bf16[104,768]{1,0:T(8,128)(2,1)S(1)}, u32[]{:S(2)}, u32[]{:S(2)}) collective-permute-start(bf16[104,768]{1,0:T(8,128)(2,1)S(1)} %get-tuple-element.66), channel_id=1, source_target_pairs={{0,2},{1,3},{2,0},{3,1},{4,6},{5,7},{6,4},{7,5},{8,10},{9,11},{10,... | collective-permute-start | bytes 479240 | tf_op jit(solution)/shard_map/ppermute | solution.py:263
  65.1 12.8 %collective-permute-start.3 = (bf16[104,768]{1,0:T(8,128)(2,1)S(1)}, bf16[104,768]{1,0:T(8,128)(2,1)S(1)}, u32[]{:S(2)}, u32[]{:S(2)}) collective-permute-start(bf16[104,768]{1,0:T(8,128)(2,1)S(1)} %get-tuple-element.50), channel_id=1, source_target_pairs={{0,1},{1,2},{2,3},{3,0},{4,5},{5,6},{6,7},{7,4},{8,9},{9,10},{10,1... | collective-permute-start | bytes 479240 | tf_op jit(solution)/shard_map/ppermute | solution.py:263
  68.2 13.4 %collective-permute-start.4 = (bf16[104,768]{1,0:T(8,128)(2,1)S(1)}, bf16[104,768]{1,0:T(8,128)(2,1)S(1)}, u32[]{:S(2)}, u32[]{:S(2)}) collective-permute-start(bf16[104,768]{1,0:T(8,128)(2,1)S(1)} %get-tuple-element.51), channel_id=1, source_target_pairs={{0,3},{1,0},{2,1},{3,2},{4,7},{5,4},{6,5},{7,6},{8,11},{9,8},{10,9... | collective-permute-start | bytes 479240 | tf_op jit(solution)/shard_map/ppermute | solution.py:263
  68.9 12.9 %collective-permute-start.5 = (bf16[104,768]{1,0:T(8,128)(2,1)S(1)}, bf16[104,768]{1,0:T(8,128)(2,1)S(1)}, u32[]{:S(2)}, u32[]{:S(2)}) collective-permute-start(bf16[104,768]{1,0:T(8,128)(2,1)S(1)} %get-tuple-element.52), channel_id=1, source_target_pairs={{0,2},{1,3},{2,0},{3,1},{4,6},{5,7},{6,4},{7,5},{8,10},{9,11},{10,... | collective-permute-start | bytes 479240 | tf_op jit(solution)/shard_map/ppermute | solution.py:263
  72.6 9.8 %collective-permute-start.20 = (bf16[104,768]{1,0:T(8,128)(2,1)S(1)}, bf16[104,768]{1,0:T(8,128)(2,1)S(1)}, u32[]{:S(2)}, u32[]{:S(2)}) collective-permute-start(bf16[104,768]{1,0:T(8,128)(2,1)S(1)} %shard_map.118), channel_id=1, source_target_pairs={{0,64},{32,96},{64,0},{96,32},{1,65},{33,97},{65,1},{97,33},{2,66}... | collective-permute-start | bytes 479240 | tf_op jit(solution)/shard_map/ppermute | solution.py:263
  81.6 40.2 %collective-permute-start.24 = (bf16[1536,256]{1,0:T(8,128)(2,1)}, bf16[1536,256]{1,0:T(8,128)(2,1)}, u32[]{:S(2)}, u32[]{:S(2)}) collective-permute-start(bf16[1536,256]{1,0:T(8,128)(2,1)} %get-tuple-element.73), channel_id=1, source_target_pairs={{0,128},{128,0},{1,129},{129,1},{2,130},{130,2},{3,131},{131,3},{4... | collective-permute-start | bytes 2359304 | tf_op jit(solution)/shard_map/ppermute | solution.py:263
  86.3 18.6 %all-to-all-start = ((bf16[8,16,896]{2,1,0:T(8,128)(2,1)}), bf16[8,16,896]{2,1,0:T(8,128)(2,1)S(1)}, u32[]{:S(2)}, u32[]{:S(2)}) async-start(bf16[8,16,896]{2,1,0:T(8,128)(2,1)} %shard_map.119), calls=%async_computation | async-start | bytes 458752 | tf_op jit(solution)/shard_map/all_to_all | solution.py:267
  94.7 27.1 %collective-permute-start.25 = (bf16[1536,256]{1,0:T(8,128)(2,1)}, bf16[1536,256]{1,0:T(8,128)(2,1)}, u32[]{:S(2)}, u32[]{:S(2)}) collective-permute-start(bf16[1536,256]{1,0:T(8,128)(2,1)} %copy-done.12), channel_id=1, source_target_pairs={{0,128},{128,0},{1,129},{129,1},{2,130},{130,2},{3,131},{131,3},{4... | collective-permute-start | bytes 2359304 | tf_op jit(solution)/shard_map/ppermute | solution.py:263
  94.7 27.1 %collective-permute-start.26 = (bf16[1536,256]{1,0:T(8,128)(2,1)}, bf16[1536,256]{1,0:T(8,128)(2,1)}, u32[]{:S(2)}, u32[]{:S(2)}) collective-permute-start(bf16[1536,256]{1,0:T(8,128)(2,1)} %copy-done.11), channel_id=1, source_target_pairs={{0,128},{128,0},{1,129},{129,1},{2,130},{130,2},{3,131},{131,3},{4... | collective-permute-start | bytes 2359304 | tf_op jit(solution)/shard_map/ppermute | solution.py:263
  119.2 9.6 %collective-permute-start.23 = (bf16[128,768]{1,0:T(8,128)(2,1)S(1)}, bf16[128,768]{1,0:T(8,128)(2,1)S(1)}, u32[]{:S(2)}, u32[]{:S(2)}) collective-permute-start(bf16[128,768]{1,0:T(8,128)(2,1)S(1)} %bitcast.11), channel_id=1, source_target_pairs={{0,2},{1,3},{2,0},{3,1},{4,6},{5,7},{6,4},{7,5},{8,10},{9,11},{10,... | collective-permute-start | bytes 589832 | tf_op jit(solution)/shard_map/ppermute | solution.py:263
  119.3 9.5 %collective-permute-start.22 = (bf16[128,768]{1,0:T(8,128)(2,1)S(1)}, bf16[128,768]{1,0:T(8,128)(2,1)S(1)}, u32[]{:S(2)}, u32[]{:S(2)}) collective-permute-start(bf16[128,768]{1,0:T(8,128)(2,1)S(1)} %bitcast.12), channel_id=1, source_target_pairs={{0,3},{1,0},{2,1},{3,2},{4,7},{5,4},{6,5},{7,6},{8,11},{9,8},{10,9... | collective-permute-start | bytes 589832 | tf_op jit(solution)/shard_map/ppermute | solution.py:263
  121.9 6.9 %collective-permute-start.21 = (bf16[128,768]{1,0:T(8,128)(2,1)S(1)}, bf16[128,768]{1,0:T(8,128)(2,1)S(1)}, u32[]{:S(2)}, u32[]{:S(2)}) collective-permute-start(bf16[128,768]{1,0:T(8,128)(2,1)S(1)} %bitcast.13), channel_id=1, source_target_pairs={{0,1},{1,2},{2,3},{3,0},{4,5},{5,6},{6,7},{7,4},{8,9},{9,10},{10,1... | collective-permute-start | bytes 589832 | tf_op jit(solution)/shard_map/ppermute | solution.py:263
  (17 other events, 254.7 us)

commit v3 on v1

--- a/solution.py
+++ b/solution.py
@@ -73,24 +73,25 @@
     return lax.dot_general(pick, facts.astype(BF), NT, preferred_element_type=F32).astype(BF)
 
 
-def far_kernel(pos, ids_ref, gw_ref, tok_ref, cot_ref, out, tok_out, cot_out, sems):
-    copies = [
-        pltpu.make_async_copy(tok_ref, tok_out, sems.at[0]),
-        pltpu.make_async_copy(cot_ref, cot_out, sems.at[1]),
-    ]
+def far_kernel(pos, ids_in, gw_in, tok_ref, cot_ref, out, tok_out, cot_out, ids_ref, gw_ref, sems):
+    pairs = ((ids_in, ids_ref), (gw_in, gw_ref), (tok_ref, tok_out), (cot_ref, cot_out))
+    copies = [pltpu.make_async_copy(a, b, sems.at[k]) for k, (a, b) in enumerate(pairs)]
     for copy in copies:
         copy.start()
+    copies[0].wait()
+    copies[1].wait()
     member, rank, hits = routing(pos, ids_ref, (2,))
     width = tok_ref.shape[1]
     slots = out.shape[0]
     pick = picks(rank, member, 0, slots, lax.rem(pos[3], 2) * slots)
     out[:, width:] = facts_of(pick, hits[0], gw_ref)
-    for copy in copies:
-        copy.wait()
+    copies[2].wait()
 
     @pl.when(pos[3] < 2)
     def _():
         out[:, :width] = jnp.dot(pick, tok_out[...], preferred_element_type=F32).astype(BF)
+
+    copies[3].wait()
 
     @pl.when(pos[3] >= 2)
     def _():
@@ -164,18 +165,22 @@
         part += lax.dot_general(dpu, wu[at : at + block, :], NT, preferred_element_type=F32)
         whole[j] = part.astype(BF)
     slots = sends[0].shape[0] - 8
-    for c in range(len(sends) // 4):
+    for c in range(len(msgs)):
         at = slice(c * slots, (c + 1) * slots)
         padded = jnp.concatenate([share[at], jnp.zeros((LANES - slots, units), F32)], axis=0)
         line = lax.dot_general(
             jnp.ones((8, units), F32), padded, NT,
             precision=lax.Precision.HIGHEST, preferred_element_type=F32,
         ).astype(BF)
-        for j in range(4):
-            send = sends[4 * c + j]
+        for j, send in enumerate(sends[4 * c : 4 * c + 4]):
             send[:slots] = whole[lax.rem(pos[3] + j, 4), at, :]
             send[slots:, :LANES] = line
             send[slots:, LANES:] = jnp.zeros((8, block - LANES), BF)
+
+
+def sum_kernel(pos, a_ref, b_ref, c_ref, d_ref, out):
+    total = a_ref[...].astype(F32) + b_ref[...].astype(F32)
+    out[...] = (total + (c_ref[...].astype(F32) + d_ref[...].astype(F32))).astype(BF)
 
 
 def combine_kernel(pos, ids_ref, *refs):
@@ -184,15 +189,17 @@
     tokens = zs * rows
     width = wide - LANES
     slots = refs[0].shape[0] - 8
+    groups = (refs[:1], refs[1:5], refs[5:9], refs[9:10])
     member, rank, _ = routing(pos, ids_ref, OFFSETS)
     result = jnp.zeros((tokens, width), F32)
     gates = []
     for k in range(4):
-        group = refs[4 * k : 4 * k + 4]
-        total = group[0][...].astype(F32)
-        for ref in group[1:]:
-            total += ref[...].astype(F32)
-        total = total.astype(BF)
+        total = groups[k][0][...]
+        if len(groups[k]) > 1:
+            total = total.astype(F32)
+            for ref in groups[k][1:]:
+                total += ref[...].astype(F32)
+            total = total.astype(BF)
         pick = picks(rank, member, k, slots, 0)
         result += lax.dot_general(pick, total[:slots], TN, preferred_element_type=F32)
         pick = picks(rank, member, k, LANES, 0)
@@ -291,8 +298,12 @@
         [array(slots // 2, width + LANES), array(*tokens.shape), array(*tokens.shape)],
         (pos, *given, tokens, cotangent),
         free=(0, 1, 2, 3),
-        unblocked=(2, 3),
-        scratch=[pltpu.SemaphoreType.DMA((2,))],
+        unblocked=(0, 1, 2, 3),
+        scratch=[
+            pltpu.VMEM(given[0].shape, jnp.int32),
+            pltpu.VMEM(given[1].shape, BF),
+            pltpu.SemaphoreType.DMA((4,)),
+        ],
     )
     given = (*given, tokens, cotangent)
     plus, minus = call(
@@ -318,20 +329,28 @@
         return call(
             functools.partial(expert_kernel, kind),
             [array(slots + 8, block)] * (4 * count)
-            + [plain(count * slots, 3 * units)]
+            + [array(count * slots, 3 * units)]
             + [array(slots, long)] * (kind == "far"),
             (pos, *msgs, *weights),
             scratch=[pltpu.VMEM((4, count * slots, block), BF)],
         )
 
-    def back(sends, offset):
-        kept = [sends[0]] if offset == 0 else [shift_two(sends[0], -offset, 0)]
-        return kept + [shift_two(sends[j], -offset, j) for j in (1, 3, 2)]
+    def scatter(sends):
+        got = [sends[0]] + [shift(sends[j], "y", j) for j in (1, 3, 2)]
+        return call(sum_kernel, [array(slots + 8, block)], (pos, *got))[0]
+
+    def direct(sends, offset):
+        return [shift_two(sends[j], -offset, j) for j in (2, 1, 3, 0)]
 
     local = expert(pos, [here], "here")
     remote = expert(after(pos, local[0]), far, "far")
     sides = expert(after(pos, remote[0]), [plus, minus], "sides")
-    groups = [*back(local[:4], 0), *back(sides[:4], 1), *back(sides[4:8], -1), *back(remote[:4], 2)]
+    groups = [
+        scatter(local[:4]),
+        *direct(sides[:4], 1),
+        *direct(sides[4:8], -1),
+        shift(scatter(remote[:4]), "expert", 2),
+    ]
     (mine,) = call(combine_kernel, [plain(zs, rows, block + LANES)], (pos, expert_ids.T, *groups))
     mine, gate_grad = call(
         gather_kernel,

time: 129 us -> 127 us (0.984)
  the two profiles are of different devices: /device:TPU:2 before, /device:TPU:8 now
where the time goes in v3:
time: 127 us; the launch traced here: 125 us
  starting transfers between devices  45.7 us (36%)
  waiting for transfers between devices  34.4 us (27%)
  Pallas kernels  27.2 us (21%)
  blocking collectives  13.1 us (10%)
  local copies, waits for them, and re-layouts  3.46 us (3%)
    pallas_call x13, Pallas kernels, call(): pl.pallas_call(kernel, out_shape=outs, in_specs=specs, out_specs=[spec] *...  27.2 us
    ppermute x22, starting transfers between devices, shift(): lax.ppermute(value, axis, [(i, (i + offset) % size) for i in range(size)])  26.5 us
    ppermute x22, waiting for transfers between devices, shift(): lax.ppermute(value, axis, [(i, (i + offset) % size) for i in range(size)])  16.1 us
    all_to_all x1, blocking collectives, exchange(): return lax.all_to_all(value, axis, split_axis=0, concat_axis=0, tiled=True)  13.1 us
    ppermute x8, starting transfers between devices, shift_two(): return lax.ppermute(value, ('expert', 'y'), pairs)  10.7 us
    all_to_all x1, waiting for transfers between devices, exchange(): return lax.all_to_all(value, axis, split_axis=0, concat_axis=0, tiled=True)  9.62 us
    ppermute x8, waiting for transfers between devices, shift_two(): return lax.ppermute(value, ('expert', 'y'), pairs)  8.76 us
    all_to_all x1, starting transfers between devices, exchange(): return lax.all_to_all(value, axis, split_axis=0, concat_axis=0, tiled=True)  8.47 us
  transfers between devices with their start and end apart: 31, of which 12 were waited for; matrix products, arithmetic and copies ran while one was open for 0% of the time, Pallas kernels for 19%

profile of v3, /device:TPU:8, one launch (start us, length us, event | category | flops | bytes accessed | tf_op | source)
XLA Modules:
  0.0 124.7 jit_solution(9831514650791420707)
XLA Ops:
  0.7 2.2 %shard_map.110 = (bf16[48,3200]{1,0:T(8,128)(2,1)S(1)}, bf16[128,3072]{1,0:T(8,128)(2,1)S(1)}, bf16[128,3072]{1,0:T(8,128)(2,1)S(1)}) custom-call(s32[4]{0:T(128)S(1)} %pad_add_fusion.pos, s32[2,128]{1,0:T(2,128)} %bitcast.15, bf16[2,128]{1,0:T(2,128)(2,1)} %bitcast.20, bf16[128,3072]{1,0:T(8,128)(2,1)} %tok_ref.1, bf16[128,3072]{1,0:T(8,128)(2,1)} %cot_ref.1), custom_call_target="tpu_custom_call" | custom-call | tf_op jit(solution)/shard_map/pallas_call | solution.py:38
  2.9 3.1 %collective-permute-start.6 = (bf16[48,3200]{1,0:T(8,128)(2,1)S(1)}, bf16[48,3200]{1,0:T(8,128)(2,1)S(1)}, u32[]{:S(2)}, u32[]{:S(2)}) collective-permute-start(bf16[48,3200]{1,0:T(8,128)(2,1)S(1)} %get-tuple-element.56), channel_id=1, source_target_pairs={{0,64},{32,96},{64,0},{96,32},{1,65},{33,97},{65,1},{97,33},{2,66}... | collective-permute-start | bytes 921608 | tf_op jit(solution)/shard_map/ppermute | solution.py:265
  9.5 4.0 %collective-permute-done.6.refs_0_ = bf16[48,3200]{1,0:T(8,128)(2,1)S(1)} collective-permute-done((bf16[48,3200]{1,0:T(8,128)(2,1)S(1)}, bf16[48,3200]{1,0:T(8,128)(2,1)S(1)}, u32[]{:S(2)}, u32[]{:S(2)}) %collective-permute-start.6) | collective-permute-done | bytes 307232 | tf_op jit(solution)/shard_map/ppermute | solution.py:265
  13.5 2.7 %collective-permute-start.10 = (bf16[96,6272]{1,0:T(8,128)(2,1)S(1)}, bf16[96,6272]{1,0:T(8,128)(2,1)S(1)}, u32[]{:S(2)}, u32[]{:S(2)}) collective-permute-start(bf16[96,6272]{1,0:T(8,128)(2,1)S(1)} %get-tuple-element.46), channel_id=1, source_target_pairs={{0,32},{32,64},{64,96},{96,0},{1,33},{33,65},{65,97},{97,1},{2,34}... | collective-permute-start | bytes 3612680 | tf_op jit(solution)/shard_map/ppermute | solution.py:265
  16.2 2.5 %collective-permute-start.9 = (bf16[48,3200]{1,0:T(8,128)(2,1)S(1)}, bf16[48,3200]{1,0:T(8,128)(2,1)S(1)}, u32[]{:S(2)}, u32[]{:S(2)}) collective-permute-start(bf16[48,3200]{1,0:T(8,128)(2,1)S(1)} %collective-permute-done.6.refs_0_), channel_id=1, source_target_pairs={{0,2},{1,3},{2,0},{3,1},{4,6},{5,7},{6,4},{7,5},{8,10},{9,11},{10,... | collective-permute-start | bytes 921608 | tf_op jit(solution)/shard_map/ppermute | solution.py:265
  22.0 2.9 %shard_map.113 = (bf16[104,768]{1,0:T(8,128)(2,1)S(1)}, bf16[104,768]{1,0:T(8,128)(2,1)S(1)}, bf16[104,768]{1,0:T(8,128)(2,1)S(1)}, bf16[104,768]{1,0:T(8,128)(2,1)S(1)}, bf16[96,768]{1,0:T(8,128)(2,1)S(1)}) custom-call(s32[4]{0:T(128)S(1)} %pad_add_fusion.pos, bf16[96,6272]{1,0:T(8,128)(2,1)S(1)} %shard_map.112.refs_0_.here_ref, ...), custom_call_target="tpu_custom_call" | custom-call | tf_op jit(solution)/shard_map/pallas_call | solution.py:38
  24.9 2.8 %collective-permute-done.9.refs_3_ = bf16[48,3200]{1,0:T(8,128)(2,1)S(1)} collective-permute-done((bf16[48,3200]{1,0:T(8,128)(2,1)S(1)}, bf16[48,3200]{1,0:T(8,128)(2,1)S(1)}, u32[]{:S(2)}, u32[]{:S(2)}) %collective-permute-start.9) | collective-permute-done | bytes 307232 | tf_op jit(solution)/shard_map/ppermute | solution.py:265
  27.7 3.2 %collective-permute-done.8.refs_2_ = bf16[48,3200]{1,0:T(8,128)(2,1)S(1)} collective-permute-done((bf16[48,3200]{1,0:T(8,128)(2,1)S(1)}, bf16[48,3200]{1,0:T(8,128)(2,1)S(1)}, u32[]{:S(2)}, u32[]{:S(2)}) %collective-permute-start.8) | collective-permute-done | bytes 307232 | tf_op jit(solution)/shard_map/ppermute | solution.py:265
  31.4 3.0 %shard_map.115 = (bf16[104,768]{1,0:T(8,128)(2,1)S(1)}, bf16[104,768]{1,0:T(8,128)(2,1)S(1)}, bf16[104,768]{1,0:T(8,128)(2,1)S(1)}, bf16[104,768]{1,0:T(8,128)(2...) custom-call(s32[4]{0:T(128)S(1)} %pad_add_fusion.pos, ...), custom_call_target="tpu_custom_call" | custom-call | tf_op jit(solution)/shard_map/pallas_call | solution.py:38
  36.4 2.1 %collective-permute-start.22 = (bf16[104,768]{1,0:T(8,128)(2,1)S(1)}, bf16[104,768]{1,0:T(8,128)(2,1)S(1)}, u32[]{:S(2)}, u32[]{:S(2)}) collective-permute-start(bf16[104,768]{1,0:T(8,128)(2,1)S(1)} %get-tuple-element.70), channel_id=1, source_target_pairs={{0,2},{1,3},{2,0},{3,1},{4,6},{5,7},{6,4},{7,5},{8,10},{9,11},{10,... | collective-permute-start | bytes 479240 | tf_op jit(solution)/shard_map/ppermute | solution.py:265
  43.1 3.8 %collective-permute-done.22.d_ref = bf16[104,768]{1,0:T(8,128)(2,1)S(1)} collective-permute-done((bf16[104,768]{1,0:T(8,128)(2,1)S(1)}, bf16[104,768]{1,0:T(8,128)(2,1)S(1)}, u32[]{:S(2)}, u32[]{:S(2)}) %collective-permute-start.22) | collective-permute-done | bytes 159776 | tf_op jit(solution)/shard_map/ppermute | solution.py:265
  48.7 2.8 %collective-permute-start.23 = (bf16[104,768]{1,0:T(8,128)(2,1)S(1)}, bf16[104,768]{1,0:T(8,128)(2,1)S(1)}, u32[]{:S(2)}, u32[]{:S(2)}) collective-permute-start(bf16[104,768]{1,0:T(8,128)(2,1)S(1)} %shard_map.117), channel_id=1, source_target_pairs={{0,64},{32,96},{64,0},{96,32},{1,65},{33,97},{65,1},{97,33},{2,66}... | collective-permute-start | bytes 479240 | tf_op jit(solution)/shard_map/ppermute | solution.py:265
  51.4 3.4 %shard_map.116 = (bf16[104,768]{1,0:T(8,128)(2,1)S(1)}, bf16[104,768]{1,0:T(8,128)(2,1)S(1)}, bf16[104,768]{1,0:T(8,128)(2,1)S(1)}, bf16[104,768]{1,0:T(8,128)(2...) custom-call(s32[4]{0:T(128)S(1)} %pad_add_fusion.pos, ...), custom_call_target="tpu_custom_call" | custom-call | tf_op jit(solution)/shard_map/pallas_call | solution.py:38
  54.9 3.4 %collective-permute-start.12 = (bf16[104,768]{1,0:T(8,128)(2,1)S(1)}, bf16[104,768]{1,0:T(8,128)(2,1)S(1)}, u32[]{:S(2)}, u32[]{:S(2)}) collective-permute-start(bf16[104,768]{1,0:T(8,128)(2,1)S(1)} %get-tuple-element.60), channel_id=1, source_target_pairs={{0,98},{1,99},{2,96},{3,97},{32,2},{33,3},{34,0},{35,1},{64,34},{6... | collective-permute-start | bytes 479240 | tf_op jit(solution)/shard_map/ppermute | solution.py:272
  58.3 1.9 %collective-permute-start.14 = (bf16[104,768]{1,0:T(8,128)(2,1)S(1)}, bf16[104,768]{1,0:T(8,128)(2,1)S(1)}, u32[]{:S(2)}, u32[]{:S(2)}) collective-permute-start(bf16[104,768]{1,0:T(8,128)(2,1)S(1)} %get-tuple-element.62), channel_id=1, source_target_pairs={{0,99},{1,96},{2,97},{3,98},{32,3},{33,0},{34,1},{35,2},{64,35},{6... | collective-permute-start | bytes 479240 | tf_op jit(solution)/shard_map/ppermute | solution.py:272
  60.3 2.1 %collective-permute-start.15 = (bf16[104,768]{1,0:T(8,128)(2,1)S(1)}, bf16[104,768]{1,0:T(8,128)(2,1)S(1)}, u32[]{:S(2)}, u32[]{:S(2)}) collective-permute-start(bf16[104,768]{1,0:T(8,128)(2,1)S(1)} %get-tuple-element.63), channel_id=1, source_target_pairs={{0,96},{1,97},{2,98},{3,99},{32,0},{33,1},{34,2},{35,3},{64,32},{6... | collective-permute-start | bytes 479240 | tf_op jit(solution)/shard_map/ppermute | solution.py:272
  62.5 2.3 %collective-permute-done.12.refs_1_ = bf16[104,768]{1,0:T(8,128)(2,1)S(1)} collective-permute-done((bf16[104,768]{1,0:T(8,128)(2,1)S(1)}, bf16[104,768]{1,0:T(8,128)(2,1)S(1)}, u32[]{:S(2)}, u32[]{:S(2)}) %collective-permute-start.12) | collective-permute-done | bytes 159776 | tf_op jit(solution)/shard_map/ppermute | solution.py:272
  65.6 2.7 %collective-permute-done.13.refs_2_ = bf16[104,768]{1,0:T(8,128)(2,1)S(1)} collective-permute-done((bf16[104,768]{1,0:T(8,128)(2,1)S(1)}, bf16[104,768]{1,0:T(8,128)(2,1)S(1)}, u32[]{:S(2)}, u32[]{:S(2)}) %collective-permute-start.13) | collective-permute-done | bytes 159776 | tf_op jit(solution)/shard_map/ppermute | solution.py:272
  70.7 2.7 %shard_map.121 = (bf16[1536,256]{1,0:T(8,128)(2,1)}, bf16[1536,256]{1,0:T(8,128)(2,1)S(1)}, bf16[1536,256]{1,0:T(8,128)(2,1)S(1)}) custom-call(s32[4]{0:T(128)S(1)} %pad_add_fusion.pos, bf16[96,6272]{1,0:T(8,128)(2,1)S(1)} %shard_map.112.refs_0_.here_ref, bf16[96,6272]{1,0:T(8,128)(2,1)S(1)} %get-tuple-element.73.far_ref, ...), custom_call_target="tpu_custom_call" | custom-call | tf_op jit(solution)/shard_map/pallas_call | solution.py:38
  76.7 1.9 %collective-permute-done.19.refs_8_ = bf16[104,768]{1,0:T(8,128)(2,1)S(1)} collective-permute-done((bf16[104,768]{1,0:T(8,128)(2,1)S(1)}, bf16[104,768]{1,0:T(8,128)(2,1)S(1)}, u32[]{:S(2)}, u32[]{:S(2)}) %collective-permute-start.19) | collective-permute-done | bytes 159776 | tf_op jit(solution)/shard_map/ppermute | solution.py:272
  80.5 8.5 %all-to-all-start = ((bf16[8,16,896]{2,1,0:T(8,128)(2,1)}), bf16[8,16,896]{2,1,0:T(8,128)(2,1)S(1)}, u32[]{:S(2)}, u32[]{:S(2)}) async-start(bf16[8,16,896]{2,1,0:T(8,128)(2,1)} %shard_map.118), calls=%async_computation | async-start | bytes 458752 | tf_op jit(solution)/shard_map/all_to_all | solution.py:276
  89.4 9.6 %all-to-all-done.got_ref = bf16[8,16,896]{2,1,0:T(8,128)(2,1)S(1)} async-done(((bf16[8,16,896]{2,1,0:T(8,128)(2,1)}), bf16[8,16,896]{2,1,0:T(8,128)(2,1)S(1)}, u32[]{:S(2)}, u32[]{:S(2)}) %all-to-all-start) | async-done | bytes 229408 | tf_op jit(solution)/shard_map/all_to_all | solution.py:276
  100.3 13.1 %all_to_all.10 = bf16[8,16,768]{2,1,0:T(8,128)(2,1)S(1)} all-to-all(bf16[8,16,768]{2,1,0:T(8,128)(2,1)} %get-tuple-element.71), channel_id=1, replica_groups=mesh['dp'=2,'expert'=4,'z'=8,'y'=4] {'z'}, dimensions={0} | all-to-all | bytes 393216 | tf_op jit(solution)/shard_map/all_to_all | solution.py:276
  118.8 4.4 %shard_map.122 = (bf16[1536,256]{1,0:T(8,128)(2,1)}, bf16[1536,256]{1,0:T(8,128)(2,1)}, bf16[1536,256]{1,0:T(8,128)(2,1)}) custom-call(s32[4]{0:T(128)S(1)} %pad_add_fusion.pos, bf16[96,6272]{1,0:T(8,128)(2,1)S(1)} %shard_map.112.refs_0_.here_ref, bf16[96,6272]{1,0:T(8,128)(2,1)S(1)} %copy-done.6, bf16[96,6272]{1,0:T(8,128)(2,1)S(1)} %copy-done.1, ...), custom_call_target="tpu_custom_call" | custom-call | tf_op jit(solution)/shard_map/pallas_call | solution.py:38
  (73 shorter events, 32.7 us)
Async XLA Ops:
  2.9 10.6 %collective-permute-start.6 = (bf16[48,3200]{1,0:T(8,128)(2,1)S(1)}, bf16[48,3200]{1,0:T(8,128)(2,1)S(1)}, u32[]{:S(2)}, u32[]{:S(2)}) collective-permute-start(bf16[48,3200]{1,0:T(8,128)(2,1)S(1)} %get-tuple-element.56), channel_id=1, source_target_pairs={{0,64},{32,96},{64,0},{96,32},{1,65},{33,97},{65,1},{97,33},{2,66}... | collective-permute-start | bytes 921608 | tf_op jit(solution)/shard_map/ppermute | solution.py:265
  7.7 11.0 %collective-permute-start.1 = (bf16[1,1536,256]{2,1,0:T(8,128)(2,1)S(1)}, bf16[1,1536,256]{2,1,0:T(8,128)(2,1)S(1)}, u32[]{:S(2)}, u32[]{:S(2)}) collective-permute-start(bf16[1,1536,256]{2,1,0:T(8,128)(2,1)S(1)} %copy-done.3), channel_id=1, source_target_pairs={{0,128},{128,0},{1,129},{129,1},{2,130},{130,2},{3,131},{131,3},{4... | collective-permute-start | bytes 2359304 | tf_op jit(solution)/shard_map/ppermute | solution.py:265
  8.2 11.8 %collective-permute-start.2 = (bf16[1,1536,256]{2,1,0:T(8,128)(2,1)S(1)}, bf16[1,1536,256]{2,1,0:T(8,128)(2,1)S(1)}, u32[]{:S(2)}, u32[]{:S(2)}) collective-permute-start(bf16[1,1536,256]{2,1,0:T(8,128)(2,1)S(1)} %copy-done.4), channel_id=1, source_target_pairs={{0,128},{128,0},{1,129},{129,1},{2,130},{130,2},{3,131},{131,3},{4... | collective-permute-start | bytes 2359304 | tf_op jit(solution)/shard_map/ppermute | solution.py:265
  8.3 40.3 %collective-permute-start.11 = (bf16[96,6272]{1,0:T(8,128)(2,1)S(1)}, bf16[96,6272]{1,0:T(8,128)(2,1)S(1)}, u32[]{:S(2)}, u32[]{:S(2)}) collective-permute-start(bf16[96,6272]{1,0:T(8,128)(2,1)S(1)} %get-tuple-element.59), channel_id=1, source_target_pairs={{0,96},{32,0},{64,32},{96,64},{1,97},{33,1},{65,33},{97,65},{2,98}... | collective-permute-start | bytes 3612680 | tf_op jit(solution)/shard_map/ppermute | solution.py:265
  13.5 38.0 %collective-permute-start.10 = (bf16[96,6272]{1,0:T(8,128)(2,1)S(1)}, bf16[96,6272]{1,0:T(8,128)(2,1)S(1)}, u32[]{:S(2)}, u32[]{:S(2)}) collective-permute-start(bf16[96,6272]{1,0:T(8,128)(2,1)S(1)} %get-tuple-element.46), channel_id=1, source_target_pairs={{0,32},{32,64},{64,96},{96,0},{1,33},{33,65},{65,97},{97,1},{2,34}... | collective-permute-start | bytes 3612680 | tf_op jit(solution)/shard_map/ppermute | solution.py:265
  16.2 11.6 %collective-permute-start.9 = (bf16[48,3200]{1,0:T(8,128)(2,1)S(1)}, bf16[48,3200]{1,0:T(8,128)(2,1)S(1)}, u32[]{:S(2)}, u32[]{:S(2)}) collective-permute-start(bf16[48,3200]{1,0:T(8,128)(2,1)S(1)} %collective-permute-done.6.refs_0_), channel_id=1, source_target_pairs={{0,2},{1,3},{2,0},{3,1},{4,6},{5,7},{6,4},{7,5},{8,10},{9,11},{10,... | collective-permute-start | bytes 921608 | tf_op jit(solution)/shard_map/ppermute | solution.py:265
  18.7 12.3 %collective-permute-start.8 = (bf16[48,3200]{1,0:T(8,128)(2,1)S(1)}, bf16[48,3200]{1,0:T(8,128)(2,1)S(1)}, u32[]{:S(2)}, u32[]{:S(2)}) collective-permute-start(bf16[48,3200]{1,0:T(8,128)(2,1)S(1)} %collective-permute-done.6.refs_0_), channel_id=1, source_target_pairs={{0,3},{1,0},{2,1},{3,2},{4,7},{5,4},{6,5},{7,6},{8,11},{9,8},{10,9... | collective-permute-start | bytes 921608 | tf_op jit(solution)/shard_map/ppermute | solution.py:265
  20.0 11.3 %collective-permute-start.7 = (bf16[48,3200]{1,0:T(8,128)(2,1)S(1)}, bf16[48,3200]{1,0:T(8,128)(2,1)S(1)}, u32[]{:S(2)}, u32[]{:S(2)}) collective-permute-start(bf16[48,3200]{1,0:T(8,128)(2,1)S(1)} %collective-permute-done.6.refs_0_), channel_id=1, source_target_pairs={{0,1},{1,2},{2,3},{3,0},{4,5},{5,6},{6,7},{7,4},{8,9},{9,10},{10,1... | collective-permute-start | bytes 921608 | tf_op jit(solution)/shard_map/ppermute | solution.py:265
  36.4 10.5 %collective-permute-start.22 = (bf16[104,768]{1,0:T(8,128)(2,1)S(1)}, bf16[104,768]{1,0:T(8,128)(2,1)S(1)}, u32[]{:S(2)}, u32[]{:S(2)}) collective-permute-start(bf16[104,768]{1,0:T(8,128)(2,1)S(1)} %get-tuple-element.70), channel_id=1, source_target_pairs={{0,2},{1,3},{2,0},{3,1},{4,6},{5,7},{6,4},{7,5},{8,10},{9,11},{10,... | collective-permute-start | bytes 479240 | tf_op jit(solution)/shard_map/ppermute | solution.py:265
  40.0 18.3 %collective-permute-start.3 = (bf16[104,768]{1,0:T(8,128)(2,1)S(1)}, bf16[104,768]{1,0:T(8,128)(2,1)S(1)}, u32[]{:S(2)}, u32[]{:S(2)}) collective-permute-start(bf16[104,768]{1,0:T(8,128)(2,1)S(1)} %get-tuple-element.52), channel_id=1, source_target_pairs={{0,1},{1,2},{2,3},{3,0},{4,5},{5,6},{6,7},{7,4},{8,9},{9,10},{10,1... | collective-permute-start | bytes 479240 | tf_op jit(solution)/shard_map/ppermute | solution.py:265
  41.8 16.5 %collective-permute-start.4 = (bf16[104,768]{1,0:T(8,128)(2,1)S(1)}, bf16[104,768]{1,0:T(8,128)(2,1)S(1)}, u32[]{:S(2)}, u32[]{:S(2)}) collective-permute-start(bf16[104,768]{1,0:T(8,128)(2,1)S(1)} %get-tuple-element.53), channel_id=1, source_target_pairs={{0,3},{1,0},{2,1},{3,2},{4,7},{5,4},{6,5},{7,6},{8,11},{9,8},{10,9... | collective-permute-start | bytes 479240 | tf_op jit(solution)/shard_map/ppermute | solution.py:265
  46.9 13.3 %collective-permute-start.5 = (bf16[104,768]{1,0:T(8,128)(2,1)S(1)}, bf16[104,768]{1,0:T(8,128)(2,1)S(1)}, u32[]{:S(2)}, u32[]{:S(2)}) collective-permute-start(bf16[104,768]{1,0:T(8,128)(2,1)S(1)} %get-tuple-element.54), channel_id=1, source_target_pairs={{0,2},{1,3},{2,0},{3,1},{4,6},{5,7},{6,4},{7,5},{8,10},{9,11},{10,... | collective-permute-start | bytes 479240 | tf_op jit(solution)/shard_map/ppermute | solution.py:265
  48.7 13.7 %collective-permute-start.23 = (bf16[104,768]{1,0:T(8,128)(2,1)S(1)}, bf16[104,768]{1,0:T(8,128)(2,1)S(1)}, u32[]{:S(2)}, u32[]{:S(2)}) collective-permute-start(bf16[104,768]{1,0:T(8,128)(2,1)S(1)} %shard_map.117), channel_id=1, source_target_pairs={{0,64},{32,96},{64,0},{96,32},{1,65},{33,97},{65,1},{97,33},{2,66}... | collective-permute-start | bytes 479240 | tf_op jit(solution)/shard_map/ppermute | solution.py:265
  54.9 10.0 %collective-permute-start.12 = (bf16[104,768]{1,0:T(8,128)(2,1)S(1)}, bf16[104,768]{1,0:T(8,128)(2,1)S(1)}, u32[]{:S(2)}, u32[]{:S(2)}) collective-permute-start(bf16[104,768]{1,0:T(8,128)(2,1)S(1)} %get-tuple-element.60), channel_id=1, source_target_pairs={{0,98},{1,99},{2,96},{3,97},{32,2},{33,3},{34,0},{35,1},{64,34},{6... | collective-permute-start | bytes 479240 | tf_op jit(solution)/shard_map/ppermute | solution.py:272
  58.3 10.0 %collective-permute-start.13 = (bf16[104,768]{1,0:T(8,128)(2,1)S(1)}, bf16[104,768]{1,0:T(8,128)(2,1)S(1)}, u32[]{:S(2)}, u32[]{:S(2)}) collective-permute-start(bf16[104,768]{1,0:T(8,128)(2,1)S(1)} %get-tuple-element.61), channel_id=1, source_target_pairs={{0,97},{1,98},{2,99},{3,96},{32,1},{33,2},{34,3},{35,0},{64,33},{6... | collective-permute-start | bytes 479240 | tf_op jit(solution)/shard_map/ppermute | solution.py:272
  58.3 11.2 %collective-permute-start.14 = (bf16[104,768]{1,0:T(8,128)(2,1)S(1)}, bf16[104,768]{1,0:T(8,128)(2,1)S(1)}, u32[]{:S(2)}, u32[]{:S(2)}) collective-permute-start(bf16[104,768]{1,0:T(8,128)(2,1)S(1)} %get-tuple-element.62), channel_id=1, source_target_pairs={{0,99},{1,96},{2,97},{3,98},{32,3},{33,0},{34,1},{35,2},{64,35},{6... | collective-permute-start | bytes 479240 | tf_op jit(solution)/shard_map/ppermute | solution.py:272
  60.3 14.0 %collective-permute-start.15 = (bf16[104,768]{1,0:T(8,128)(2,1)S(1)}, bf16[104,768]{1,0:T(8,128)(2,1)S(1)}, u32[]{:S(2)}, u32[]{:S(2)}) collective-permute-start(bf16[104,768]{1,0:T(8,128)(2,1)S(1)} %get-tuple-element.63), channel_id=1, source_target_pairs={{0,96},{1,97},{2,98},{3,99},{32,0},{33,1},{34,2},{35,3},{64,32},{6... | collective-permute-start | bytes 479240 | tf_op jit(solution)/shard_map/ppermute | solution.py:272
  62.4 12.5 %collective-permute-start.16 = (bf16[104,768]{1,0:T(8,128)(2,1)S(1)}, bf16[104,768]{1,0:T(8,128)(2,1)S(1)}, u32[]{:S(2)}, u32[]{:S(2)}) collective-permute-start(bf16[104,768]{1,0:T(8,128)(2,1)S(1)} %get-tuple-element.64), channel_id=1, source_target_pairs={{0,34},{1,35},{2,32},{3,33},{32,66},{33,67},{34,64},{35,65},{64,98... | collective-permute-start | bytes 479240 | tf_op jit(solution)/shard_map/ppermute | solution.py:272
  64.8 10.1 %collective-permute-start.17 = (bf16[104,768]{1,0:T(8,128)(2,1)S(1)}, bf16[104,768]{1,0:T(8,128)(2,1)S(1)}, u32[]{:S(2)}, u32[]{:S(2)}) collective-permute-start(bf16[104,768]{1,0:T(8,128)(2,1)S(1)} %get-tuple-element.65), channel_id=1, source_target_pairs={{0,33},{1,34},{2,35},{3,32},{32,65},{33,66},{34,67},{35,64},{64,97... | collective-permute-start | bytes 479240 | tf_op jit(solution)/shard_map/ppermute | solution.py:272
  74.3 41.5 %collective-permute-start.27 = (bf16[1536,256]{1,0:T(8,128)(2,1)}, bf16[1536,256]{1,0:T(8,128)(2,1)}, u32[]{:S(2)}, u32[]{:S(2)}) collective-permute-start(bf16[1536,256]{1,0:T(8,128)(2,1)} %get-tuple-element.77), channel_id=1, source_target_pairs={{0,128},{128,0},{1,129},{129,1},{2,130},{130,2},{3,131},{131,3},{4... | collective-permute-start | bytes 2359304 | tf_op jit(solution)/shard_map/ppermute | solution.py:265
  80.5 18.6 %all-to-all-start = ((bf16[8,16,896]{2,1,0:T(8,128)(2,1)}), bf16[8,16,896]{2,1,0:T(8,128)(2,1)S(1)}, u32[]{:S(2)}, u32[]{:S(2)}) async-start(bf16[8,16,896]{2,1,0:T(8,128)(2,1)} %shard_map.118), calls=%async_computation | async-start | bytes 458752 | tf_op jit(solution)/shard_map/all_to_all | solution.py:276
  88.9 27.4 %collective-permute-start.28 = (bf16[1536,256]{1,0:T(8,128)(2,1)}, bf16[1536,256]{1,0:T(8,128)(2,1)}, u32[]{:S(2)}, u32[]{:S(2)}) collective-permute-start(bf16[1536,256]{1,0:T(8,128)(2,1)} %copy-done.9), channel_id=1, source_target_pairs={{0,128},{128,0},{1,129},{129,1},{2,130},{130,2},{3,131},{131,3},{4... | collective-permute-start | bytes 2359304 | tf_op jit(solution)/shard_map/ppermute | solution.py:265
  88.9 27.4 %collective-permute-start.29 = (bf16[1536,256]{1,0:T(8,128)(2,1)}, bf16[1536,256]{1,0:T(8,128)(2,1)}, u32[]{:S(2)}, u32[]{:S(2)}) collective-permute-start(bf16[1536,256]{1,0:T(8,128)(2,1)} %copy-done.8), channel_id=1, source_target_pairs={{0,128},{128,0},{1,129},{129,1},{2,130},{130,2},{3,131},{131,3},{4... | collective-permute-start | bytes 2359304 | tf_op jit(solution)/shard_map/ppermute | solution.py:265
  113.4 9.8 %collective-permute-start.26 = (bf16[128,768]{1,0:T(8,128)(2,1)S(1)}, bf16[128,768]{1,0:T(8,128)(2,1)S(1)}, u32[]{:S(2)}, u32[]{:S(2)}) collective-permute-start(bf16[128,768]{1,0:T(8,128)(2,1)S(1)} %bitcast.11), channel_id=1, source_target_pairs={{0,2},{1,3},{2,0},{3,1},{4,6},{5,7},{6,4},{7,5},{8,10},{9,11},{10,... | collective-permute-start | bytes 589832 | tf_op jit(solution)/shard_map/ppermute | solution.py:265
  (17 other events, 146.9 us)

commit v4 on v2

--- a/solution.py
+++ b/solution.py
@@ -73,24 +73,25 @@
     return lax.dot_general(pick, facts.astype(BF), NT, preferred_element_type=F32).astype(BF)
 
 
-def far_kernel(pos, ids_ref, gw_ref, tok_ref, cot_ref, out, tok_out, cot_out, sems):
-    copies = [
-        pltpu.make_async_copy(tok_ref, tok_out, sems.at[0]),
-        pltpu.make_async_copy(cot_ref, cot_out, sems.at[1]),
-    ]
+def far_kernel(pos, ids_in, gw_in, tok_ref, cot_ref, out, tok_out, cot_out, ids_ref, gw_ref, sems):
+    pairs = ((ids_in, ids_ref), (gw_in, gw_ref), (tok_ref, tok_out), (cot_ref, cot_out))
+    copies = [pltpu.make_async_copy(a, b, sems.at[k]) for k, (a, b) in enumerate(pairs)]
     for copy in copies:
         copy.start()
+    copies[0].wait()
+    copies[1].wait()
     member, rank, hits = routing(pos, ids_ref, (2,))
     width = tok_ref.shape[1]
     slots = out.shape[0]
     pick = picks(rank, member, 0, slots, lax.rem(pos[3], 2) * slots)
     out[:, width:] = facts_of(pick, hits[0], gw_ref)
-    for copy in copies:
-        copy.wait()
+    copies[2].wait()
 
     @pl.when(pos[3] < 2)
     def _():
         out[:, :width] = jnp.dot(pick, tok_out[...], preferred_element_type=F32).astype(BF)
+
+    copies[3].wait()
 
     @pl.when(pos[3] >= 2)
     def _():
@@ -289,8 +290,12 @@
         [array(slots // 2, width + LANES), array(*tokens.shape), array(*tokens.shape)],
         (pos, *given, tokens, cotangent),
         free=(0, 1, 2, 3),
-        unblocked=(2, 3),
-        scratch=[pltpu.SemaphoreType.DMA((2,))],
+        unblocked=(0, 1, 2, 3),
+        scratch=[
+            pltpu.VMEM(given[0].shape, jnp.int32),
+            pltpu.VMEM(given[1].shape, BF),
+            pltpu.SemaphoreType.DMA((4,)),
+        ],
     )
     given = (*given, tokens, cotangent)
     plus, minus = call(
@@ -316,7 +321,7 @@
         return call(
             functools.partial(expert_kernel, kind),
             [array(count * (slots + 8), block)] * 4
-            + [plain(count * slots, 3 * units)]
+            + [array(count * slots, 3 * units)]
             + [array(slots, long)] * (kind == "far"),
             (pos, *msgs, *weights),
             scratch=[pltpu.VMEM((4, count * slots, block), BF)],

time: 133 us -> 132 us (level)
  Pallas kernels: 29.8 us -> 27.9 us
    pallas_call x14, Pallas kernels: 29.8 us -> 27.9 us  [call(): pl.pallas_call(kernel, out_shape=outs, in_specs=specs, out_specs=[spec] *...]
  transfers between devices with their start and end apart: 28 -> 28, of which waited for: 9 -> 9; matrix products, arithmetic and copies ran while one was open for 0% -> 0% of each run, Pallas kernels for 20% -> 19%
where the time goes in v4:
time: 132 us; the launch traced here: 130 us
  waiting for transfers between devices  43.6 us (33%)
  starting transfers between devices  41.9 us (32%)
  Pallas kernels  27.9 us (21%)
  blocking collectives  13.1 us (10%)
  local copies, waits for them, and re-layouts  2.58 us (2%)
    ppermute x27, waiting for transfers between devices, shift(): lax.ppermute(value, axis, [(i, (i + offset) % size) for i in range(size)])  34 us
    ppermute x27, starting transfers between devices, shift(): lax.ppermute(value, axis, [(i, (i + offset) % size) for i in range(size)])  33.4 us
    pallas_call x14, Pallas kernels, call(): pl.pallas_call(kernel, out_shape=outs, in_specs=specs, out_specs=[spec] *...  27.9 us
    all_to_all x1, blocking collectives, exchange(): return lax.all_to_all(value, axis, split_axis=0, concat_axis=0, tiled=True)  13.1 us
    all_to_all x1, waiting for transfers between devices, exchange(): return lax.all_to_all(value, axis, split_axis=0, concat_axis=0, tiled=True)  9.62 us
    all_to_all x1, starting transfers between devices, exchange(): return lax.all_to_all(value, axis, split_axis=0, concat_axis=0, tiled=True)  8.45 us
  transfers between devices with their start and end apart: 28, of which 9 were waited for; matrix products, arithmetic and copies ran while one was open for 0% of the time, Pallas kernels for 19%

profile of v4, /device:TPU:8, one launch (start us, length us, event | category | flops | bytes accessed | tf_op | source)
XLA Modules:
  0.0 129.9 jit_solution(2896906349713618706)
XLA Ops:
  0.7 2.2 %shard_map.110 = (bf16[48,3200]{1,0:T(8,128)(2,1)S(1)}, bf16[128,3072]{1,0:T(8,128)(2,1)S(1)}, bf16[128,3072]{1,0:T(8,128)(2,1)S(1)}) custom-call(s32[4]{0:T(128)S(1)} %pad_add_fusion.pos, s32[2,128]{1,0:T(2,128)} %bitcast.15, bf16[2,128]{1,0:T(2,128)(2,1)} %bitcast.20, bf16[128,3072]{1,0:T(8,128)(2,1)} %tok_ref.1, bf16[128,3072]{1,0:T(8,128)(2,1)} %cot_ref.1), custom_call_target="tpu_custom_call" | custom-call | tf_op jit(solution)/shard_map/pallas_call | solution.py:38
  2.9 3.1 %collective-permute-start.6 = (bf16[48,3200]{1,0:T(8,128)(2,1)S(1)}, bf16[48,3200]{1,0:T(8,128)(2,1)S(1)}, u32[]{:S(2)}, u32[]{:S(2)}) collective-permute-start(bf16[48,3200]{1,0:T(8,128)(2,1)S(1)} %get-tuple-element.54), channel_id=1, source_target_pairs={{0,64},{32,96},{64,0},{96,32},{1,65},{33,97},{65,1},{97,33},{2,66}... | collective-permute-start | bytes 921608 | tf_op jit(solution)/shard_map/ppermute | solution.py:264
  10.2 4.4 %collective-permute-done.6.refs_0_ = bf16[48,3200]{1,0:T(8,128)(2,1)S(1)} collective-permute-done((bf16[48,3200]{1,0:T(8,128)(2,1)S(1)}, bf16[48,3200]{1,0:T(8,128)(2,1)S(1)}, u32[]{:S(2)}, u32[]{:S(2)}) %collective-permute-start.6) | collective-permute-done | bytes 307232 | tf_op jit(solution)/shard_map/ppermute | solution.py:264
  14.6 2.6 %collective-permute-start.9 = (bf16[48,3200]{1,0:T(8,128)(2,1)S(1)}, bf16[48,3200]{1,0:T(8,128)(2,1)S(1)}, u32[]{:S(2)}, u32[]{:S(2)}) collective-permute-start(bf16[48,3200]{1,0:T(8,128)(2,1)S(1)} %collective-permute-done.6.refs_0_), channel_id=1, source_target_pairs={{0,2},{1,3},{2,0},{3,1},{4,6},{5,7},{6,4},{7,5},{8,10},{9,11},{10,... | collective-permute-start | bytes 921608 | tf_op jit(solution)/shard_map/ppermute | solution.py:264
  20.6 2.9 %shard_map.113 = (bf16[104,768]{1,0:T(8,128)(2,1)S(1)}, bf16[104,768]{1,0:T(8,128)(2,1)S(1)}, bf16[104,768]{1,0:T(8,128)(2,1)S(1)}, bf16[104,768]{1,0:T(8,128)(2,1)S(1)}, bf16[96,768]{1,0:T(8,128)(2,1)S(1)}) custom-call(s32[4]{0:T(128)S(1)} %pad_add_fusion.pos, bf16[96,6272]{1,0:T(8,128)(2,1)S(1)} %shard_map.112.refs_0_.here_ref, ...), custom_call_target="tpu_custom_call" | custom-call | tf_op jit(solution)/shard_map/pallas_call | solution.py:38
  23.5 3.0 %collective-permute-done.9.refs_3_ = bf16[48,3200]{1,0:T(8,128)(2,1)S(1)} collective-permute-done((bf16[48,3200]{1,0:T(8,128)(2,1)S(1)}, bf16[48,3200]{1,0:T(8,128)(2,1)S(1)}, u32[]{:S(2)}, u32[]{:S(2)}) %collective-permute-start.9) | collective-permute-done | bytes 307232 | tf_op jit(solution)/shard_map/ppermute | solution.py:264
  26.4 6.0 %collective-permute-done.8.refs_2_ = bf16[48,3200]{1,0:T(8,128)(2,1)S(1)} collective-permute-done((bf16[48,3200]{1,0:T(8,128)(2,1)S(1)}, bf16[48,3200]{1,0:T(8,128)(2,1)S(1)}, u32[]{:S(2)}, u32[]{:S(2)}) %collective-permute-start.8) | collective-permute-done | bytes 307232 | tf_op jit(solution)/shard_map/ppermute | solution.py:264
  32.8 2.9 %shard_map.115 = (bf16[104,768]{1,0:T(8,128)(2,1)S(1)}, bf16[104,768]{1,0:T(8,128)(2,1)S(1)}, bf16[104,768]{1,0:T(8,128)(2,1)S(1)}, bf16[104,768]{1,0:T(8,128)(2...) custom-call(s32[4]{0:T(128)S(1)} %pad_add_fusion.pos, ...), custom_call_target="tpu_custom_call" | custom-call | tf_op jit(solution)/shard_map/pallas_call | solution.py:38
  37.3 2.1 %collective-permute-done.11.refs_1_.minus_ref = bf16[96,6272]{1,0:T(8,128)(2,1)S(1)} collective-permute-done((bf16[96,6272]{1,0:T(8,128)(2,1)S(1)}, bf16[96,6272]{1,0:T(8,128)(2,1)S(1)}, u32[]{:S(2)}, u32[]{:S(2)}) %collective-permute-start.11) | collective-permute-done | bytes 1204256 | tf_op jit(solution)/shard_map/ppermute | solution.py:264
  39.4 3.4 %shard_map.116 = (bf16[208,768]{1,0:T(8,128)(2,1)S(1)}, bf16[208,768]{1,0:T(8,128)(2,1)S(1)}, bf16[208,768]{1,0:T(8,128)(2,1)S(1)}, bf16[208,768]{1,0:T(8,128)(2,1)S(1)}, bf16[192,768]{1,0:T(8,128)(2,1)S(1)}) custom-call(s32[4]{0:T(128)S(1)} %pad_add_fusion.pos, bf16[96,6272]{1,0:T(8,128)(2,1)S(1)} %collective-permute-done.10.refs_0_.plus_ref, ...), custom_call_target="tpu_custom_call" | custom-call | tf_op jit(solution)/shard_map/pallas_call | solution.py:38
  42.9 1.9 %collective-permute-start.12 = (bf16[208,768]{1,0:T(8,128)(2,1)S(1)}, bf16[208,768]{1,0:T(8,128)(2,1)S(1)}, u32[]{:S(2)}, u32[]{:S(2)}) collective-permute-start(bf16[208,768]{1,0:T(8,128)(2,1)S(1)} %get-tuple-element.59), channel_id=1, source_target_pairs={{0,1},{1,2},{2,3},{3,0},{4,5},{5,6},{6,7},{7,4},{8,9},{9,10},{10,1... | collective-permute-start | bytes 958472 | tf_op jit(solution)/shard_map/ppermute | solution.py:264
  45.0 2.5 %collective-permute-start.14 = (bf16[208,768]{1,0:T(8,128)(2,1)S(1)}, bf16[208,768]{1,0:T(8,128)(2,1)S(1)}, u32[]{:S(2)}, u32[]{:S(2)}) collective-permute-start(bf16[208,768]{1,0:T(8,128)(2,1)S(1)} %get-tuple-element.61), channel_id=1, source_target_pairs={{0,2},{1,3},{2,0},{3,1},{4,6},{5,7},{6,4},{7,5},{8,10},{9,11},{10,... | collective-permute-start | bytes 958472 | tf_op jit(solution)/shard_map/ppermute | solution.py:264
  49.9 14.7 %collective-permute-done.18.c_ref = bf16[104,768]{1,0:T(8,128)(2,1)S(1)} collective-permute-done((bf16[104,768]{1,0:T(8,128)(2,1)S(1)}, bf16[104,768]{1,0:T(8,128)(2,1)S(1)}, u32[]{:S(2)}, u32[]{:S(2)}) %collective-permute-start.18) | collective-permute-done | bytes 159776 | tf_op jit(solution)/shard_map/ppermute | solution.py:264
  64.7 1.9 %collective-permute-start.3 = (bf16[104,768]{1,0:T(8,128)(2,1)S(1)}, bf16[104,768]{1,0:T(8,128)(2,1)S(1)}, u32[]{:S(2)}, u32[]{:S(2)}) collective-permute-start(bf16[104,768]{1,0:T(8,128)(2,1)S(1)} %get-tuple-element.50), channel_id=1, source_target_pairs={{0,1},{1,2},{2,3},{3,0},{4,5},{5,6},{6,7},{7,4},{8,9},{9,10},{10,1... | collective-permute-start | bytes 479240 | tf_op jit(solution)/shard_map/ppermute | solution.py:264
  68.5 3.6 %collective-permute-start.5 = (bf16[104,768]{1,0:T(8,128)(2,1)S(1)}, bf16[104,768]{1,0:T(8,128)(2,1)S(1)}, u32[]{:S(2)}, u32[]{:S(2)}) collective-permute-start(bf16[104,768]{1,0:T(8,128)(2,1)S(1)} %get-tuple-element.52), channel_id=1, source_target_pairs={{0,2},{1,3},{2,0},{3,1},{4,6},{5,7},{6,4},{7,5},{8,10},{9,11},{10,... | collective-permute-start | bytes 479240 | tf_op jit(solution)/shard_map/ppermute | solution.py:264
  72.1 3.6 %collective-permute-start.20 = (bf16[104,768]{1,0:T(8,128)(2,1)S(1)}, bf16[104,768]{1,0:T(8,128)(2,1)S(1)}, u32[]{:S(2)}, u32[]{:S(2)}) collective-permute-start(bf16[104,768]{1,0:T(8,128)(2,1)S(1)} %shard_map.118), channel_id=1, source_target_pairs={{0,64},{32,96},{64,0},{96,32},{1,65},{33,97},{65,1},{97,33},{2,66}... | collective-permute-start | bytes 479240 | tf_op jit(solution)/shard_map/ppermute | solution.py:264
  78.4 2.7 %shard_map.122 = (bf16[1536,256]{1,0:T(8,128)(2,1)}, bf16[1536,256]{1,0:T(8,128)(2,1)S(1)}, bf16[1536,256]{1,0:T(8,128)(2,1)S(1)}) custom-call(s32[4]{0:T(128)S(1)} %pad_add_fusion.pos, bf16[96,6272]{1,0:T(8,128)(2,1)S(1)} %shard_map.112.refs_0_.here_ref, bf16[96,6272]{1,0:T(8,128)(2,1)S(1)} %get-tuple-element.69.far_ref, ...), custom_call_target="tpu_custom_call" | custom-call | tf_op jit(solution)/shard_map/pallas_call | solution.py:38
  81.9 2.1 %collective-permute-done.16.refs_2_ = bf16[104,768]{1,0:T(8,128)(2,1)S(1)} collective-permute-done((bf16[104,768]{1,0:T(8,128)(2,1)S(1)}, bf16[104,768]{1,0:T(8,128)(2,1)S(1)}, u32[]{:S(2)}, u32[]{:S(2)}) %collective-permute-start.16) | collective-permute-done | bytes 159776 | tf_op jit(solution)/shard_map/ppermute | solution.py:264
  84.0 1.8 %shard_map.119 = bf16[8,16,896]{2,1,0:T(8,128)(2,1)} custom-call(s32[4]{0:T(128)S(1)} %pad_add_fusion.pos, s32[2,128]{1,0:T(2,128)S(1)} %bitcast.18, bf16[104,768]{1,0:T(8,128)(2,1)S(1)} %shard_map.114.refs_0_, bf16[104,768]{1,0:T(8,128)(2,1)S(1)} %collective-permute-done.15.refs_1_, bf16[104,768]{1,0:T(8,128)(2,1)S(1)} %collective-permute-done.16.refs_2_, ...), custom_call_target="tpu_custom_call" | custom-call | tf_op jit(solution)/shard_map/pallas_call | solution.py:38
  85.8 8.5 %all-to-all-start = ((bf16[8,16,896]{2,1,0:T(8,128)(2,1)}), bf16[8,16,896]{2,1,0:T(8,128)(2,1)S(1)}, u32[]{:S(2)}, u32[]{:S(2)}) async-start(bf16[8,16,896]{2,1,0:T(8,128)(2,1)} %shard_map.119), calls=%async_computation | async-start | bytes 458752 | tf_op jit(solution)/shard_map/all_to_all | solution.py:268
  94.8 9.6 %all-to-all-done.got_ref = bf16[8,16,896]{2,1,0:T(8,128)(2,1)S(1)} async-done(((bf16[8,16,896]{2,1,0:T(8,128)(2,1)}), bf16[8,16,896]{2,1,0:T(8,128)(2,1)S(1)}, u32[]{:S(2)}, u32[]{:S(2)}) %all-to-all-start) | async-done | bytes 229408 | tf_op jit(solution)/shard_map/all_to_all | solution.py:268
  105.7 13.1 %all_to_all.10 = bf16[8,16,768]{2,1,0:T(8,128)(2,1)S(1)} all-to-all(bf16[8,16,768]{2,1,0:T(8,128)(2,1)} %get-tuple-element.67), channel_id=1, replica_groups=mesh['dp'=2,'expert'=4,'z'=8,'y'=4] {'z'}, dimensions={0} | all-to-all | bytes 393216 | tf_op jit(solution)/shard_map/all_to_all | solution.py:268
  118.9 2.6 %collective-permute-start.22 = (bf16[128,768]{1,0:T(8,128)(2,1)S(1)}, bf16[128,768]{1,0:T(8,128)(2,1)S(1)}, u32[]{:S(2)}, u32[]{:S(2)}) collective-permute-start(bf16[128,768]{1,0:T(8,128)(2,1)S(1)} %bitcast.12), channel_id=1, source_target_pairs={{0,3},{1,0},{2,1},{3,2},{4,7},{5,4},{6,5},{7,6},{8,11},{9,8},{10,9... | collective-permute-start | bytes 589832 | tf_op jit(solution)/shard_map/ppermute | solution.py:264
  124.0 4.3 %shard_map.123 = (bf16[1536,256]{1,0:T(8,128)(2,1)}, bf16[1536,256]{1,0:T(8,128)(2,1)}, bf16[1536,256]{1,0:T(8,128)(2,1)}) custom-call(s32[4]{0:T(128)S(1)} %pad_add_fusion.pos, bf16[96,6272]{1,0:T(8,128)(2,1)S(1)} %shard_map.112.refs_0_.here_ref, bf16[96,6272]{1,0:T(8,128)(2,1)S(1)} %copy-done.6, bf16[96,6272]{1,0:T(8,128)(2,1)S(1)} %copy-done.1, ...), custom_call_target="tpu_custom_call" | custom-call | tf_op jit(solution)/shard_map/pallas_call | solution.py:38
  (68 shorter events, 23.6 us)
Async XLA Ops:
  2.9 11.7 %collective-permute-start.6 = (bf16[48,3200]{1,0:T(8,128)(2,1)S(1)}, bf16[48,3200]{1,0:T(8,128)(2,1)S(1)}, u32[]{:S(2)}, u32[]{:S(2)}) collective-permute-start(bf16[48,3200]{1,0:T(8,128)(2,1)S(1)} %get-tuple-element.54), channel_id=1, source_target_pairs={{0,64},{32,96},{64,0},{96,32},{1,65},{33,97},{65,1},{97,33},{2,66}... | collective-permute-start | bytes 921608 | tf_op jit(solution)/shard_map/ppermute | solution.py:264
  7.6 31.8 %collective-permute-start.11 = (bf16[96,6272]{1,0:T(8,128)(2,1)S(1)}, bf16[96,6272]{1,0:T(8,128)(2,1)S(1)}, u32[]{:S(2)}, u32[]{:S(2)}) collective-permute-start(bf16[96,6272]{1,0:T(8,128)(2,1)S(1)} %get-tuple-element.57), channel_id=1, source_target_pairs={{0,96},{32,0},{64,32},{96,64},{1,97},{33,1},{65,33},{97,65},{2,98}... | collective-permute-start | bytes 3612680 | tf_op jit(solution)/shard_map/ppermute | solution.py:264
  8.8 30.6 %collective-permute-start.10 = (bf16[96,6272]{1,0:T(8,128)(2,1)S(1)}, bf16[96,6272]{1,0:T(8,128)(2,1)S(1)}, u32[]{:S(2)}, u32[]{:S(2)}) collective-permute-start(bf16[96,6272]{1,0:T(8,128)(2,1)S(1)} %get-tuple-element.44), channel_id=1, source_target_pairs={{0,32},{32,64},{64,96},{96,0},{1,33},{33,65},{65,97},{97,1},{2,34}... | collective-permute-start | bytes 3612680 | tf_op jit(solution)/shard_map/ppermute | solution.py:264
  9.7 7.5 %collective-permute-start.1 = (bf16[1,1536,256]{2,1,0:T(8,128)(2,1)S(1)}, bf16[1,1536,256]{2,1,0:T(8,128)(2,1)S(1)}, u32[]{:S(2)}, u32[]{:S(2)}) collective-permute-start(bf16[1,1536,256]{2,1,0:T(8,128)(2,1)S(1)} %copy-done.3), channel_id=1, source_target_pairs={{0,128},{128,0},{1,129},{129,1},{2,130},{130,2},{3,131},{131,3},{4... | collective-permute-start | bytes 2359304 | tf_op jit(solution)/shard_map/ppermute | solution.py:264
  14.6 11.8 %collective-permute-start.9 = (bf16[48,3200]{1,0:T(8,128)(2,1)S(1)}, bf16[48,3200]{1,0:T(8,128)(2,1)S(1)}, u32[]{:S(2)}, u32[]{:S(2)}) collective-permute-start(bf16[48,3200]{1,0:T(8,128)(2,1)S(1)} %collective-permute-done.6.refs_0_), channel_id=1, source_target_pairs={{0,2},{1,3},{2,0},{3,1},{4,6},{5,7},{6,4},{7,5},{8,10},{9,11},{10,... | collective-permute-start | bytes 921608 | tf_op jit(solution)/shard_map/ppermute | solution.py:264
  17.3 15.2 %collective-permute-start.8 = (bf16[48,3200]{1,0:T(8,128)(2,1)S(1)}, bf16[48,3200]{1,0:T(8,128)(2,1)S(1)}, u32[]{:S(2)}, u32[]{:S(2)}) collective-permute-start(bf16[48,3200]{1,0:T(8,128)(2,1)S(1)} %collective-permute-done.6.refs_0_), channel_id=1, source_target_pairs={{0,3},{1,0},{2,1},{3,2},{4,7},{5,4},{6,5},{7,6},{8,11},{9,8},{10,9... | collective-permute-start | bytes 921608 | tf_op jit(solution)/shard_map/ppermute | solution.py:264
  18.6 14.2 %collective-permute-start.7 = (bf16[48,3200]{1,0:T(8,128)(2,1)S(1)}, bf16[48,3200]{1,0:T(8,128)(2,1)S(1)}, u32[]{:S(2)}, u32[]{:S(2)}) collective-permute-start(bf16[48,3200]{1,0:T(8,128)(2,1)S(1)} %collective-permute-done.6.refs_0_), channel_id=1, source_target_pairs={{0,1},{1,2},{2,3},{3,0},{4,5},{5,6},{6,7},{7,4},{8,9},{9,10},{10,1... | collective-permute-start | bytes 921608 | tf_op jit(solution)/shard_map/ppermute | solution.py:264
  35.7 13.1 %collective-permute-start.17 = (bf16[104,768]{1,0:T(8,128)(2,1)S(1)}, bf16[104,768]{1,0:T(8,128)(2,1)S(1)}, u32[]{:S(2)}, u32[]{:S(2)}) collective-permute-start(bf16[104,768]{1,0:T(8,128)(2,1)S(1)} %get-tuple-element.64), channel_id=1, source_target_pairs={{0,1},{1,2},{2,3},{3,0},{4,5},{5,6},{6,7},{7,4},{8,9},{9,10},{10,1... | collective-permute-start | bytes 479240 | tf_op jit(solution)/shard_map/ppermute | solution.py:264
  42.9 25.6 %collective-permute-start.12 = (bf16[208,768]{1,0:T(8,128)(2,1)S(1)}, bf16[208,768]{1,0:T(8,128)(2,1)S(1)}, u32[]{:S(2)}, u32[]{:S(2)}) collective-permute-start(bf16[208,768]{1,0:T(8,128)(2,1)S(1)} %get-tuple-element.59), channel_id=1, source_target_pairs={{0,1},{1,2},{2,3},{3,0},{4,5},{5,6},{6,7},{7,4},{8,9},{9,10},{10,1... | collective-permute-start | bytes 958472 | tf_op jit(solution)/shard_map/ppermute | solution.py:264
  44.8 27.3 %collective-permute-start.13 = (bf16[208,768]{1,0:T(8,128)(2,1)S(1)}, bf16[208,768]{1,0:T(8,128)(2,1)S(1)}, u32[]{:S(2)}, u32[]{:S(2)}) collective-permute-start(bf16[208,768]{1,0:T(8,128)(2,1)S(1)} %get-tuple-element.60), channel_id=1, source_target_pairs={{0,3},{1,0},{2,1},{3,2},{4,7},{5,4},{6,5},{7,6},{8,11},{9,8},{10,9... | collective-permute-start | bytes 958472 | tf_op jit(solution)/shard_map/ppermute | solution.py:264
  45.0 30.6 %collective-permute-start.14 = (bf16[208,768]{1,0:T(8,128)(2,1)S(1)}, bf16[208,768]{1,0:T(8,128)(2,1)S(1)}, u32[]{:S(2)}, u32[]{:S(2)}) collective-permute-start(bf16[208,768]{1,0:T(8,128)(2,1)S(1)} %get-tuple-element.61), channel_id=1, source_target_pairs={{0,2},{1,3},{2,0},{3,1},{4,6},{5,7},{6,4},{7,5},{8,10},{9,11},{10,... | collective-permute-start | bytes 958472 | tf_op jit(solution)/shard_map/ppermute | solution.py:264
  47.5 17.1 %collective-permute-start.18 = (bf16[104,768]{1,0:T(8,128)(2,1)S(1)}, bf16[104,768]{1,0:T(8,128)(2,1)S(1)}, u32[]{:S(2)}, u32[]{:S(2)}) collective-permute-start(bf16[104,768]{1,0:T(8,128)(2,1)S(1)} %get-tuple-element.65), channel_id=1, source_target_pairs={{0,3},{1,0},{2,1},{3,2},{4,7},{5,4},{6,5},{7,6},{8,11},{9,8},{10,9... | collective-permute-start | bytes 479240 | tf_op jit(solution)/shard_map/ppermute | solution.py:264
  48.9 19.0 %collective-permute-start.19 = (bf16[104,768]{1,0:T(8,128)(2,1)S(1)}, bf16[104,768]{1,0:T(8,128)(2,1)S(1)}, u32[]{:S(2)}, u32[]{:S(2)}) collective-permute-start(bf16[104,768]{1,0:T(8,128)(2,1)S(1)} %get-tuple-element.66), channel_id=1, source_target_pairs={{0,2},{1,3},{2,0},{3,1},{4,6},{5,7},{6,4},{7,5},{8,10},{9,11},{10,... | collective-permute-start | bytes 479240 | tf_op jit(solution)/shard_map/ppermute | solution.py:264
  64.7 12.9 %collective-permute-start.3 = (bf16[104,768]{1,0:T(8,128)(2,1)S(1)}, bf16[104,768]{1,0:T(8,128)(2,1)S(1)}, u32[]{:S(2)}, u32[]{:S(2)}) collective-permute-start(bf16[104,768]{1,0:T(8,128)(2,1)S(1)} %get-tuple-element.50), channel_id=1, source_target_pairs={{0,1},{1,2},{2,3},{3,0},{4,5},{5,6},{6,7},{7,4},{8,9},{9,10},{10,1... | collective-permute-start | bytes 479240 | tf_op jit(solution)/shard_map/ppermute | solution.py:264
  67.9 13.3 %collective-permute-start.4 = (bf16[104,768]{1,0:T(8,128)(2,1)S(1)}, bf16[104,768]{1,0:T(8,128)(2,1)S(1)}, u32[]{:S(2)}, u32[]{:S(2)}) collective-permute-start(bf16[104,768]{1,0:T(8,128)(2,1)S(1)} %get-tuple-element.51), channel_id=1, source_target_pairs={{0,3},{1,0},{2,1},{3,2},{4,7},{5,4},{6,5},{7,6},{8,11},{9,8},{10,9... | collective-permute-start | bytes 479240 | tf_op jit(solution)/shard_map/ppermute | solution.py:264
  68.5 12.8 %collective-permute-start.5 = (bf16[104,768]{1,0:T(8,128)(2,1)S(1)}, bf16[104,768]{1,0:T(8,128)(2,1)S(1)}, u32[]{:S(2)}, u32[]{:S(2)}) collective-permute-start(bf16[104,768]{1,0:T(8,128)(2,1)S(1)} %get-tuple-element.52), channel_id=1, source_target_pairs={{0,2},{1,3},{2,0},{3,1},{4,6},{5,7},{6,4},{7,5},{8,10},{9,11},{10,... | collective-permute-start | bytes 479240 | tf_op jit(solution)/shard_map/ppermute | solution.py:264
  72.1 9.8 %collective-permute-start.20 = (bf16[104,768]{1,0:T(8,128)(2,1)S(1)}, bf16[104,768]{1,0:T(8,128)(2,1)S(1)}, u32[]{:S(2)}, u32[]{:S(2)}) collective-permute-start(bf16[104,768]{1,0:T(8,128)(2,1)S(1)} %shard_map.118), channel_id=1, source_target_pairs={{0,64},{32,96},{64,0},{96,32},{1,65},{33,97},{65,1},{97,33},{2,66}... | collective-permute-start | bytes 479240 | tf_op jit(solution)/shard_map/ppermute | solution.py:264
  81.2 40.3 %collective-permute-start.24 = (bf16[1536,256]{1,0:T(8,128)(2,1)}, bf16[1536,256]{1,0:T(8,128)(2,1)}, u32[]{:S(2)}, u32[]{:S(2)}) collective-permute-start(bf16[1536,256]{1,0:T(8,128)(2,1)} %get-tuple-element.73), channel_id=1, source_target_pairs={{0,128},{128,0},{1,129},{129,1},{2,130},{130,2},{3,131},{131,3},{4... | collective-permute-start | bytes 2359304 | tf_op jit(solution)/shard_map/ppermute | solution.py:264
  85.8 18.6 %all-to-all-start = ((bf16[8,16,896]{2,1,0:T(8,128)(2,1)}), bf16[8,16,896]{2,1,0:T(8,128)(2,1)S(1)}, u32[]{:S(2)}, u32[]{:S(2)}) async-start(bf16[8,16,896]{2,1,0:T(8,128)(2,1)} %shard_map.119), calls=%async_computation | async-start | bytes 458752 | tf_op jit(solution)/shard_map/all_to_all | solution.py:268
  94.3 27.1 %collective-permute-start.25 = (bf16[1536,256]{1,0:T(8,128)(2,1)}, bf16[1536,256]{1,0:T(8,128)(2,1)}, u32[]{:S(2)}, u32[]{:S(2)}) collective-permute-start(bf16[1536,256]{1,0:T(8,128)(2,1)} %copy-done.9), channel_id=1, source_target_pairs={{0,128},{128,0},{1,129},{129,1},{2,130},{130,2},{3,131},{131,3},{4... | collective-permute-start | bytes 2359304 | tf_op jit(solution)/shard_map/ppermute | solution.py:264
  94.3 27.1 %collective-permute-start.26 = (bf16[1536,256]{1,0:T(8,128)(2,1)}, bf16[1536,256]{1,0:T(8,128)(2,1)}, u32[]{:S(2)}, u32[]{:S(2)}) collective-permute-start(bf16[1536,256]{1,0:T(8,128)(2,1)} %copy-done.8), channel_id=1, source_target_pairs={{0,128},{128,0},{1,129},{129,1},{2,130},{130,2},{3,131},{131,3},{4... | collective-permute-start | bytes 2359304 | tf_op jit(solution)/shard_map/ppermute | solution.py:264
  118.7 9.6 %collective-permute-start.23 = (bf16[128,768]{1,0:T(8,128)(2,1)S(1)}, bf16[128,768]{1,0:T(8,128)(2,1)S(1)}, u32[]{:S(2)}, u32[]{:S(2)}) collective-permute-start(bf16[128,768]{1,0:T(8,128)(2,1)S(1)} %bitcast.11), channel_id=1, source_target_pairs={{0,2},{1,3},{2,0},{3,1},{4,6},{5,7},{6,4},{7,5},{8,10},{9,11},{10,... | collective-permute-start | bytes 589832 | tf_op jit(solution)/shard_map/ppermute | solution.py:264
  118.9 9.5 %collective-permute-start.22 = (bf16[128,768]{1,0:T(8,128)(2,1)S(1)}, bf16[128,768]{1,0:T(8,128)(2,1)S(1)}, u32[]{:S(2)}, u32[]{:S(2)}) collective-permute-start(bf16[128,768]{1,0:T(8,128)(2,1)S(1)} %bitcast.12), channel_id=1, source_target_pairs={{0,3},{1,0},{2,1},{3,2},{4,7},{5,4},{6,5},{7,6},{8,11},{9,8},{10,9... | collective-permute-start | bytes 589832 | tf_op jit(solution)/shard_map/ppermute | solution.py:264
  121.4 6.9 %collective-permute-start.21 = (bf16[128,768]{1,0:T(8,128)(2,1)S(1)}, bf16[128,768]{1,0:T(8,128)(2,1)S(1)}, u32[]{:S(2)}, u32[]{:S(2)}) collective-permute-start(bf16[128,768]{1,0:T(8,128)(2,1)S(1)} %bitcast.13), channel_id=1, source_target_pairs={{0,1},{1,2},{2,3},{3,0},{4,5},{5,6},{6,7},{7,4},{8,9},{9,10},{10,1... | collective-permute-start | bytes 589832 | tf_op jit(solution)/shard_map/ppermute | solution.py:264
  (14 other events, 148.5 us)

commit v5 on v4

--- a/solution.py
+++ b/solution.py
@@ -108,6 +108,13 @@
             pick, cot_ref[...], preferred_element_type=F32
         ).astype(BF)
         out[:, 2 * width :] = facts_of(pick, hits[j], gw_ref)
+
+
+def here_kernel(pos, ids_ref, gw_ref, tok_ref, cot_ref, out, picks_ref):
+    near_kernel((0,), pos, ids_ref, gw_ref, tok_ref, cot_ref, out)
+    member, rank, _ = routing(pos, ids_ref, OFFSETS)
+    for k in range(4):
+        picks_ref[k] = picks(rank, member, k, picks_ref.shape[1], 0)
 
 
 def expert_kernel(kind, pos, *refs):
@@ -188,21 +195,19 @@
         out[...] = (total + (c_ref[at].astype(F32) + d_ref[at].astype(F32))).astype(BF)
 
 
-def combine_kernel(pos, ids_ref, *refs):
+def combine_kernel(pos, picks_ref, *refs):
     out_ref = refs[-1]
     zs, rows, wide = out_ref.shape
     tokens = zs * rows
     width = wide - LANES
     slots = refs[0].shape[0] - 8
-    member, rank, _ = routing(pos, ids_ref, OFFSETS)
     result = jnp.zeros((tokens, width), F32)
     gates = []
     for k in range(4):
         total = refs[k][...]
-        pick = picks(rank, member, k, slots, 0)
+        pick = picks_ref[k, :slots]
         result += lax.dot_general(pick, total[:slots], TN, preferred_element_type=F32)
-        pick = picks(rank, member, k, LANES, 0)
-        line = jnp.dot(total[slots:, :LANES], pick, preferred_element_type=F32)
+        line = jnp.dot(total[slots:, :LANES], picks_ref[k], preferred_element_type=F32)
         gates.append(line[:1])
     gates = jnp.concatenate(gates + [jnp.zeros((rows - 4, tokens), F32)], axis=0).astype(BF)
     result = result.astype(BF)
@@ -305,9 +310,8 @@
         free=(0, 1),
     )
     then = after(pos, plus)
-    (here,) = call(
-        functools.partial(near_kernel, (0,)), [array(slots, long)], (then, *given),
-        free=(0, 1),
+    here, chosen = call(
+        here_kernel, [array(slots, long), array(4, LANES, tok_count)], (then, *given), free=(0, 1)
     )
     weights = []
     for own in (w_gate, w_up, w_down):
@@ -344,10 +348,10 @@
         shift(from_minus, "expert", 1),
         shift(from_far, "expert", 2),
     ]
-    (mine,) = call(combine_kernel, [plain(zs, rows, block + LANES)], (pos, expert_ids.T, *groups))
+    (mine,) = call(combine_kernel, [array(zs, rows, block + LANES)], (pos, chosen, *groups))
     mine, gate_grad = call(
         gather_kernel,
-        [plain(zs, rows, block), plain(2, tok_count)],
+        [array(zs, rows, block), plain(2, tok_count)],
         (pos, expert_ids.T, exchange(mine, "z")),
     )
     slab = exchange(mine, "z").reshape(tok_count, block)

time: 132 us -> 131 us (level)
  no operation moved by 1% of the time
where the time goes in v5:
time: 131 us; the launch traced here: 129 us
  waiting for transfers between devices  43.5 us (33%)
  starting transfers between devices  41.9 us (32%)
  Pallas kernels  27.5 us (21%)
  blocking collectives  12.2 us (9%)
  local copies, waits for them, and re-layouts  2.58 us (2%)
    ppermute x27, waiting for transfers between devices, shift(): lax.ppermute(value, axis, [(i, (i + offset) % size) for i in range(size)])  33.9 us
    ppermute x27, starting transfers between devices, shift(): lax.ppermute(value, axis, [(i, (i + offset) % size) for i in range(size)])  33.4 us
    pallas_call x14, Pallas kernels, call(): pl.pallas_call(kernel, out_shape=outs, in_specs=specs, out_specs=[spec] *...  27.5 us
    all_to_all x1, blocking collectives, exchange(): return lax.all_to_all(value, axis, split_axis=0, concat_axis=0, tiled=True)  12.2 us
    all_to_all x1, waiting for transfers between devices, exchange(): return lax.all_to_all(value, axis, split_axis=0, concat_axis=0, tiled=True)  9.62 us
    all_to_all x1, starting transfers between devices, exchange(): return lax.all_to_all(value, axis, split_axis=0, concat_axis=0, tiled=True)  8.47 us
  transfers between devices with their start and end apart: 28, of which 9 were waited for; matrix products, arithmetic and copies ran while one was open for 0% of the time, Pallas kernels for 19%

profile of v5, /device:TPU:8, one launch (start us, length us, event | category | flops | bytes accessed | tf_op | source)
XLA Modules:
  0.0 128.6 jit_solution(3458971156606493847)
XLA Ops:
  0.7 2.2 %shard_map.110 = (bf16[48,3200]{1,0:T(8,128)(2,1)S(1)}, bf16[128,3072]{1,0:T(8,128)(2,1)S(1)}, bf16[128,3072]{1,0:T(8,128)(2,1)S(1)}) custom-call(s32[4]{0:T(128)S(1)} %pad_add_fusion.pos, s32[2,128]{1,0:T(2,128)} %bitcast.15, bf16[2,128]{1,0:T(2,128)(2,1)} %bitcast.19, bf16[128,3072]{1,0:T(8,128)(2,1)} %tok_ref.1, bf16[128,3072]{1,0:T(8,128)(2,1)} %cot_ref.1), custom_call_target="tpu_custom_call" | custom-call | tf_op jit(solution)/shard_map/pallas_call | solution.py:38
  2.9 3.1 %collective-permute-start.6 = (bf16[48,3200]{1,0:T(8,128)(2,1)S(1)}, bf16[48,3200]{1,0:T(8,128)(2,1)S(1)}, u32[]{:S(2)}, u32[]{:S(2)}) collective-permute-start(bf16[48,3200]{1,0:T(8,128)(2,1)S(1)} %get-tuple-element.58), channel_id=1, source_target_pairs={{0,64},{32,96},{64,0},{96,32},{1,65},{33,97},{65,1},{97,33},{2,66}... | collective-permute-start | bytes 921608 | tf_op jit(solution)/shard_map/ppermute | solution.py:269
  10.2 4.4 %collective-permute-done.6.refs_0_ = bf16[48,3200]{1,0:T(8,128)(2,1)S(1)} collective-permute-done((bf16[48,3200]{1,0:T(8,128)(2,1)S(1)}, bf16[48,3200]{1,0:T(8,128)(2,1)S(1)}, u32[]{:S(2)}, u32[]{:S(2)}) %collective-permute-start.6) | collective-permute-done | bytes 307232 | tf_op jit(solution)/shard_map/ppermute | solution.py:269
  14.6 2.6 %collective-permute-start.9 = (bf16[48,3200]{1,0:T(8,128)(2,1)S(1)}, bf16[48,3200]{1,0:T(8,128)(2,1)S(1)}, u32[]{:S(2)}, u32[]{:S(2)}) collective-permute-start(bf16[48,3200]{1,0:T(8,128)(2,1)S(1)} %collective-permute-done.6.refs_0_), channel_id=1, source_target_pairs={{0,2},{1,3},{2,0},{3,1},{4,6},{5,7},{6,4},{7,5},{8,10},{9,11},{10,... | collective-permute-start | bytes 921608 | tf_op jit(solution)/shard_map/ppermute | solution.py:269
  20.6 2.9 %shard_map.113 = (bf16[104,768]{1,0:T(8,128)(2,1)S(1)}, bf16[104,768]{1,0:T(8,128)(2,1)S(1)}, bf16[104,768]{1,0:T(8,128)(2,1)S(1)}, bf16[104,768]{1,0:T(8,128)(2,1)S(1)}, bf16[96,768]{1,0:T(8,128)(2,1)S(1)}) custom-call(s32[4]{0:T(128)S(1)} %pad_add_fusion.pos, bf16[96,6272]{1,0:T(8,128)(2,1)S(1)} %get-tuple-element.49.refs_0_.here_ref, ...), custom_call_target="tpu_custom_call" | custom-call | tf_op jit(solution)/shard_map/pallas_call | solution.py:38
  23.5 2.9 %collective-permute-done.9.refs_3_ = bf16[48,3200]{1,0:T(8,128)(2,1)S(1)} collective-permute-done((bf16[48,3200]{1,0:T(8,128)(2,1)S(1)}, bf16[48,3200]{1,0:T(8,128)(2,1)S(1)}, u32[]{:S(2)}, u32[]{:S(2)}) %collective-permute-start.9) | collective-permute-done | bytes 307232 | tf_op jit(solution)/shard_map/ppermute | solution.py:269
  26.4 6.0 %collective-permute-done.8.refs_2_ = bf16[48,3200]{1,0:T(8,128)(2,1)S(1)} collective-permute-done((bf16[48,3200]{1,0:T(8,128)(2,1)S(1)}, bf16[48,3200]{1,0:T(8,128)(2,1)S(1)}, u32[]{:S(2)}, u32[]{:S(2)}) %collective-permute-start.8) | collective-permute-done | bytes 307232 | tf_op jit(solution)/shard_map/ppermute | solution.py:269
  32.8 2.9 %shard_map.115 = (bf16[104,768]{1,0:T(8,128)(2,1)S(1)}, bf16[104,768]{1,0:T(8,128)(2,1)S(1)}, bf16[104,768]{1,0:T(8,128)(2,1)S(1)}, bf16[104,768]{1,0:T(8,128)(2...) custom-call(s32[4]{0:T(128)S(1)} %pad_add_fusion.pos, ...), custom_call_target="tpu_custom_call" | custom-call | tf_op jit(solution)/shard_map/pallas_call | solution.py:38
  37.3 2.1 %collective-permute-done.11.refs_1_.minus_ref = bf16[96,6272]{1,0:T(8,128)(2,1)S(1)} collective-permute-done((bf16[96,6272]{1,0:T(8,128)(2,1)S(1)}, bf16[96,6272]{1,0:T(8,128)(2,1)S(1)}, u32[]{:S(2)}, u32[]{:S(2)}) %collective-permute-start.11) | collective-permute-done | bytes 1204256 | tf_op jit(solution)/shard_map/ppermute | solution.py:269
  39.4 3.4 %shard_map.116 = (bf16[208,768]{1,0:T(8,128)(2,1)S(1)}, bf16[208,768]{1,0:T(8,128)(2,1)S(1)}, bf16[208,768]{1,0:T(8,128)(2,1)S(1)}, bf16[208,768]{1,0:T(8,128)(2,1)S(1)}, bf16[192,768]{1,0:T(8,128)(2,1)S(1)}) custom-call(s32[4]{0:T(128)S(1)} %pad_add_fusion.pos, bf16[96,6272]{1,0:T(8,128)(2,1)S(1)} %collective-permute-done.10.refs_0_.plus_ref, ...), custom_call_target="tpu_custom_call" | custom-call | tf_op jit(solution)/shard_map/pallas_call | solution.py:38
  42.9 1.9 %collective-permute-start.12 = (bf16[208,768]{1,0:T(8,128)(2,1)S(1)}, bf16[208,768]{1,0:T(8,128)(2,1)S(1)}, u32[]{:S(2)}, u32[]{:S(2)}) collective-permute-start(bf16[208,768]{1,0:T(8,128)(2,1)S(1)} %get-tuple-element.63), channel_id=1, source_target_pairs={{0,1},{1,2},{2,3},{3,0},{4,5},{5,6},{6,7},{7,4},{8,9},{9,10},{10,1... | collective-permute-start | bytes 958472 | tf_op jit(solution)/shard_map/ppermute | solution.py:269
  45.0 2.6 %collective-permute-start.14 = (bf16[208,768]{1,0:T(8,128)(2,1)S(1)}, bf16[208,768]{1,0:T(8,128)(2,1)S(1)}, u32[]{:S(2)}, u32[]{:S(2)}) collective-permute-start(bf16[208,768]{1,0:T(8,128)(2,1)S(1)} %get-tuple-element.65), channel_id=1, source_target_pairs={{0,2},{1,3},{2,0},{3,1},{4,6},{5,7},{6,4},{7,5},{8,10},{9,11},{10,... | collective-permute-start | bytes 958472 | tf_op jit(solution)/shard_map/ppermute | solution.py:269
  49.9 14.7 %collective-permute-done.18.c_ref = bf16[104,768]{1,0:T(8,128)(2,1)S(1)} collective-permute-done((bf16[104,768]{1,0:T(8,128)(2,1)S(1)}, bf16[104,768]{1,0:T(8,128)(2,1)S(1)}, u32[]{:S(2)}, u32[]{:S(2)}) %collective-permute-start.18) | collective-permute-done | bytes 159776 | tf_op jit(solution)/shard_map/ppermute | solution.py:269
  64.7 1.9 %collective-permute-start.3 = (bf16[104,768]{1,0:T(8,128)(2,1)S(1)}, bf16[104,768]{1,0:T(8,128)(2,1)S(1)}, u32[]{:S(2)}, u32[]{:S(2)}) collective-permute-start(bf16[104,768]{1,0:T(8,128)(2,1)S(1)} %get-tuple-element.54), channel_id=1, source_target_pairs={{0,1},{1,2},{2,3},{3,0},{4,5},{5,6},{6,7},{7,4},{8,9},{9,10},{10,1... | collective-permute-start | bytes 479240 | tf_op jit(solution)/shard_map/ppermute | solution.py:269
  68.5 3.6 %collective-permute-start.5 = (bf16[104,768]{1,0:T(8,128)(2,1)S(1)}, bf16[104,768]{1,0:T(8,128)(2,1)S(1)}, u32[]{:S(2)}, u32[]{:S(2)}) collective-permute-start(bf16[104,768]{1,0:T(8,128)(2,1)S(1)} %get-tuple-element.56), channel_id=1, source_target_pairs={{0,2},{1,3},{2,0},{3,1},{4,6},{5,7},{6,4},{7,5},{8,10},{9,11},{10,... | collective-permute-start | bytes 479240 | tf_op jit(solution)/shard_map/ppermute | solution.py:269
  72.1 3.6 %collective-permute-start.20 = (bf16[104,768]{1,0:T(8,128)(2,1)S(1)}, bf16[104,768]{1,0:T(8,128)(2,1)S(1)}, u32[]{:S(2)}, u32[]{:S(2)}) collective-permute-start(bf16[104,768]{1,0:T(8,128)(2,1)S(1)} %shard_map.118), channel_id=1, source_target_pairs={{0,64},{32,96},{64,0},{96,32},{1,65},{33,97},{65,1},{97,33},{2,66}... | collective-permute-start | bytes 479240 | tf_op jit(solution)/shard_map/ppermute | solution.py:269
  78.4 2.7 %shard_map.122 = (bf16[1536,256]{1,0:T(8,128)(2,1)}, bf16[1536,256]{1,0:T(8,128)(2,1)S(1)}, bf16[1536,256]{1,0:T(8,128)(2,1)S(1)}) custom-call(s32[4]{0:T(128)S(1)} %pad_add_fusion.pos, bf16[96,6272]{1,0:T(8,128)(2,1)S(1)} %get-tuple-element.49.refs_0_.here_ref, bf16[96,6272]{1,0:T(8,128)(2,1)S(1)} %get-tuple-element.73.far_ref, ...), custom_call_target="tpu_custom_call" | custom-call | tf_op jit(solution)/shard_map/pallas_call | solution.py:38
  81.9 2.1 %collective-permute-done.16.refs_2_ = bf16[104,768]{1,0:T(8,128)(2,1)S(1)} collective-permute-done((bf16[104,768]{1,0:T(8,128)(2,1)S(1)}, bf16[104,768]{1,0:T(8,128)(2,1)S(1)}, u32[]{:S(2)}, u32[]{:S(2)}) %collective-permute-start.16) | collective-permute-done | bytes 159776 | tf_op jit(solution)/shard_map/ppermute | solution.py:269
  84.0 1.7 %shard_map.119 = bf16[8,16,896]{2,1,0:T(8,128)(2,1)} custom-call(s32[4]{0:T(128)S(1)} %pad_add_fusion.pos, bf16[4,128,128]{2,1,0:T(8,128)(2,1)S(1)} %get-tuple-element.48.picks_ref, bf16[104,768]{1,0:T(8,128)(2,1)S(1)} %shard_map.114.refs_0_, bf16[104,768]{1,0:T(8,128)(2,1)S(1)} %collective-permute-done.15.refs_1_, ...), custom_call_target="tpu_custom_call" | custom-call | tf_op jit(solution)/shard_map/pallas_call | solution.py:38
  85.7 8.5 %all-to-all-start = ((bf16[8,16,896]{2,1,0:T(8,128)(2,1)}), bf16[8,16,896]{2,1,0:T(8,128)(2,1)S(1)}, u32[]{:S(2)}, u32[]{:S(2)}) async-start(bf16[8,16,896]{2,1,0:T(8,128)(2,1)} %shard_map.119), calls=%async_computation | async-start | bytes 458752 | tf_op jit(solution)/shard_map/all_to_all | solution.py:273
  94.7 9.6 %all-to-all-done.got_ref = bf16[8,16,896]{2,1,0:T(8,128)(2,1)S(1)} async-done(((bf16[8,16,896]{2,1,0:T(8,128)(2,1)}), bf16[8,16,896]{2,1,0:T(8,128)(2,1)S(1)}, u32[]{:S(2)}, u32[]{:S(2)}) %all-to-all-start) | async-done | bytes 229408 | tf_op jit(solution)/shard_map/all_to_all | solution.py:273
  105.4 12.2 %all_to_all.10 = bf16[8,16,768]{2,1,0:T(8,128)(2,1)S(1)} all-to-all(bf16[8,16,768]{2,1,0:T(8,128)(2,1)S(1)} %get-tuple-element.71), channel_id=1, replica_groups=mesh['dp'=2,'expert'=4,'z'=8,'y'=4] {'z'}, dimensions={0} | all-to-all | bytes 393216 | tf_op jit(solution)/shard_map/all_to_all | solution.py:273
  117.6 2.6 %collective-permute-start.22 = (bf16[128,768]{1,0:T(8,128)(2,1)S(1)}, bf16[128,768]{1,0:T(8,128)(2,1)S(1)}, u32[]{:S(2)}, u32[]{:S(2)}) collective-permute-start(bf16[128,768]{1,0:T(8,128)(2,1)S(1)} %bitcast.12), channel_id=1, source_target_pairs={{0,3},{1,0},{2,1},{3,2},{4,7},{5,4},{6,5},{7,6},{8,11},{9,8},{10,9... | collective-permute-start | bytes 589832 | tf_op jit(solution)/shard_map/ppermute | solution.py:269
  122.8 4.3 %shard_map.123 = (bf16[1536,256]{1,0:T(8,128)(2,1)}, bf16[1536,256]{1,0:T(8,128)(2,1)}, bf16[1536,256]{1,0:T(8,128)(2,1)}) custom-call(s32[4]{0:T(128)S(1)} %pad_add_fusion.pos, bf16[96,6272]{1,0:T(8,128)(2,1)S(1)} %copy-done.1, bf16[96,6272]{1,0:T(8,128)(2,1)S(1)} %copy-done.6, bf16[96,6272]{1,0:T(8,128)(2,1)S(1)} %collective-permute-done.10.refs_0_.plus_ref, ...), custom_call_target="tpu_custom_call" | custom-call | tf_op jit(solution)/shard_map/pallas_call | solution.py:38
  (68 shorter events, 23.4 us)
Async XLA Ops:
  2.9 11.7 %collective-permute-start.6 = (bf16[48,3200]{1,0:T(8,128)(2,1)S(1)}, bf16[48,3200]{1,0:T(8,128)(2,1)S(1)}, u32[]{:S(2)}, u32[]{:S(2)}) collective-permute-start(bf16[48,3200]{1,0:T(8,128)(2,1)S(1)} %get-tuple-element.58), channel_id=1, source_target_pairs={{0,64},{32,96},{64,0},{96,32},{1,65},{33,97},{65,1},{97,33},{2,66}... | collective-permute-start | bytes 921608 | tf_op jit(solution)/shard_map/ppermute | solution.py:269
  7.6 31.8 %collective-permute-start.11 = (bf16[96,6272]{1,0:T(8,128)(2,1)S(1)}, bf16[96,6272]{1,0:T(8,128)(2,1)S(1)}, u32[]{:S(2)}, u32[]{:S(2)}) collective-permute-start(bf16[96,6272]{1,0:T(8,128)(2,1)S(1)} %get-tuple-element.61), channel_id=1, source_target_pairs={{0,96},{32,0},{64,32},{96,64},{1,97},{33,1},{65,33},{97,65},{2,98}... | collective-permute-start | bytes 3612680 | tf_op jit(solution)/shard_map/ppermute | solution.py:269
  8.8 30.6 %collective-permute-start.10 = (bf16[96,6272]{1,0:T(8,128)(2,1)S(1)}, bf16[96,6272]{1,0:T(8,128)(2,1)S(1)}, u32[]{:S(2)}, u32[]{:S(2)}) collective-permute-start(bf16[96,6272]{1,0:T(8,128)(2,1)S(1)} %get-tuple-element.46), channel_id=1, source_target_pairs={{0,32},{32,64},{64,96},{96,0},{1,33},{33,65},{65,97},{97,1},{2,34}... | collective-permute-start | bytes 3612680 | tf_op jit(solution)/shard_map/ppermute | solution.py:269
  9.7 7.5 %collective-permute-start.1 = (bf16[1,1536,256]{2,1,0:T(8,128)(2,1)S(1)}, bf16[1,1536,256]{2,1,0:T(8,128)(2,1)S(1)}, u32[]{:S(2)}, u32[]{:S(2)}) collective-permute-start(bf16[1,1536,256]{2,1,0:T(8,128)(2,1)S(1)} %copy-done.3), channel_id=1, source_target_pairs={{0,128},{128,0},{1,129},{129,1},{2,130},{130,2},{3,131},{131,3},{4... | collective-permute-start | bytes 2359304 | tf_op jit(solution)/shard_map/ppermute | solution.py:269
  14.6 11.8 %collective-permute-start.9 = (bf16[48,3200]{1,0:T(8,128)(2,1)S(1)}, bf16[48,3200]{1,0:T(8,128)(2,1)S(1)}, u32[]{:S(2)}, u32[]{:S(2)}) collective-permute-start(bf16[48,3200]{1,0:T(8,128)(2,1)S(1)} %collective-permute-done.6.refs_0_), channel_id=1, source_target_pairs={{0,2},{1,3},{2,0},{3,1},{4,6},{5,7},{6,4},{7,5},{8,10},{9,11},{10,... | collective-permute-start | bytes 921608 | tf_op jit(solution)/shard_map/ppermute | solution.py:269
  17.3 15.2 %collective-permute-start.8 = (bf16[48,3200]{1,0:T(8,128)(2,1)S(1)}, bf16[48,3200]{1,0:T(8,128)(2,1)S(1)}, u32[]{:S(2)}, u32[]{:S(2)}) collective-permute-start(bf16[48,3200]{1,0:T(8,128)(2,1)S(1)} %collective-permute-done.6.refs_0_), channel_id=1, source_target_pairs={{0,3},{1,0},{2,1},{3,2},{4,7},{5,4},{6,5},{7,6},{8,11},{9,8},{10,9... | collective-permute-start | bytes 921608 | tf_op jit(solution)/shard_map/ppermute | solution.py:269
  18.6 14.2 %collective-permute-start.7 = (bf16[48,3200]{1,0:T(8,128)(2,1)S(1)}, bf16[48,3200]{1,0:T(8,128)(2,1)S(1)}, u32[]{:S(2)}, u32[]{:S(2)}) collective-permute-start(bf16[48,3200]{1,0:T(8,128)(2,1)S(1)} %collective-permute-done.6.refs_0_), channel_id=1, source_target_pairs={{0,1},{1,2},{2,3},{3,0},{4,5},{5,6},{6,7},{7,4},{8,9},{9,10},{10,1... | collective-permute-start | bytes 921608 | tf_op jit(solution)/shard_map/ppermute | solution.py:269
  35.7 13.1 %collective-permute-start.17 = (bf16[104,768]{1,0:T(8,128)(2,1)S(1)}, bf16[104,768]{1,0:T(8,128)(2,1)S(1)}, u32[]{:S(2)}, u32[]{:S(2)}) collective-permute-start(bf16[104,768]{1,0:T(8,128)(2,1)S(1)} %get-tuple-element.68), channel_id=1, source_target_pairs={{0,1},{1,2},{2,3},{3,0},{4,5},{5,6},{6,7},{7,4},{8,9},{9,10},{10,1... | collective-permute-start | bytes 479240 | tf_op jit(solution)/shard_map/ppermute | solution.py:269
  42.9 25.6 %collective-permute-start.12 = (bf16[208,768]{1,0:T(8,128)(2,1)S(1)}, bf16[208,768]{1,0:T(8,128)(2,1)S(1)}, u32[]{:S(2)}, u32[]{:S(2)}) collective-permute-start(bf16[208,768]{1,0:T(8,128)(2,1)S(1)} %get-tuple-element.63), channel_id=1, source_target_pairs={{0,1},{1,2},{2,3},{3,0},{4,5},{5,6},{6,7},{7,4},{8,9},{9,10},{10,1... | collective-permute-start | bytes 958472 | tf_op jit(solution)/shard_map/ppermute | solution.py:269
  44.8 27.3 %collective-permute-start.13 = (bf16[208,768]{1,0:T(8,128)(2,1)S(1)}, bf16[208,768]{1,0:T(8,128)(2,1)S(1)}, u32[]{:S(2)}, u32[]{:S(2)}) collective-permute-start(bf16[208,768]{1,0:T(8,128)(2,1)S(1)} %get-tuple-element.64), channel_id=1, source_target_pairs={{0,3},{1,0},{2,1},{3,2},{4,7},{5,4},{6,5},{7,6},{8,11},{9,8},{10,9... | collective-permute-start | bytes 958472 | tf_op jit(solution)/shard_map/ppermute | solution.py:269
  45.0 30.6 %collective-permute-start.14 = (bf16[208,768]{1,0:T(8,128)(2,1)S(1)}, bf16[208,768]{1,0:T(8,128)(2,1)S(1)}, u32[]{:S(2)}, u32[]{:S(2)}) collective-permute-start(bf16[208,768]{1,0:T(8,128)(2,1)S(1)} %get-tuple-element.65), channel_id=1, source_target_pairs={{0,2},{1,3},{2,0},{3,1},{4,6},{5,7},{6,4},{7,5},{8,10},{9,11},{10,... | collective-permute-start | bytes 958472 | tf_op jit(solution)/shard_map/ppermute | solution.py:269
  47.5 17.1 %collective-permute-start.18 = (bf16[104,768]{1,0:T(8,128)(2,1)S(1)}, bf16[104,768]{1,0:T(8,128)(2,1)S(1)}, u32[]{:S(2)}, u32[]{:S(2)}) collective-permute-start(bf16[104,768]{1,0:T(8,128)(2,1)S(1)} %get-tuple-element.69), channel_id=1, source_target_pairs={{0,3},{1,0},{2,1},{3,2},{4,7},{5,4},{6,5},{7,6},{8,11},{9,8},{10,9... | collective-permute-start | bytes 479240 | tf_op jit(solution)/shard_map/ppermute | solution.py:269
  48.9 19.0 %collective-permute-start.19 = (bf16[104,768]{1,0:T(8,128)(2,1)S(1)}, bf16[104,768]{1,0:T(8,128)(2,1)S(1)}, u32[]{:S(2)}, u32[]{:S(2)}) collective-permute-start(bf16[104,768]{1,0:T(8,128)(2,1)S(1)} %get-tuple-element.70), channel_id=1, source_target_pairs={{0,2},{1,3},{2,0},{3,1},{4,6},{5,7},{6,4},{7,5},{8,10},{9,11},{10,... | collective-permute-start | bytes 479240 | tf_op jit(solution)/shard_map/ppermute | solution.py:269
  64.7 12.9 %collective-permute-start.3 = (bf16[104,768]{1,0:T(8,128)(2,1)S(1)}, bf16[104,768]{1,0:T(8,128)(2,1)S(1)}, u32[]{:S(2)}, u32[]{:S(2)}) collective-permute-start(bf16[104,768]{1,0:T(8,128)(2,1)S(1)} %get-tuple-element.54), channel_id=1, source_target_pairs={{0,1},{1,2},{2,3},{3,0},{4,5},{5,6},{6,7},{7,4},{8,9},{9,10},{10,1... | collective-permute-start | bytes 479240 | tf_op jit(solution)/shard_map/ppermute | solution.py:269
  67.9 13.3 %collective-permute-start.4 = (bf16[104,768]{1,0:T(8,128)(2,1)S(1)}, bf16[104,768]{1,0:T(8,128)(2,1)S(1)}, u32[]{:S(2)}, u32[]{:S(2)}) collective-permute-start(bf16[104,768]{1,0:T(8,128)(2,1)S(1)} %get-tuple-element.55), channel_id=1, source_target_pairs={{0,3},{1,0},{2,1},{3,2},{4,7},{5,4},{6,5},{7,6},{8,11},{9,8},{10,9... | collective-permute-start | bytes 479240 | tf_op jit(solution)/shard_map/ppermute | solution.py:269
  68.5 12.8 %collective-permute-start.5 = (bf16[104,768]{1,0:T(8,128)(2,1)S(1)}, bf16[104,768]{1,0:T(8,128)(2,1)S(1)}, u32[]{:S(2)}, u32[]{:S(2)}) collective-permute-start(bf16[104,768]{1,0:T(8,128)(2,1)S(1)} %get-tuple-element.56), channel_id=1, source_target_pairs={{0,2},{1,3},{2,0},{3,1},{4,6},{5,7},{6,4},{7,5},{8,10},{9,11},{10,... | collective-permute-start | bytes 479240 | tf_op jit(solution)/shard_map/ppermute | solution.py:269
  72.1 9.9 %collective-permute-start.20 = (bf16[104,768]{1,0:T(8,128)(2,1)S(1)}, bf16[104,768]{1,0:T(8,128)(2,1)S(1)}, u32[]{:S(2)}, u32[]{:S(2)}) collective-permute-start(bf16[104,768]{1,0:T(8,128)(2,1)S(1)} %shard_map.118), channel_id=1, source_target_pairs={{0,64},{32,96},{64,0},{96,32},{1,65},{33,97},{65,1},{97,33},{2,66}... | collective-permute-start | bytes 479240 | tf_op jit(solution)/shard_map/ppermute | solution.py:269
  81.2 39.0 %collective-permute-start.24 = (bf16[1536,256]{1,0:T(8,128)(2,1)}, bf16[1536,256]{1,0:T(8,128)(2,1)}, u32[]{:S(2)}, u32[]{:S(2)}) collective-permute-start(bf16[1536,256]{1,0:T(8,128)(2,1)} %get-tuple-element.77), channel_id=1, source_target_pairs={{0,128},{128,0},{1,129},{129,1},{2,130},{130,2},{3,131},{131,3},{4... | collective-permute-start | bytes 2359304 | tf_op jit(solution)/shard_map/ppermute | solution.py:269
  85.7 18.6 %all-to-all-start = ((bf16[8,16,896]{2,1,0:T(8,128)(2,1)}), bf16[8,16,896]{2,1,0:T(8,128)(2,1)S(1)}, u32[]{:S(2)}, u32[]{:S(2)}) async-start(bf16[8,16,896]{2,1,0:T(8,128)(2,1)} %shard_map.119), calls=%async_computation | async-start | bytes 458752 | tf_op jit(solution)/shard_map/all_to_all | solution.py:273
  94.2 26.0 %collective-permute-start.25 = (bf16[1536,256]{1,0:T(8,128)(2,1)}, bf16[1536,256]{1,0:T(8,128)(2,1)}, u32[]{:S(2)}, u32[]{:S(2)}) collective-permute-start(bf16[1536,256]{1,0:T(8,128)(2,1)} %copy-done.9), channel_id=1, source_target_pairs={{0,128},{128,0},{1,129},{129,1},{2,130},{130,2},{3,131},{131,3},{4... | collective-permute-start | bytes 2359304 | tf_op jit(solution)/shard_map/ppermute | solution.py:269
  94.2 26.0 %collective-permute-start.26 = (bf16[1536,256]{1,0:T(8,128)(2,1)}, bf16[1536,256]{1,0:T(8,128)(2,1)}, u32[]{:S(2)}, u32[]{:S(2)}) collective-permute-start(bf16[1536,256]{1,0:T(8,128)(2,1)} %copy-done.8), channel_id=1, source_target_pairs={{0,128},{128,0},{1,129},{129,1},{2,130},{130,2},{3,131},{131,3},{4... | collective-permute-start | bytes 2359304 | tf_op jit(solution)/shard_map/ppermute | solution.py:269
  117.5 9.6 %collective-permute-start.23 = (bf16[128,768]{1,0:T(8,128)(2,1)S(1)}, bf16[128,768]{1,0:T(8,128)(2,1)S(1)}, u32[]{:S(2)}, u32[]{:S(2)}) collective-permute-start(bf16[128,768]{1,0:T(8,128)(2,1)S(1)} %bitcast.11), channel_id=1, source_target_pairs={{0,2},{1,3},{2,0},{3,1},{4,6},{5,7},{6,4},{7,5},{8,10},{9,11},{10,... | collective-permute-start | bytes 589832 | tf_op jit(solution)/shard_map/ppermute | solution.py:269
  117.6 9.5 %collective-permute-start.22 = (bf16[128,768]{1,0:T(8,128)(2,1)S(1)}, bf16[128,768]{1,0:T(8,128)(2,1)S(1)}, u32[]{:S(2)}, u32[]{:S(2)}) collective-permute-start(bf16[128,768]{1,0:T(8,128)(2,1)S(1)} %bitcast.12), channel_id=1, source_target_pairs={{0,3},{1,0},{2,1},{3,2},{4,7},{5,4},{6,5},{7,6},{8,11},{9,8},{10,9... | collective-permute-start | bytes 589832 | tf_op jit(solution)/shard_map/ppermute | solution.py:269
  120.2 6.9 %collective-permute-start.21 = (bf16[128,768]{1,0:T(8,128)(2,1)S(1)}, bf16[128,768]{1,0:T(8,128)(2,1)S(1)}, u32[]{:S(2)}, u32[]{:S(2)}) collective-permute-start(bf16[128,768]{1,0:T(8,128)(2,1)S(1)} %bitcast.13), channel_id=1, source_target_pairs={{0,1},{1,2},{2,3},{3,0},{4,5},{5,6},{6,7},{7,4},{8,9},{9,10},{10,1... | collective-permute-start | bytes 589832 | tf_op jit(solution)/shard_map/ppermute | solution.py:269
  (14 other events, 184.9 us)

commit v6 on v5

--- a/solution.py
+++ b/solution.py
@@ -110,6 +110,24 @@
         out[:, 2 * width :] = facts_of(pick, hits[j], gw_ref)
 
 
+def sides_kernel(pos, ids_ref, gw_ref, tok_ref, cot_ref, *outs):
+    member, rank, hits = routing(pos, ids_ref, (1, -1))
+    width = tok_ref.shape[1]
+    half, part = width // 2, width // 4
+    at = pl.multiple_of(half + lax.rem(pos[2], 2) * part, LANES)
+    for j in range(2):
+        out, piece = outs[j], outs[2 + j]
+        pick = picks(rank, member, j, out.shape[0], 0)
+        piece[...] = jnp.dot(
+            pick, cot_ref[:, pl.ds(at, part)], preferred_element_type=F32
+        ).astype(BF)
+        out[:, :width] = jnp.dot(pick, tok_ref[...], preferred_element_type=F32).astype(BF)
+        out[:, width : width + half] = jnp.dot(
+            pick, cot_ref[:, :half], preferred_element_type=F32
+        ).astype(BF)
+        out[:, width + half :] = facts_of(pick, hits[j], gw_ref)
+
+
 def here_kernel(pos, ids_ref, gw_ref, tok_ref, cot_ref, out, picks_ref):
     near_kernel((0,), pos, ids_ref, gw_ref, tok_ref, cot_ref, out)
     member, rank, _ = routing(pos, ids_ref, OFFSETS)
@@ -118,7 +136,7 @@
 
 
 def expert_kernel(kind, pos, *refs):
-    count = {"here": 1, "far": 4, "sides": 2}[kind]
+    count = {"here": 1, "far": 4, "sides": 6}[kind]
     pieces, refs = refs[:count], refs[count:]
     wg_own, wg_sib, wu_own, wu_sib, wd_own, wd_sib = (ref.at[0] for ref in refs[:6])
     sends, aux_ref, whole = refs[6:10], refs[10], refs[-1]
@@ -134,6 +152,18 @@
             column = pl.multiple_of(lax.div(source, 2) * width, LANES)
             msgs[0][pl.ds(at, rows), pl.ds(column, width)] = piece[:, :width]
             msgs[0][pl.ds(at, rows), 2 * width :] = piece[:, width:]
+    elif kind == "sides":
+        msgs = refs[11:13]
+        part = half // 2
+        first = lax.rem(pos[2], 2)
+        ours = pl.multiple_of(width + half + first * part, LANES)
+        theirs = pl.multiple_of(width + half + (1 - first) * part, LANES)
+        for j, msg in enumerate(msgs):
+            main = pieces[j]
+            msg[:, : width + half] = main[:, : width + half]
+            msg[:, 2 * width :] = main[:, width + half :]
+            msg[:, pl.ds(ours, part)] = pieces[2 + j][...]
+            msg[:, pl.ds(theirs, part)] = pieces[4 + j][...]
     else:
         msgs = pieces
     own = pl.multiple_of(pos[0] * half, LANES)
@@ -269,6 +299,11 @@
     return lax.ppermute(value, axis, [(i, (i + offset) % size) for i in range(size)])
 
 
+def swap(value):
+    size = lax.axis_size("z")
+    return lax.ppermute(value, "z", [(i, i ^ 1) for i in range(size)])
+
+
 def exchange(value, axis):
     return lax.all_to_all(value, axis, split_axis=0, concat_axis=0, tiled=True)
 
@@ -303,9 +338,10 @@
         ],
     )
     given = (*given, tokens, cotangent)
-    plus, minus = call(
-        functools.partial(near_kernel, (1, -1)),
-        [array(slots, long)] * 2,
+    part = width // 4
+    plus, minus, plus_part, minus_part = call(
+        sides_kernel,
+        [array(slots, long - 2 * part)] * 2 + [array(slots, part)] * 2,
         (pos, *given),
         free=(0, 1),
     )
@@ -316,7 +352,10 @@
     weights = []
     for own in (w_gate, w_up, w_down):
         weights += [own, shift(after(own, plus), "dp", 1)]
+    plus_part = shift(plus_part, "expert", 1)
+    minus_part = shift(minus_part, "expert", -1)
     plus, minus = shift(plus, "expert", 1), shift(minus, "expert", -1)
+    sides_in = [plus, minus, plus_part, minus_part, swap(plus_part), swap(minus_part)]
     far = shift(far, "expert", 2)
     far = [far] + [shift(far, "y", offset) for offset in (1, -1, 2)]
 
@@ -326,7 +365,7 @@
             functools.partial(expert_kernel, kind),
             [array(count * (slots + 8), block)] * 4
             + [array(count * slots, 3 * units)]
-            + [array(slots, long)] * (kind == "far"),
+            + [array(slots, long)] * {"here": 0, "far": 1, "sides": 2}[kind],
             (pos, *msgs, *weights),
             scratch=[pltpu.VMEM((4, count * slots, block), BF)],
         )
@@ -338,7 +377,7 @@
 
     local = expert(pos, [here], "here")
     remote = expert(after(pos, local[0]), far, "far")
-    sides = expert(after(pos, remote[0]), [plus, minus], "sides")
+    sides = expert(after(pos, remote[0]), sides_in, "sides")
     (from_here,) = scatter(local[:4], "here")
     (from_far,) = scatter(remote[:4], "far")
     from_plus, from_minus = scatter(sides[:4], "sides")
@@ -360,7 +399,7 @@
         [plain(tok_count, width)],
         (pos, slab, *[shift(slab, "y", offset) for offset in (1, -1, 2)]),
     )
-    used = [here, remote[5], plus, minus, local[4], remote[4], sides[4]]
+    used = [here, remote[5], sides[5], sides[6], local[4], remote[4], sides[4]]
     half = width // 2
     away = call(
         functools.partial(grad_kernel, True), [array(half, units)] * 3, (pos, *used),

time: 131 us -> 143 us (1.092)
  waiting for transfers between devices: 43.5 us -> 50.3 us
  starting transfers between devices: 41.9 us -> 46.8 us
    ppermute x27 -> x29, waiting for transfers between devices: 33.9 us -> 40.7 us  [shift(): lax.ppermute(value, axis, [(i, (i + offset) % size) for i in range(size)])]
    ppermute x27 -> x29, starting transfers between devices: 33.4 us -> 36.2 us  [shift(): lax.ppermute(value, axis, [(i, (i + offset) % size) for i in range(size)])]
    ppermute x0 -> x2, starting transfers between devices: none -> 2.2 us  [swap(): return lax.ppermute(value, 'z', [(i, i ^ 1) for i in range(size)])]
  transfers between devices with their start and end apart: 28 -> 32, of which waited for: 9 -> 10; matrix products, arithmetic and copies ran while one was open for 0% -> 0% of each run, Pallas kernels for 19% -> 17%
where the time goes in v6:
time: 143 us; the launch traced here: 140 us
  waiting for transfers between devices  50.3 us (35%)
  starting transfers between devices  46.8 us (33%)
  Pallas kernels  27.6 us (19%)
  blocking collectives  12.2 us (9%)
  local copies, waits for them, and re-layouts  2.58 us (2%)
    ppermute x29, waiting for transfers between devices, shift(): lax.ppermute(value, axis, [(i, (i + offset) % size) for i in range(size)])  40.7 us
    ppermute x29, starting transfers between devices, shift(): lax.ppermute(value, axis, [(i, (i + offset) % size) for i in range(size)])  36.2 us
    pallas_call x14, Pallas kernels, call(): pl.pallas_call(kernel, out_shape=outs, in_specs=specs, out_specs=[spec] *...  27.6 us
    all_to_all x1, blocking collectives, exchange(): return lax.all_to_all(value, axis, split_axis=0, concat_axis=0, tiled=True)  12.2 us
    all_to_all x1, waiting for transfers between devices, exchange(): return lax.all_to_all(value, axis, split_axis=0, concat_axis=0, tiled=True)  9.62 us
    all_to_all x1, starting transfers between devices, exchange(): return lax.all_to_all(value, axis, split_axis=0, concat_axis=0, tiled=True)  8.46 us
  transfers between devices with their start and end apart: 32, of which 10 were waited for; matrix products, arithmetic and copies ran while one was open for 0% of the time, Pallas kernels for 17%

profile of v6, /device:TPU:8, one launch (start us, length us, event | category | flops | bytes accessed | tf_op | source)
XLA Modules:
  0.0 140.5 jit_solution(13340501437750121647)
XLA Ops:
  0.7 2.2 %shard_map.110 = (bf16[48,3200]{1,0:T(8,128)(2,1)S(1)}, bf16[128,3072]{1,0:T(8,128)(2,1)S(1)}, bf16[128,3072]{1,0:T(8,128)(2,1)S(1)}) custom-call(s32[4]{0:T(128)S(1)} %pad_add_fusion.pos, s32[2,128]{1,0:T(2,128)} %bitcast.15, bf16[2,128]{1,0:T(2,128)(2,1)} %bitcast.19, bf16[128,3072]{1,0:T(8,128)(2,1)} %tok_ref.1, bf16[128,3072]{1,0:T(8,128)(2,1)} %cot_ref.1), custom_call_target="tpu_custom_call" | custom-call | tf_op jit(solution)/shard_map/pallas_call | solution.py:38
  2.9 3.1 %collective-permute-start.6 = (bf16[48,3200]{1,0:T(8,128)(2,1)S(1)}, bf16[48,3200]{1,0:T(8,128)(2,1)S(1)}, u32[]{:S(2)}, u32[]{:S(2)}) collective-permute-start(bf16[48,3200]{1,0:T(8,128)(2,1)S(1)} %get-tuple-element.62), channel_id=1, source_target_pairs={{0,64},{32,96},{64,0},{96,32},{1,65},{33,97},{65,1},{97,33},{2,66}... | collective-permute-start | bytes 921608 | tf_op jit(solution)/shard_map/ppermute | solution.py:299
  6.0 7.5 %collective-permute-done.6.refs_0_ = bf16[48,3200]{1,0:T(8,128)(2,1)S(1)} collective-permute-done((bf16[48,3200]{1,0:T(8,128)(2,1)S(1)}, bf16[48,3200]{1,0:T(8,128)(2,1)S(1)}, u32[]{:S(2)}, u32[]{:S(2)}) %collective-permute-start.6) | collective-permute-done | bytes 307232 | tf_op jit(solution)/shard_map/ppermute | solution.py:299
  13.5 2.5 %collective-permute-start.9 = (bf16[48,3200]{1,0:T(8,128)(2,1)S(1)}, bf16[48,3200]{1,0:T(8,128)(2,1)S(1)}, u32[]{:S(2)}, u32[]{:S(2)}) collective-permute-start(bf16[48,3200]{1,0:T(8,128)(2,1)S(1)} %collective-permute-done.6.refs_0_), channel_id=1, source_target_pairs={{0,2},{1,3},{2,0},{3,1},{4,6},{5,7},{6,4},{7,5},{8,10},{9,11},{10,... | collective-permute-start | bytes 921608 | tf_op jit(solution)/shard_map/ppermute | solution.py:299
  22.3 4.1 %collective-permute-done.12.refs_2_ = bf16[96,768]{1,0:T(8,128)(2,1)S(1)} collective-permute-done((bf16[96,768]{1,0:T(8,128)(2,1)S(1)}, bf16[96,768]{1,0:T(8,128)(2,1)S(1)}, u32[]{:S(2)}, u32[]{:S(2)}) %collective-permute-start.12) | collective-permute-done | bytes 147488 | tf_op jit(solution)/shard_map/ppermute | solution.py:299
  27.0 2.5 %collective-permute-start.11 = (bf16[96,4736]{1,0:T(8,128)(2,1)S(1)}, bf16[96,4736]{1,0:T(8,128)(2,1)S(1)}, u32[]{:S(2)}, u32[]{:S(2)}) collective-permute-start(bf16[96,4736]{1,0:T(8,128)(2,1)S(1)} %get-tuple-element.65), channel_id=1, source_target_pairs={{0,96},{32,0},{64,32},{96,64},{1,97},{33,1},{65,33},{97,65},{2,98}... | collective-permute-start | bytes 2727944 | tf_op jit(solution)/shard_map/ppermute | solution.py:299
  31.8 1.9 %collective-permute-start.14 = (bf16[96,768]{1,0:T(8,128)(2,1)S(1)}, bf16[96,768]{1,0:T(8,128)(2,1)S(1)}, u32[]{:S(2)}, u32[]{:S(2)}) collective-permute-start(bf16[96,768]{1,0:T(8,128)(2,1)S(1)} %collective-permute-done.12.refs_2_), channel_id=1, source_target_pairs={{0,4},{4,0},{8,12},{12,8},{16,20},{20,16},{24,28},{28,24},{1,5},{5... | collective-permute-start | bytes 442376 | tf_op jit(solution)/shard_map/ppermute | solution.py:304
  35.3 2.9 %shard_map.113 = (bf16[104,768]{1,0:T(8,128)(2,1)S(1)}, bf16[104,768]{1,0:T(8,128)(2,1)S(1)}, bf16[104,768]{1,0:T(8,128)(2,1)S(1)}, bf16[104,768]{1,0:T(8,128)(2,1)S(1)}, bf16[96,768]{1,0:T(8,128)(2,1)S(1)}) custom-call(s32[4]{0:T(128)S(1)} %pad_add_fusion.pos, bf16[96,6272]{1,0:T(8,128)(2,1)S(1)} %get-tuple-element.53.refs_0_.here_ref, ...), custom_call_target="tpu_custom_call" | custom-call | tf_op jit(solution)/shard_map/pallas_call | solution.py:38
  38.2 1.9 %collective-permute-done.7.refs_1_ = bf16[48,3200]{1,0:T(8,128)(2,1)S(1)} collective-permute-done((bf16[48,3200]{1,0:T(8,128)(2,1)S(1)}, bf16[48,3200]{1,0:T(8,128)(2,1)S(1)}, u32[]{:S(2)}, u32[]{:S(2)}) %collective-permute-start.7) | collective-permute-done | bytes 307232 | tf_op jit(solution)/shard_map/ppermute | solution.py:299
  40.1 3.0 %shard_map.115 = (bf16[104,768]{1,0:T(8,128)(2,1)S(1)}, bf16[104,768]{1,0:T(8,128)(2,1)S(1)}, bf16[104,768]{1,0:T(8,128)(2,1)S(1)}, bf16[104,768]{1,0:T(8,128)(2...) custom-call(s32[4]{0:T(128)S(1)} %pad_add_fusion.pos, ...), custom_call_target="tpu_custom_call" | custom-call | tf_op jit(solution)/shard_map/pallas_call | solution.py:38
  43.7 5.8 %collective-permute-done.11.refs_1_ = bf16[96,4736]{1,0:T(8,128)(2,1)S(1)} collective-permute-done((bf16[96,4736]{1,0:T(8,128)(2,1)S(1)}, bf16[96,4736]{1,0:T(8,128)(2,1)S(1)}, u32[]{:S(2)}, u32[]{:S(2)}) %collective-permute-start.11) | collective-permute-done | bytes 909344 | tf_op jit(solution)/shard_map/ppermute | solution.py:299
  49.5 3.5 %collective-permute-done.10.refs_0_ = bf16[96,4736]{1,0:T(8,128)(2,1)S(1)} collective-permute-done((bf16[96,4736]{1,0:T(8,128)(2,1)S(1)}, bf16[96,4736]{1,0:T(8,128)(2,1)S(1)}, u32[]{:S(2)}, u32[]{:S(2)}) %collective-permute-start.10) | collective-permute-done | bytes 909344 | tf_op jit(solution)/shard_map/ppermute | solution.py:299
  53.0 3.6 %shard_map.116 = (bf16[208,768]{1,0:T(8,128)(2,1)S(1)}, bf16[208,768]{1,0:T(8,128)(2,1)S(1)}, bf16[208,768]{1,0:T(8,128)(2,1)S(1)}, bf16[208,768]{1,0:T(8,128)(2...) custom-call(s32[4]{0:T(128)S(1)} %pad_add_fusion.pos, ...), custom_call_target="tpu_custom_call" | custom-call | tf_op jit(solution)/shard_map/pallas_call | solution.py:38
  58.8 2.5 %collective-permute-start.18 = (bf16[208,768]{1,0:T(8,128)(2,1)S(1)}, bf16[208,768]{1,0:T(8,128)(2,1)S(1)}, u32[]{:S(2)}, u32[]{:S(2)}) collective-permute-start(bf16[208,768]{1,0:T(8,128)(2,1)S(1)} %get-tuple-element.71), channel_id=1, source_target_pairs={{0,2},{1,3},{2,0},{3,1},{4,6},{5,7},{6,4},{7,5},{8,10},{9,11},{10,... | collective-permute-start | bytes 958472 | tf_op jit(solution)/shard_map/ppermute | solution.py:299
  63.6 13.9 %collective-permute-done.22.c_ref = bf16[104,768]{1,0:T(8,128)(2,1)S(1)} collective-permute-done((bf16[104,768]{1,0:T(8,128)(2,1)S(1)}, bf16[104,768]{1,0:T(8,128)(2,1)S(1)}, u32[]{:S(2)}, u32[]{:S(2)}) %collective-permute-start.22) | collective-permute-done | bytes 159776 | tf_op jit(solution)/shard_map/ppermute | solution.py:299
  77.5 2.6 %collective-permute-start.3 = (bf16[104,768]{1,0:T(8,128)(2,1)S(1)}, bf16[104,768]{1,0:T(8,128)(2,1)S(1)}, u32[]{:S(2)}, u32[]{:S(2)}) collective-permute-start(bf16[104,768]{1,0:T(8,128)(2,1)S(1)} %get-tuple-element.58), channel_id=1, source_target_pairs={{0,1},{1,2},{2,3},{3,0},{4,5},{5,6},{6,7},{7,4},{8,9},{9,10},{10,1... | collective-permute-start | bytes 479240 | tf_op jit(solution)/shard_map/ppermute | solution.py:299
  82.4 3.2 %collective-permute-start.5 = (bf16[104,768]{1,0:T(8,128)(2,1)S(1)}, bf16[104,768]{1,0:T(8,128)(2,1)S(1)}, u32[]{:S(2)}, u32[]{:S(2)}) collective-permute-start(bf16[104,768]{1,0:T(8,128)(2,1)S(1)} %get-tuple-element.60), channel_id=1, source_target_pairs={{0,2},{1,3},{2,0},{3,1},{4,6},{5,7},{6,4},{7,5},{8,10},{9,11},{10,... | collective-permute-start | bytes 479240 | tf_op jit(solution)/shard_map/ppermute | solution.py:299
  90.3 2.7 %shard_map.122 = (bf16[1536,256]{1,0:T(8,128)(2,1)}, bf16[1536,256]{1,0:T(8,128)(2,1)S(1)}, bf16[1536,256]{1,0:T(8,128)(2,1)S(1)}) custom-call(s32[4]{0:T(128)S(1)} %pad_add_fusion.pos, bf16[96,6272]{1,0:T(8,128)(2,1)S(1)} %get-tuple-element.53.refs_0_.here_ref, bf16[96,6272]{1,0:T(8,128)(2,1)S(1)} %get-tuple-element.79.far_ref, ...), custom_call_target="tpu_custom_call" | custom-call | tf_op jit(solution)/shard_map/pallas_call | solution.py:38
  93.8 2.1 %collective-permute-done.20.refs_2_ = bf16[104,768]{1,0:T(8,128)(2,1)S(1)} collective-permute-done((bf16[104,768]{1,0:T(8,128)(2,1)S(1)}, bf16[104,768]{1,0:T(8,128)(2,1)S(1)}, u32[]{:S(2)}, u32[]{:S(2)}) %collective-permute-start.20) | collective-permute-done | bytes 159776 | tf_op jit(solution)/shard_map/ppermute | solution.py:299
  97.5 8.5 %all-to-all-start = ((bf16[8,16,896]{2,1,0:T(8,128)(2,1)}), bf16[8,16,896]{2,1,0:T(8,128)(2,1)S(1)}, u32[]{:S(2)}, u32[]{:S(2)}) async-start(bf16[8,16,896]{2,1,0:T(8,128)(2,1)} %shard_map.119), calls=%async_computation | async-start | bytes 458752 | tf_op jit(solution)/shard_map/all_to_all | solution.py:308
  106.5 9.6 %all-to-all-done.got_ref = bf16[8,16,896]{2,1,0:T(8,128)(2,1)S(1)} async-done(((bf16[8,16,896]{2,1,0:T(8,128)(2,1)}), bf16[8,16,896]{2,1,0:T(8,128)(2,1)S(1)}, u32[]{:S(2)}, u32[]{:S(2)}) %all-to-all-start) | async-done | bytes 229408 | tf_op jit(solution)/shard_map/all_to_all | solution.py:308
  117.2 12.2 %all_to_all.10 = bf16[8,16,768]{2,1,0:T(8,128)(2,1)S(1)} all-to-all(bf16[8,16,768]{2,1,0:T(8,128)(2,1)S(1)} %get-tuple-element.77), channel_id=1, replica_groups=mesh['dp'=2,'expert'=4,'z'=8,'y'=4] {'z'}, dimensions={0} | all-to-all | bytes 393216 | tf_op jit(solution)/shard_map/all_to_all | solution.py:308
  129.7 2.3 %collective-permute-start.26 = (bf16[128,768]{1,0:T(8,128)(2,1)S(1)}, bf16[128,768]{1,0:T(8,128)(2,1)S(1)}, u32[]{:S(2)}, u32[]{:S(2)}) collective-permute-start(bf16[128,768]{1,0:T(8,128)(2,1)S(1)} %bitcast.12), channel_id=1, source_target_pairs={{0,3},{1,0},{2,1},{3,2},{4,7},{5,4},{6,5},{7,6},{8,11},{9,8},{10,9... | collective-permute-start | bytes 589832 | tf_op jit(solution)/shard_map/ppermute | solution.py:299
  134.6 4.3 %shard_map.123 = (bf16[1536,256]{1,0:T(8,128)(2,1)}, bf16[1536,256]{1,0:T(8,128)(2,1)}, bf16[1536,256]{1,0:T(8,128)(2,1)}) custom-call(s32[4]{0:T(128)S(1)} %pad_add_fusion.pos, bf16[96,6272]{1,0:T(8,128)(2,1)S(1)} %get-tuple-element.53.refs_0_.here_ref, bf16[96,6272]{1,0:T(8,128)(2,1)S(1)} %get-tuple-element.79.far_ref, bf16[96,6272]{1,0:T(8,128)(2,1)S(1)} %copy-done.4, ...), custom_call_target="tpu_custom_call" | custom-call | tf_op jit(solution)/shard_map/pallas_call | solution.py:38
  (76 shorter events, 31.1 us)
Async XLA Ops:
  2.9 10.6 %collective-permute-start.6 = (bf16[48,3200]{1,0:T(8,128)(2,1)S(1)}, bf16[48,3200]{1,0:T(8,128)(2,1)S(1)}, u32[]{:S(2)}, u32[]{:S(2)}) collective-permute-start(bf16[48,3200]{1,0:T(8,128)(2,1)S(1)} %get-tuple-element.62), channel_id=1, source_target_pairs={{0,64},{32,96},{64,0},{96,32},{1,65},{33,97},{65,1},{97,33},{2,66}... | collective-permute-start | bytes 921608 | tf_op jit(solution)/shard_map/ppermute | solution.py:299
  13.5 13.5 %collective-permute-start.9 = (bf16[48,3200]{1,0:T(8,128)(2,1)S(1)}, bf16[48,3200]{1,0:T(8,128)(2,1)S(1)}, u32[]{:S(2)}, u32[]{:S(2)}) collective-permute-start(bf16[48,3200]{1,0:T(8,128)(2,1)S(1)} %collective-permute-done.6.refs_0_), channel_id=1, source_target_pairs={{0,2},{1,3},{2,0},{3,1},{4,6},{5,7},{6,4},{7,5},{8,10},{9,11},{10,... | collective-permute-start | bytes 921608 | tf_op jit(solution)/shard_map/ppermute | solution.py:299
  16.0 13.7 %collective-permute-start.8 = (bf16[48,3200]{1,0:T(8,128)(2,1)S(1)}, bf16[48,3200]{1,0:T(8,128)(2,1)S(1)}, u32[]{:S(2)}, u32[]{:S(2)}) collective-permute-start(bf16[48,3200]{1,0:T(8,128)(2,1)S(1)} %collective-permute-done.6.refs_0_), channel_id=1, source_target_pairs={{0,3},{1,0},{2,1},{3,2},{4,7},{5,4},{6,5},{7,6},{8,11},{9,8},{10,9... | collective-permute-start | bytes 921608 | tf_op jit(solution)/shard_map/ppermute | solution.py:299
  18.9 12.3 %collective-permute-start = (bf16[1,1536,256]{2,1,0:T(8,128)(2,1)S(1)}, bf16[1,1536,256]{2,1,0:T(8,128)(2,1)S(1)}, u32[]{:S(2)}, u32[]{:S(2)}) collective-permute-start(bf16[1,1536,256]{2,1,0:T(8,128)(2,1)S(1)} %copy-done), channel_id=1, source_target_pairs={{0,128},{128,0},{1,129},{129,1},{2,130},{130,2},{3,131},{131,3},{4... | collective-permute-start | bytes 2359304 | tf_op jit(solution)/shard_map/ppermute | solution.py:299
  27.0 22.5 %collective-permute-start.11 = (bf16[96,4736]{1,0:T(8,128)(2,1)S(1)}, bf16[96,4736]{1,0:T(8,128)(2,1)S(1)}, u32[]{:S(2)}, u32[]{:S(2)}) collective-permute-start(bf16[96,4736]{1,0:T(8,128)(2,1)S(1)} %get-tuple-element.65), channel_id=1, source_target_pairs={{0,96},{32,0},{64,32},{96,64},{1,97},{33,1},{65,33},{97,65},{2,98}... | collective-permute-start | bytes 2727944 | tf_op jit(solution)/shard_map/ppermute | solution.py:299
  29.7 23.3 %collective-permute-start.10 = (bf16[96,4736]{1,0:T(8,128)(2,1)S(1)}, bf16[96,4736]{1,0:T(8,128)(2,1)S(1)}, u32[]{:S(2)}, u32[]{:S(2)}) collective-permute-start(bf16[96,4736]{1,0:T(8,128)(2,1)S(1)} %get-tuple-element.50), channel_id=1, source_target_pairs={{0,32},{32,64},{64,96},{96,0},{1,33},{33,65},{65,97},{97,1},{2,34}... | collective-permute-start | bytes 2727944 | tf_op jit(solution)/shard_map/ppermute | solution.py:299
  31.2 8.9 %collective-permute-start.7 = (bf16[48,3200]{1,0:T(8,128)(2,1)S(1)}, bf16[48,3200]{1,0:T(8,128)(2,1)S(1)}, u32[]{:S(2)}, u32[]{:S(2)}) collective-permute-start(bf16[48,3200]{1,0:T(8,128)(2,1)S(1)} %collective-permute-done.6.refs_0_), channel_id=1, source_target_pairs={{0,1},{1,2},{2,3},{3,0},{4,5},{5,6},{6,7},{7,4},{8,9},{9,10},{10,1... | collective-permute-start | bytes 921608 | tf_op jit(solution)/shard_map/ppermute | solution.py:299
  31.8 11.9 %collective-permute-start.14 = (bf16[96,768]{1,0:T(8,128)(2,1)S(1)}, bf16[96,768]{1,0:T(8,128)(2,1)S(1)}, u32[]{:S(2)}, u32[]{:S(2)}) collective-permute-start(bf16[96,768]{1,0:T(8,128)(2,1)S(1)} %collective-permute-done.12.refs_2_), channel_id=1, source_target_pairs={{0,4},{4,0},{8,12},{12,8},{16,20},{20,16},{24,28},{28,24},{1,5},{5... | collective-permute-start | bytes 442376 | tf_op jit(solution)/shard_map/ppermute | solution.py:304
  33.8 10.0 %collective-permute-start.15 = (bf16[96,768]{1,0:T(8,128)(2,1)S(1)}, bf16[96,768]{1,0:T(8,128)(2,1)S(1)}, u32[]{:S(2)}, u32[]{:S(2)}) collective-permute-start(bf16[96,768]{1,0:T(8,128)(2,1)S(1)} %collective-permute-done.13.refs_3_), channel_id=1, source_target_pairs={{0,4},{4,0},{8,12},{12,8},{16,20},{20,16},{24,28},{28,24},{1,5},{5... | collective-permute-start | bytes 442376 | tf_op jit(solution)/shard_map/ppermute | solution.py:304
  43.1 18.8 %collective-permute-start.21 = (bf16[104,768]{1,0:T(8,128)(2,1)S(1)}, bf16[104,768]{1,0:T(8,128)(2,1)S(1)}, u32[]{:S(2)}, u32[]{:S(2)}) collective-permute-start(bf16[104,768]{1,0:T(8,128)(2,1)S(1)} %get-tuple-element.74), channel_id=1, source_target_pairs={{0,1},{1,2},{2,3},{3,0},{4,5},{5,6},{6,7},{7,4},{8,9},{9,10},{10,1... | collective-permute-start | bytes 479240 | tf_op jit(solution)/shard_map/ppermute | solution.py:299
  56.6 25.7 %collective-permute-start.16 = (bf16[208,768]{1,0:T(8,128)(2,1)S(1)}, bf16[208,768]{1,0:T(8,128)(2,1)S(1)}, u32[]{:S(2)}, u32[]{:S(2)}) collective-permute-start(bf16[208,768]{1,0:T(8,128)(2,1)S(1)} %get-tuple-element.69), channel_id=1, source_target_pairs={{0,1},{1,2},{2,3},{3,0},{4,5},{5,6},{6,7},{7,4},{8,9},{9,10},{10,1... | collective-permute-start | bytes 958472 | tf_op jit(solution)/shard_map/ppermute | solution.py:299
  57.3 28.3 %collective-permute-start.17 = (bf16[208,768]{1,0:T(8,128)(2,1)S(1)}, bf16[208,768]{1,0:T(8,128)(2,1)S(1)}, u32[]{:S(2)}, u32[]{:S(2)}) collective-permute-start(bf16[208,768]{1,0:T(8,128)(2,1)S(1)} %get-tuple-element.70), channel_id=1, source_target_pairs={{0,3},{1,0},{2,1},{3,2},{4,7},{5,4},{6,5},{7,6},{8,11},{9,8},{10,9... | collective-permute-start | bytes 958472 | tf_op jit(solution)/shard_map/ppermute | solution.py:299
  58.8 28.7 %collective-permute-start.18 = (bf16[208,768]{1,0:T(8,128)(2,1)S(1)}, bf16[208,768]{1,0:T(8,128)(2,1)S(1)}, u32[]{:S(2)}, u32[]{:S(2)}) collective-permute-start(bf16[208,768]{1,0:T(8,128)(2,1)S(1)} %get-tuple-element.71), channel_id=1, source_target_pairs={{0,2},{1,3},{2,0},{3,1},{4,6},{5,7},{6,4},{7,5},{8,10},{9,11},{10,... | collective-permute-start | bytes 958472 | tf_op jit(solution)/shard_map/ppermute | solution.py:299
  61.3 16.2 %collective-permute-start.22 = (bf16[104,768]{1,0:T(8,128)(2,1)S(1)}, bf16[104,768]{1,0:T(8,128)(2,1)S(1)}, u32[]{:S(2)}, u32[]{:S(2)}) collective-permute-start(bf16[104,768]{1,0:T(8,128)(2,1)S(1)} %get-tuple-element.75), channel_id=1, source_target_pairs={{0,3},{1,0},{2,1},{3,2},{4,7},{5,4},{6,5},{7,6},{8,11},{9,8},{10,9... | collective-permute-start | bytes 479240 | tf_op jit(solution)/shard_map/ppermute | solution.py:299
  61.9 19.8 %collective-permute-start.23 = (bf16[104,768]{1,0:T(8,128)(2,1)S(1)}, bf16[104,768]{1,0:T(8,128)(2,1)S(1)}, u32[]{:S(2)}, u32[]{:S(2)}) collective-permute-start(bf16[104,768]{1,0:T(8,128)(2,1)S(1)} %get-tuple-element.76), channel_id=1, source_target_pairs={{0,2},{1,3},{2,0},{3,1},{4,6},{5,7},{6,4},{7,5},{8,10},{9,11},{10,... | collective-permute-start | bytes 479240 | tf_op jit(solution)/shard_map/ppermute | solution.py:299
  77.5 11.8 %collective-permute-start.3 = (bf16[104,768]{1,0:T(8,128)(2,1)S(1)}, bf16[104,768]{1,0:T(8,128)(2,1)S(1)}, u32[]{:S(2)}, u32[]{:S(2)}) collective-permute-start(bf16[104,768]{1,0:T(8,128)(2,1)S(1)} %get-tuple-element.58), channel_id=1, source_target_pairs={{0,1},{1,2},{2,3},{3,0},{4,5},{5,6},{6,7},{7,4},{8,9},{9,10},{10,1... | collective-permute-start | bytes 479240 | tf_op jit(solution)/shard_map/ppermute | solution.py:299
  81.7 11.3 %collective-permute-start.4 = (bf16[104,768]{1,0:T(8,128)(2,1)S(1)}, bf16[104,768]{1,0:T(8,128)(2,1)S(1)}, u32[]{:S(2)}, u32[]{:S(2)}) collective-permute-start(bf16[104,768]{1,0:T(8,128)(2,1)S(1)} %get-tuple-element.59), channel_id=1, source_target_pairs={{0,3},{1,0},{2,1},{3,2},{4,7},{5,4},{6,5},{7,6},{8,11},{9,8},{10,9... | collective-permute-start | bytes 479240 | tf_op jit(solution)/shard_map/ppermute | solution.py:299
  82.4 10.7 %collective-permute-start.5 = (bf16[104,768]{1,0:T(8,128)(2,1)S(1)}, bf16[104,768]{1,0:T(8,128)(2,1)S(1)}, u32[]{:S(2)}, u32[]{:S(2)}) collective-permute-start(bf16[104,768]{1,0:T(8,128)(2,1)S(1)} %get-tuple-element.60), channel_id=1, source_target_pairs={{0,2},{1,3},{2,0},{3,1},{4,6},{5,7},{6,4},{7,5},{8,10},{9,11},{10,... | collective-permute-start | bytes 479240 | tf_op jit(solution)/shard_map/ppermute | solution.py:299
  93.0 39.0 %collective-permute-start.28 = (bf16[1536,256]{1,0:T(8,128)(2,1)}, bf16[1536,256]{1,0:T(8,128)(2,1)}, u32[]{:S(2)}, u32[]{:S(2)}) collective-permute-start(bf16[1536,256]{1,0:T(8,128)(2,1)} %get-tuple-element.85), channel_id=1, source_target_pairs={{0,128},{128,0},{1,129},{129,1},{2,130},{130,2},{3,131},{131,3},{4... | collective-permute-start | bytes 2359304 | tf_op jit(solution)/shard_map/ppermute | solution.py:299
  97.5 18.6 %all-to-all-start = ((bf16[8,16,896]{2,1,0:T(8,128)(2,1)}), bf16[8,16,896]{2,1,0:T(8,128)(2,1)S(1)}, u32[]{:S(2)}, u32[]{:S(2)}) async-start(bf16[8,16,896]{2,1,0:T(8,128)(2,1)} %shard_map.119), calls=%async_computation | async-start | bytes 458752 | tf_op jit(solution)/shard_map/all_to_all | solution.py:308
  106.0 26.0 %collective-permute-start.29 = (bf16[1536,256]{1,0:T(8,128)(2,1)}, bf16[1536,256]{1,0:T(8,128)(2,1)}, u32[]{:S(2)}, u32[]{:S(2)}) collective-permute-start(bf16[1536,256]{1,0:T(8,128)(2,1)} %copy-done.9), channel_id=1, source_target_pairs={{0,128},{128,0},{1,129},{129,1},{2,130},{130,2},{3,131},{131,3},{4... | collective-permute-start | bytes 2359304 | tf_op jit(solution)/shard_map/ppermute | solution.py:299
  106.0 26.0 %collective-permute-start.30 = (bf16[1536,256]{1,0:T(8,128)(2,1)}, bf16[1536,256]{1,0:T(8,128)(2,1)}, u32[]{:S(2)}, u32[]{:S(2)}) collective-permute-start(bf16[1536,256]{1,0:T(8,128)(2,1)} %copy-done.8), channel_id=1, source_target_pairs={{0,128},{128,0},{1,129},{129,1},{2,130},{130,2},{3,131},{131,3},{4... | collective-permute-start | bytes 2359304 | tf_op jit(solution)/shard_map/ppermute | solution.py:299
  129.3 9.6 %collective-permute-start.27 = (bf16[128,768]{1,0:T(8,128)(2,1)S(1)}, bf16[128,768]{1,0:T(8,128)(2,1)S(1)}, u32[]{:S(2)}, u32[]{:S(2)}) collective-permute-start(bf16[128,768]{1,0:T(8,128)(2,1)S(1)} %bitcast.11), channel_id=1, source_target_pairs={{0,2},{1,3},{2,0},{3,1},{4,6},{5,7},{6,4},{7,5},{8,10},{9,11},{10,... | collective-permute-start | bytes 589832 | tf_op jit(solution)/shard_map/ppermute | solution.py:299
  129.7 9.2 %collective-permute-start.26 = (bf16[128,768]{1,0:T(8,128)(2,1)S(1)}, bf16[128,768]{1,0:T(8,128)(2,1)S(1)}, u32[]{:S(2)}, u32[]{:S(2)}) collective-permute-start(bf16[128,768]{1,0:T(8,128)(2,1)S(1)} %bitcast.12), channel_id=1, source_target_pairs={{0,3},{1,0},{2,1},{3,2},{4,7},{5,4},{6,5},{7,6},{8,11},{9,8},{10,9... | collective-permute-start | bytes 589832 | tf_op jit(solution)/shard_map/ppermute | solution.py:299
  (18 other events, 227.0 us)

commit v7 on v6

--- a/solution.py
+++ b/solution.py
@@ -27,7 +27,7 @@
     return pltpu.HBM(shape, BF)
 
 
-def call(kernel, outs, operands, limit=8, scratch=(), free=(), unblocked=()):
+def call(kernel, outs, operands, limit=8, scratch=(), free=(), unblocked=(), out=None):
     spec = pl.BlockSpec(memory_space=pltpu.VMEM)
     specs = [pl.BlockSpec(memory_space=pltpu.SMEM)]
     kept = [operands[0]]
@@ -39,7 +39,7 @@
         kernel,
         out_shape=outs,
         in_specs=specs,
-        out_specs=[spec] * len(outs),
+        out_specs=[out or spec] * len(outs),
         scratch_shapes=list(scratch),
         compiler_params=pltpu.CompilerParams(vmem_limit_bytes=limit * MIB),
     )(*kept)
@@ -263,11 +263,19 @@
 
 
 def columns_kernel(pos, *refs):
-    pieces, out_ref = refs[:4], refs[4]
+    pieces, out_ref, sems = refs[:4], refs[4], refs[5]
     width = pieces[0].shape[1]
-    for piece, shift in zip(pieces, (0, 1, -1, 2)):
+    copies = []
+    for k, shift in enumerate((0, 1, -1, 2)):
         block = lax.rem(pos[3] - shift + 4 + 2 * pos[0], 4)
-        out_ref[:, pl.ds(pl.multiple_of(block * width, LANES), width)] = piece[...]
+        at = pl.multiple_of(block * width, LANES)
+        copies.append(
+            pltpu.make_async_copy(pieces[k], out_ref.at[:, pl.ds(at, width)], sems.at[k])
+        )
+    for copy in copies:
+        copy.start()
+    for copy in copies:
+        copy.wait()
 
 
 def grad_kernel(other, pos, here_ref, far_ref, plus_ref, minus_ref, *refs):
@@ -371,7 +379,9 @@
         )
 
     def scatter(sends, name):
-        got = [sends[0]] + [shift(sends[j], "y", j) for j in (1, 3, 2)]
+        got = [sends[0]]
+        for j in (1, 3, 2):
+            got.append(shift(sends[j], "y", j))
         count = 2 if name == "sides" else 1
         return call(sum_kernel, [array(slots + 8, block)] * count, (pos, *got))
 
@@ -398,6 +408,8 @@
         columns_kernel,
         [plain(tok_count, width)],
         (pos, slab, *[shift(slab, "y", offset) for offset in (1, -1, 2)]),
+        out=pl.BlockSpec(memory_space=pl.ANY),
+        scratch=[pltpu.SemaphoreType.DMA((4,))],
     )
     used = [here, remote[5], sides[5], sides[6], local[4], remote[4], sides[4]]
     half = width // 2

time: 143 us -> 143 us (level)
  no operation moved by 1% of the time
where the time goes in v7:
time: 143 us; the launch traced here: 141 us
  waiting for transfers between devices  50.3 us (35%)
  starting transfers between devices  46.8 us (33%)
  Pallas kernels  27.6 us (19%)
  blocking collectives  12.2 us (9%)
  local copies, waits for them, and re-layouts  2.58 us (2%)
    ppermute x29, waiting for transfers between devices, shift(): lax.ppermute(value, axis, [(i, (i + offset) % size) for i in range(size)])  40.7 us
    ppermute x29, starting transfers between devices, shift(): lax.ppermute(value, axis, [(i, (i + offset) % size) for i in range(size)])  36.2 us
    pallas_call x14, Pallas kernels, call(): pl.pallas_call(kernel, out_shape=outs, in_specs=specs, out_specs=[out or...  27.6 us
    all_to_all x1, blocking collectives, exchange(): return lax.all_to_all(value, axis, split_axis=0, concat_axis=0, tiled=True)  12.2 us
    all_to_all x1, waiting for transfers between devices, exchange(): return lax.all_to_all(value, axis, split_axis=0, concat_axis=0, tiled=True)  9.62 us
    all_to_all x1, starting transfers between devices, exchange(): return lax.all_to_all(value, axis, split_axis=0, concat_axis=0, tiled=True)  8.46 us
  transfers between devices with their start and end apart: 32, of which 10 were waited for; matrix products, arithmetic and copies ran while one was open for 0% of the time, Pallas kernels for 17%

profile of v7, /device:TPU:8, one launch (start us, length us, event | category | flops | bytes accessed | tf_op | source)
XLA Modules:
  0.0 140.6 jit_solution(17629018350855543331)
XLA Ops:
  0.7 2.2 %shard_map.110 = (bf16[48,3200]{1,0:T(8,128)(2,1)S(1)}, bf16[128,3072]{1,0:T(8,128)(2,1)S(1)}, bf16[128,3072]{1,0:T(8,128)(2,1)S(1)}) custom-call(s32[4]{0:T(128)S(1)} %pad_add_fusion.pos, s32[2,128]{1,0:T(2,128)} %bitcast.15, bf16[2,128]{1,0:T(2,128)(2,1)} %bitcast.19, bf16[128,3072]{1,0:T(8,128)(2,1)} %tok_ref.1, bf16[128,3072]{1,0:T(8,128)(2,1)} %cot_ref.1), custom_call_target="tpu_custom_call" | custom-call | tf_op jit(solution)/shard_map/pallas_call | solution.py:38
  2.9 3.1 %collective-permute-start.6 = (bf16[48,3200]{1,0:T(8,128)(2,1)S(1)}, bf16[48,3200]{1,0:T(8,128)(2,1)S(1)}, u32[]{:S(2)}, u32[]{:S(2)}) collective-permute-start(bf16[48,3200]{1,0:T(8,128)(2,1)S(1)} %get-tuple-element.62), channel_id=1, source_target_pairs={{0,64},{32,96},{64,0},{96,32},{1,65},{33,97},{65,1},{97,33},{2,66}... | collective-permute-start | bytes 921608 | tf_op jit(solution)/shard_map/ppermute | solution.py:307
  6.0 7.5 %collective-permute-done.6.refs_0_ = bf16[48,3200]{1,0:T(8,128)(2,1)S(1)} collective-permute-done((bf16[48,3200]{1,0:T(8,128)(2,1)S(1)}, bf16[48,3200]{1,0:T(8,128)(2,1)S(1)}, u32[]{:S(2)}, u32[]{:S(2)}) %collective-permute-start.6) | collective-permute-done | bytes 307232 | tf_op jit(solution)/shard_map/ppermute | solution.py:307
  13.5 2.5 %collective-permute-start.9 = (bf16[48,3200]{1,0:T(8,128)(2,1)S(1)}, bf16[48,3200]{1,0:T(8,128)(2,1)S(1)}, u32[]{:S(2)}, u32[]{:S(2)}) collective-permute-start(bf16[48,3200]{1,0:T(8,128)(2,1)S(1)} %collective-permute-done.6.refs_0_), channel_id=1, source_target_pairs={{0,2},{1,3},{2,0},{3,1},{4,6},{5,7},{6,4},{7,5},{8,10},{9,11},{10,... | collective-permute-start | bytes 921608 | tf_op jit(solution)/shard_map/ppermute | solution.py:307
  22.3 4.1 %collective-permute-done.12.refs_2_ = bf16[96,768]{1,0:T(8,128)(2,1)S(1)} collective-permute-done((bf16[96,768]{1,0:T(8,128)(2,1)S(1)}, bf16[96,768]{1,0:T(8,128)(2,1)S(1)}, u32[]{:S(2)}, u32[]{:S(2)}) %collective-permute-start.12) | collective-permute-done | bytes 147488 | tf_op jit(solution)/shard_map/ppermute | solution.py:307
  27.0 2.5 %collective-permute-start.11 = (bf16[96,4736]{1,0:T(8,128)(2,1)S(1)}, bf16[96,4736]{1,0:T(8,128)(2,1)S(1)}, u32[]{:S(2)}, u32[]{:S(2)}) collective-permute-start(bf16[96,4736]{1,0:T(8,128)(2,1)S(1)} %get-tuple-element.65), channel_id=1, source_target_pairs={{0,96},{32,0},{64,32},{96,64},{1,97},{33,1},{65,33},{97,65},{2,98}... | collective-permute-start | bytes 2727944 | tf_op jit(solution)/shard_map/ppermute | solution.py:307
  31.8 1.9 %collective-permute-start.14 = (bf16[96,768]{1,0:T(8,128)(2,1)S(1)}, bf16[96,768]{1,0:T(8,128)(2,1)S(1)}, u32[]{:S(2)}, u32[]{:S(2)}) collective-permute-start(bf16[96,768]{1,0:T(8,128)(2,1)S(1)} %collective-permute-done.12.refs_2_), channel_id=1, source_target_pairs={{0,4},{4,0},{8,12},{12,8},{16,20},{20,16},{24,28},{28,24},{1,5},{5... | collective-permute-start | bytes 442376 | tf_op jit(solution)/shard_map/ppermute | solution.py:312
  35.3 2.9 %shard_map.113 = (bf16[104,768]{1,0:T(8,128)(2,1)S(1)}, bf16[104,768]{1,0:T(8,128)(2,1)S(1)}, bf16[104,768]{1,0:T(8,128)(2,1)S(1)}, bf16[104,768]{1,0:T(8,128)(2,1)S(1)}, bf16[96,768]{1,0:T(8,128)(2,1)S(1)}) custom-call(s32[4]{0:T(128)S(1)} %pad_add_fusion.pos, bf16[96,6272]{1,0:T(8,128)(2,1)S(1)} %get-tuple-element.53.refs_0_.here_ref, ...), custom_call_target="tpu_custom_call" | custom-call | tf_op jit(solution)/shard_map/pallas_call | solution.py:38
  38.2 1.9 %collective-permute-done.7.refs_1_ = bf16[48,3200]{1,0:T(8,128)(2,1)S(1)} collective-permute-done((bf16[48,3200]{1,0:T(8,128)(2,1)S(1)}, bf16[48,3200]{1,0:T(8,128)(2,1)S(1)}, u32[]{:S(2)}, u32[]{:S(2)}) %collective-permute-start.7) | collective-permute-done | bytes 307232 | tf_op jit(solution)/shard_map/ppermute | solution.py:307
  40.1 3.0 %shard_map.115 = (bf16[104,768]{1,0:T(8,128)(2,1)S(1)}, bf16[104,768]{1,0:T(8,128)(2,1)S(1)}, bf16[104,768]{1,0:T(8,128)(2,1)S(1)}, bf16[104,768]{1,0:T(8,128)(2...) custom-call(s32[4]{0:T(128)S(1)} %pad_add_fusion.pos, ...), custom_call_target="tpu_custom_call" | custom-call | tf_op jit(solution)/shard_map/pallas_call | solution.py:38
  43.7 5.8 %collective-permute-done.11.refs_1_ = bf16[96,4736]{1,0:T(8,128)(2,1)S(1)} collective-permute-done((bf16[96,4736]{1,0:T(8,128)(2,1)S(1)}, bf16[96,4736]{1,0:T(8,128)(2,1)S(1)}, u32[]{:S(2)}, u32[]{:S(2)}) %collective-permute-start.11) | collective-permute-done | bytes 909344 | tf_op jit(solution)/shard_map/ppermute | solution.py:307
  49.5 3.5 %collective-permute-done.10.refs_0_ = bf16[96,4736]{1,0:T(8,128)(2,1)S(1)} collective-permute-done((bf16[96,4736]{1,0:T(8,128)(2,1)S(1)}, bf16[96,4736]{1,0:T(8,128)(2,1)S(1)}, u32[]{:S(2)}, u32[]{:S(2)}) %collective-permute-start.10) | collective-permute-done | bytes 909344 | tf_op jit(solution)/shard_map/ppermute | solution.py:307
  53.0 3.6 %shard_map.116 = (bf16[208,768]{1,0:T(8,128)(2,1)S(1)}, bf16[208,768]{1,0:T(8,128)(2,1)S(1)}, bf16[208,768]{1,0:T(8,128)(2,1)S(1)}, bf16[208,768]{1,0:T(8,128)(2...) custom-call(s32[4]{0:T(128)S(1)} %pad_add_fusion.pos, ...), custom_call_target="tpu_custom_call" | custom-call | tf_op jit(solution)/shard_map/pallas_call | solution.py:38
  58.8 2.5 %collective-permute-start.18 = (bf16[208,768]{1,0:T(8,128)(2,1)S(1)}, bf16[208,768]{1,0:T(8,128)(2,1)S(1)}, u32[]{:S(2)}, u32[]{:S(2)}) collective-permute-start(bf16[208,768]{1,0:T(8,128)(2,1)S(1)} %get-tuple-element.71), channel_id=1, source_target_pairs={{0,2},{1,3},{2,0},{3,1},{4,6},{5,7},{6,4},{7,5},{8,10},{9,11},{10,... | collective-permute-start | bytes 958472 | tf_op jit(solution)/shard_map/ppermute | solution.py:307
  63.6 13.9 %collective-permute-done.22.c_ref = bf16[104,768]{1,0:T(8,128)(2,1)S(1)} collective-permute-done((bf16[104,768]{1,0:T(8,128)(2,1)S(1)}, bf16[104,768]{1,0:T(8,128)(2,1)S(1)}, u32[]{:S(2)}, u32[]{:S(2)}) %collective-permute-start.22) | collective-permute-done | bytes 159776 | tf_op jit(solution)/shard_map/ppermute | solution.py:307
  77.5 2.6 %collective-permute-start.3 = (bf16[104,768]{1,0:T(8,128)(2,1)S(1)}, bf16[104,768]{1,0:T(8,128)(2,1)S(1)}, u32[]{:S(2)}, u32[]{:S(2)}) collective-permute-start(bf16[104,768]{1,0:T(8,128)(2,1)S(1)} %get-tuple-element.58), channel_id=1, source_target_pairs={{0,1},{1,2},{2,3},{3,0},{4,5},{5,6},{6,7},{7,4},{8,9},{9,10},{10,1... | collective-permute-start | bytes 479240 | tf_op jit(solution)/shard_map/ppermute | solution.py:307
  82.4 3.2 %collective-permute-start.5 = (bf16[104,768]{1,0:T(8,128)(2,1)S(1)}, bf16[104,768]{1,0:T(8,128)(2,1)S(1)}, u32[]{:S(2)}, u32[]{:S(2)}) collective-permute-start(bf16[104,768]{1,0:T(8,128)(2,1)S(1)} %get-tuple-element.60), channel_id=1, source_target_pairs={{0,2},{1,3},{2,0},{3,1},{4,6},{5,7},{6,4},{7,5},{8,10},{9,11},{10,... | collective-permute-start | bytes 479240 | tf_op jit(solution)/shard_map/ppermute | solution.py:307
  90.3 2.7 %shard_map.122 = (bf16[1536,256]{1,0:T(8,128)(2,1)}, bf16[1536,256]{1,0:T(8,128)(2,1)S(1)}, bf16[1536,256]{1,0:T(8,128)(2,1)S(1)}) custom-call(s32[4]{0:T(128)S(1)} %pad_add_fusion.pos, bf16[96,6272]{1,0:T(8,128)(2,1)S(1)} %get-tuple-element.53.refs_0_.here_ref, bf16[96,6272]{1,0:T(8,128)(2,1)S(1)} %get-tuple-element.79.far_ref, ...), custom_call_target="tpu_custom_call" | custom-call | tf_op jit(solution)/shard_map/pallas_call | solution.py:38
  93.8 2.1 %collective-permute-done.20.refs_2_ = bf16[104,768]{1,0:T(8,128)(2,1)S(1)} collective-permute-done((bf16[104,768]{1,0:T(8,128)(2,1)S(1)}, bf16[104,768]{1,0:T(8,128)(2,1)S(1)}, u32[]{:S(2)}, u32[]{:S(2)}) %collective-permute-start.20) | collective-permute-done | bytes 159776 | tf_op jit(solution)/shard_map/ppermute | solution.py:307
  97.5 8.5 %all-to-all-start = ((bf16[8,16,896]{2,1,0:T(8,128)(2,1)}), bf16[8,16,896]{2,1,0:T(8,128)(2,1)S(1)}, u32[]{:S(2)}, u32[]{:S(2)}) async-start(bf16[8,16,896]{2,1,0:T(8,128)(2,1)} %shard_map.119), calls=%async_computation | async-start | bytes 458752 | tf_op jit(solution)/shard_map/all_to_all | solution.py:316
  106.5 9.6 %all-to-all-done.got_ref = bf16[8,16,896]{2,1,0:T(8,128)(2,1)S(1)} async-done(((bf16[8,16,896]{2,1,0:T(8,128)(2,1)}), bf16[8,16,896]{2,1,0:T(8,128)(2,1)S(1)}, u32[]{:S(2)}, u32[]{:S(2)}) %all-to-all-start) | async-done | bytes 229408 | tf_op jit(solution)/shard_map/all_to_all | solution.py:316
  117.2 12.2 %all_to_all.10 = bf16[8,16,768]{2,1,0:T(8,128)(2,1)S(1)} all-to-all(bf16[8,16,768]{2,1,0:T(8,128)(2,1)S(1)} %get-tuple-element.77), channel_id=1, replica_groups=mesh['dp'=2,'expert'=4,'z'=8,'y'=4] {'z'}, dimensions={0} | all-to-all | bytes 393216 | tf_op jit(solution)/shard_map/all_to_all | solution.py:316
  129.7 2.3 %collective-permute-start.26 = (bf16[128,768]{1,0:T(8,128)(2,1)S(1)}, bf16[128,768]{1,0:T(8,128)(2,1)S(1)}, u32[]{:S(2)}, u32[]{:S(2)}) collective-permute-start(bf16[128,768]{1,0:T(8,128)(2,1)S(1)} %bitcast.12), channel_id=1, source_target_pairs={{0,3},{1,0},{2,1},{3,2},{4,7},{5,4},{6,5},{7,6},{8,11},{9,8},{10,9... | collective-permute-start | bytes 589832 | tf_op jit(solution)/shard_map/ppermute | solution.py:307
  134.6 4.3 %shard_map.123 = (bf16[1536,256]{1,0:T(8,128)(2,1)}, bf16[1536,256]{1,0:T(8,128)(2,1)}, bf16[1536,256]{1,0:T(8,128)(2,1)}) custom-call(s32[4]{0:T(128)S(1)} %pad_add_fusion.pos, bf16[96,6272]{1,0:T(8,128)(2,1)S(1)} %get-tuple-element.53.refs_0_.here_ref, bf16[96,6272]{1,0:T(8,128)(2,1)S(1)} %get-tuple-element.79.far_ref, bf16[96,6272]{1,0:T(8,128)(2,1)S(1)} %copy-done.4, ...), custom_call_target="tpu_custom_call" | custom-call | tf_op jit(solution)/shard_map/pallas_call | solution.py:38
  (76 shorter events, 31.1 us)
Async XLA Ops:
  2.9 10.6 %collective-permute-start.6 = (bf16[48,3200]{1,0:T(8,128)(2,1)S(1)}, bf16[48,3200]{1,0:T(8,128)(2,1)S(1)}, u32[]{:S(2)}, u32[]{:S(2)}) collective-permute-start(bf16[48,3200]{1,0:T(8,128)(2,1)S(1)} %get-tuple-element.62), channel_id=1, source_target_pairs={{0,64},{32,96},{64,0},{96,32},{1,65},{33,97},{65,1},{97,33},{2,66}... | collective-permute-start | bytes 921608 | tf_op jit(solution)/shard_map/ppermute | solution.py:307
  13.5 13.5 %collective-permute-start.9 = (bf16[48,3200]{1,0:T(8,128)(2,1)S(1)}, bf16[48,3200]{1,0:T(8,128)(2,1)S(1)}, u32[]{:S(2)}, u32[]{:S(2)}) collective-permute-start(bf16[48,3200]{1,0:T(8,128)(2,1)S(1)} %collective-permute-done.6.refs_0_), channel_id=1, source_target_pairs={{0,2},{1,3},{2,0},{3,1},{4,6},{5,7},{6,4},{7,5},{8,10},{9,11},{10,... | collective-permute-start | bytes 921608 | tf_op jit(solution)/shard_map/ppermute | solution.py:307
  16.0 13.7 %collective-permute-start.8 = (bf16[48,3200]{1,0:T(8,128)(2,1)S(1)}, bf16[48,3200]{1,0:T(8,128)(2,1)S(1)}, u32[]{:S(2)}, u32[]{:S(2)}) collective-permute-start(bf16[48,3200]{1,0:T(8,128)(2,1)S(1)} %collective-permute-done.6.refs_0_), channel_id=1, source_target_pairs={{0,3},{1,0},{2,1},{3,2},{4,7},{5,4},{6,5},{7,6},{8,11},{9,8},{10,9... | collective-permute-start | bytes 921608 | tf_op jit(solution)/shard_map/ppermute | solution.py:307
  18.9 12.3 %collective-permute-start = (bf16[1,1536,256]{2,1,0:T(8,128)(2,1)S(1)}, bf16[1,1536,256]{2,1,0:T(8,128)(2,1)S(1)}, u32[]{:S(2)}, u32[]{:S(2)}) collective-permute-start(bf16[1,1536,256]{2,1,0:T(8,128)(2,1)S(1)} %copy-done), channel_id=1, source_target_pairs={{0,128},{128,0},{1,129},{129,1},{2,130},{130,2},{3,131},{131,3},{4... | collective-permute-start | bytes 2359304 | tf_op jit(solution)/shard_map/ppermute | solution.py:307
  27.0 22.5 %collective-permute-start.11 = (bf16[96,4736]{1,0:T(8,128)(2,1)S(1)}, bf16[96,4736]{1,0:T(8,128)(2,1)S(1)}, u32[]{:S(2)}, u32[]{:S(2)}) collective-permute-start(bf16[96,4736]{1,0:T(8,128)(2,1)S(1)} %get-tuple-element.65), channel_id=1, source_target_pairs={{0,96},{32,0},{64,32},{96,64},{1,97},{33,1},{65,33},{97,65},{2,98}... | collective-permute-start | bytes 2727944 | tf_op jit(solution)/shard_map/ppermute | solution.py:307
  29.7 23.3 %collective-permute-start.10 = (bf16[96,4736]{1,0:T(8,128)(2,1)S(1)}, bf16[96,4736]{1,0:T(8,128)(2,1)S(1)}, u32[]{:S(2)}, u32[]{:S(2)}) collective-permute-start(bf16[96,4736]{1,0:T(8,128)(2,1)S(1)} %get-tuple-element.50), channel_id=1, source_target_pairs={{0,32},{32,64},{64,96},{96,0},{1,33},{33,65},{65,97},{97,1},{2,34}... | collective-permute-start | bytes 2727944 | tf_op jit(solution)/shard_map/ppermute | solution.py:307
  31.2 8.9 %collective-permute-start.7 = (bf16[48,3200]{1,0:T(8,128)(2,1)S(1)}, bf16[48,3200]{1,0:T(8,128)(2,1)S(1)}, u32[]{:S(2)}, u32[]{:S(2)}) collective-permute-start(bf16[48,3200]{1,0:T(8,128)(2,1)S(1)} %collective-permute-done.6.refs_0_), channel_id=1, source_target_pairs={{0,1},{1,2},{2,3},{3,0},{4,5},{5,6},{6,7},{7,4},{8,9},{9,10},{10,1... | collective-permute-start | bytes 921608 | tf_op jit(solution)/shard_map/ppermute | solution.py:307
  31.8 11.9 %collective-permute-start.14 = (bf16[96,768]{1,0:T(8,128)(2,1)S(1)}, bf16[96,768]{1,0:T(8,128)(2,1)S(1)}, u32[]{:S(2)}, u32[]{:S(2)}) collective-permute-start(bf16[96,768]{1,0:T(8,128)(2,1)S(1)} %collective-permute-done.12.refs_2_), channel_id=1, source_target_pairs={{0,4},{4,0},{8,12},{12,8},{16,20},{20,16},{24,28},{28,24},{1,5},{5... | collective-permute-start | bytes 442376 | tf_op jit(solution)/shard_map/ppermute | solution.py:312
  33.8 10.0 %collective-permute-start.15 = (bf16[96,768]{1,0:T(8,128)(2,1)S(1)}, bf16[96,768]{1,0:T(8,128)(2,1)S(1)}, u32[]{:S(2)}, u32[]{:S(2)}) collective-permute-start(bf16[96,768]{1,0:T(8,128)(2,1)S(1)} %collective-permute-done.13.refs_3_), channel_id=1, source_target_pairs={{0,4},{4,0},{8,12},{12,8},{16,20},{20,16},{24,28},{28,24},{1,5},{5... | collective-permute-start | bytes 442376 | tf_op jit(solution)/shard_map/ppermute | solution.py:312
  43.1 18.8 %collective-permute-start.21 = (bf16[104,768]{1,0:T(8,128)(2,1)S(1)}, bf16[104,768]{1,0:T(8,128)(2,1)S(1)}, u32[]{:S(2)}, u32[]{:S(2)}) collective-permute-start(bf16[104,768]{1,0:T(8,128)(2,1)S(1)} %get-tuple-element.74), channel_id=1, source_target_pairs={{0,1},{1,2},{2,3},{3,0},{4,5},{5,6},{6,7},{7,4},{8,9},{9,10},{10,1... | collective-permute-start | bytes 479240 | tf_op jit(solution)/shard_map/ppermute | solution.py:307
  56.6 25.7 %collective-permute-start.16 = (bf16[208,768]{1,0:T(8,128)(2,1)S(1)}, bf16[208,768]{1,0:T(8,128)(2,1)S(1)}, u32[]{:S(2)}, u32[]{:S(2)}) collective-permute-start(bf16[208,768]{1,0:T(8,128)(2,1)S(1)} %get-tuple-element.69), channel_id=1, source_target_pairs={{0,1},{1,2},{2,3},{3,0},{4,5},{5,6},{6,7},{7,4},{8,9},{9,10},{10,1... | collective-permute-start | bytes 958472 | tf_op jit(solution)/shard_map/ppermute | solution.py:307
  57.3 28.3 %collective-permute-start.17 = (bf16[208,768]{1,0:T(8,128)(2,1)S(1)}, bf16[208,768]{1,0:T(8,128)(2,1)S(1)}, u32[]{:S(2)}, u32[]{:S(2)}) collective-permute-start(bf16[208,768]{1,0:T(8,128)(2,1)S(1)} %get-tuple-element.70), channel_id=1, source_target_pairs={{0,3},{1,0},{2,1},{3,2},{4,7},{5,4},{6,5},{7,6},{8,11},{9,8},{10,9... | collective-permute-start | bytes 958472 | tf_op jit(solution)/shard_map/ppermute | solution.py:307
  58.8 28.7 %collective-permute-start.18 = (bf16[208,768]{1,0:T(8,128)(2,1)S(1)}, bf16[208,768]{1,0:T(8,128)(2,1)S(1)}, u32[]{:S(2)}, u32[]{:S(2)}) collective-permute-start(bf16[208,768]{1,0:T(8,128)(2,1)S(1)} %get-tuple-element.71), channel_id=1, source_target_pairs={{0,2},{1,3},{2,0},{3,1},{4,6},{5,7},{6,4},{7,5},{8,10},{9,11},{10,... | collective-permute-start | bytes 958472 | tf_op jit(solution)/shard_map/ppermute | solution.py:307
  61.3 16.2 %collective-permute-start.22 = (bf16[104,768]{1,0:T(8,128)(2,1)S(1)}, bf16[104,768]{1,0:T(8,128)(2,1)S(1)}, u32[]{:S(2)}, u32[]{:S(2)}) collective-permute-start(bf16[104,768]{1,0:T(8,128)(2,1)S(1)} %get-tuple-element.75), channel_id=1, source_target_pairs={{0,3},{1,0},{2,1},{3,2},{4,7},{5,4},{6,5},{7,6},{8,11},{9,8},{10,9... | collective-permute-start | bytes 479240 | tf_op jit(solution)/shard_map/ppermute | solution.py:307
  61.9 19.8 %collective-permute-start.23 = (bf16[104,768]{1,0:T(8,128)(2,1)S(1)}, bf16[104,768]{1,0:T(8,128)(2,1)S(1)}, u32[]{:S(2)}, u32[]{:S(2)}) collective-permute-start(bf16[104,768]{1,0:T(8,128)(2,1)S(1)} %get-tuple-element.76), channel_id=1, source_target_pairs={{0,2},{1,3},{2,0},{3,1},{4,6},{5,7},{6,4},{7,5},{8,10},{9,11},{10,... | collective-permute-start | bytes 479240 | tf_op jit(solution)/shard_map/ppermute | solution.py:307
  77.5 11.8 %collective-permute-start.3 = (bf16[104,768]{1,0:T(8,128)(2,1)S(1)}, bf16[104,768]{1,0:T(8,128)(2,1)S(1)}, u32[]{:S(2)}, u32[]{:S(2)}) collective-permute-start(bf16[104,768]{1,0:T(8,128)(2,1)S(1)} %get-tuple-element.58), channel_id=1, source_target_pairs={{0,1},{1,2},{2,3},{3,0},{4,5},{5,6},{6,7},{7,4},{8,9},{9,10},{10,1... | collective-permute-start | bytes 479240 | tf_op jit(solution)/shard_map/ppermute | solution.py:307
  81.7 11.3 %collective-permute-start.4 = (bf16[104,768]{1,0:T(8,128)(2,1)S(1)}, bf16[104,768]{1,0:T(8,128)(2,1)S(1)}, u32[]{:S(2)}, u32[]{:S(2)}) collective-permute-start(bf16[104,768]{1,0:T(8,128)(2,1)S(1)} %get-tuple-element.59), channel_id=1, source_target_pairs={{0,3},{1,0},{2,1},{3,2},{4,7},{5,4},{6,5},{7,6},{8,11},{9,8},{10,9... | collective-permute-start | bytes 479240 | tf_op jit(solution)/shard_map/ppermute | solution.py:307
  82.4 10.7 %collective-permute-start.5 = (bf16[104,768]{1,0:T(8,128)(2,1)S(1)}, bf16[104,768]{1,0:T(8,128)(2,1)S(1)}, u32[]{:S(2)}, u32[]{:S(2)}) collective-permute-start(bf16[104,768]{1,0:T(8,128)(2,1)S(1)} %get-tuple-element.60), channel_id=1, source_target_pairs={{0,2},{1,3},{2,0},{3,1},{4,6},{5,7},{6,4},{7,5},{8,10},{9,11},{10,... | collective-permute-start | bytes 479240 | tf_op jit(solution)/shard_map/ppermute | solution.py:307
  93.0 39.0 %collective-permute-start.28 = (bf16[1536,256]{1,0:T(8,128)(2,1)}, bf16[1536,256]{1,0:T(8,128)(2,1)}, u32[]{:S(2)}, u32[]{:S(2)}) collective-permute-start(bf16[1536,256]{1,0:T(8,128)(2,1)} %get-tuple-element.85), channel_id=1, source_target_pairs={{0,128},{128,0},{1,129},{129,1},{2,130},{130,2},{3,131},{131,3},{4... | collective-permute-start | bytes 2359304 | tf_op jit(solution)/shard_map/ppermute | solution.py:307
  97.5 18.6 %all-to-all-start = ((bf16[8,16,896]{2,1,0:T(8,128)(2,1)}), bf16[8,16,896]{2,1,0:T(8,128)(2,1)S(1)}, u32[]{:S(2)}, u32[]{:S(2)}) async-start(bf16[8,16,896]{2,1,0:T(8,128)(2,1)} %shard_map.119), calls=%async_computation | async-start | bytes 458752 | tf_op jit(solution)/shard_map/all_to_all | solution.py:316
  106.0 26.0 %collective-permute-start.29 = (bf16[1536,256]{1,0:T(8,128)(2,1)}, bf16[1536,256]{1,0:T(8,128)(2,1)}, u32[]{:S(2)}, u32[]{:S(2)}) collective-permute-start(bf16[1536,256]{1,0:T(8,128)(2,1)} %copy-done.9), channel_id=1, source_target_pairs={{0,128},{128,0},{1,129},{129,1},{2,130},{130,2},{3,131},{131,3},{4... | collective-permute-start | bytes 2359304 | tf_op jit(solution)/shard_map/ppermute | solution.py:307
  106.0 26.0 %collective-permute-start.30 = (bf16[1536,256]{1,0:T(8,128)(2,1)}, bf16[1536,256]{1,0:T(8,128)(2,1)}, u32[]{:S(2)}, u32[]{:S(2)}) collective-permute-start(bf16[1536,256]{1,0:T(8,128)(2,1)} %copy-done.8), channel_id=1, source_target_pairs={{0,128},{128,0},{1,129},{129,1},{2,130},{130,2},{3,131},{131,3},{4... | collective-permute-start | bytes 2359304 | tf_op jit(solution)/shard_map/ppermute | solution.py:307
  129.3 9.6 %collective-permute-start.27 = (bf16[128,768]{1,0:T(8,128)(2,1)S(1)}, bf16[128,768]{1,0:T(8,128)(2,1)S(1)}, u32[]{:S(2)}, u32[]{:S(2)}) collective-permute-start(bf16[128,768]{1,0:T(8,128)(2,1)S(1)} %bitcast.11), channel_id=1, source_target_pairs={{0,2},{1,3},{2,0},{3,1},{4,6},{5,7},{6,4},{7,5},{8,10},{9,11},{10,... | collective-permute-start | bytes 589832 | tf_op jit(solution)/shard_map/ppermute | solution.py:307
  129.7 9.2 %collective-permute-start.26 = (bf16[128,768]{1,0:T(8,128)(2,1)S(1)}, bf16[128,768]{1,0:T(8,128)(2,1)S(1)}, u32[]{:S(2)}, u32[]{:S(2)}) collective-permute-start(bf16[128,768]{1,0:T(8,128)(2,1)S(1)} %bitcast.12), channel_id=1, source_target_pairs={{0,3},{1,0},{2,1},{3,2},{4,7},{5,4},{6,5},{7,6},{8,11},{9,8},{10,9... | collective-permute-start | bytes 589832 | tf_op jit(solution)/shard_map/ppermute | solution.py:307
  (18 other events, 227.0 us)
